TPU v7x, 32 devices: a whole 2x2x4 slice. The times are simulated.
32 devices in a mesh: dp: 8 (over z, core), ctx: 4 (over y, x).
Axes of the slice: x: 2, y: 2, z: 4, core: 2. Of those that a mesh axis runs over, the one named last changes fastest.
Arguments:
- inputs: bfloat16 [8, 1024, 1536], P('dp', 'ctx'), may hold values from -6 to 6
- cotangent: bfloat16 [8, 1024, 1536], P('dp', 'ctx'), may hold values from -6 to 6
- segment_ids: int32 [8, 1024], P('dp', 'ctx'), may hold values from 0 to 3, never falling along the last dimension, each value on 1 to 512 neighbouring positions
- attn_gain: bfloat16 [1536], P(('dp', 'ctx')), may hold values from 0.5 to 1.5
- qkv_weight: bfloat16 [1536, 2048], P(('dp', 'ctx')), may hold values from -0.15625 to 0.15625
- qkv_bias: bfloat16 [2048], P(('dp', 'ctx')), may hold values from -4 to 4
- out_weight: bfloat16 [1536, 1536], P(('dp', 'ctx')), may hold values from -0.875 to 0.875
- mlp_gain: bfloat16 [1536], P(('dp', 'ctx')), may hold values from 0.5 to 1.5
- gate_weight: bfloat16 [1536, 8960], P(('dp', 'ctx')), may hold values from -0.15625 to 0.15625
- up_weight: bfloat16 [1536, 8960], P(('dp', 'ctx')), may hold values from -0.15625 to 0.15625
- down_weight: bfloat16 [8960, 1536], P(('dp', 'ctx')), may hold values from -0.0625 to 0.0625
Outputs:
- output: bfloat16 [8, 1024, 1536], P('dp', 'ctx')
- input_grad: float32 [8, 1024, 1536], P('dp', 'ctx')
- attn_gain_grad: float32 [1536], P(('dp', 'ctx'))
- qkv_weight_grad: float32 [1536, 2048], P(('dp', 'ctx'))
- qkv_bias_grad: float32 [2048], P(('dp', 'ctx'))
- out_weight_grad: float32 [1536, 1536], P(('dp', 'ctx'))
- mlp_gain_grad: float32 [1536], P(('dp', 'ctx'))
- gate_weight_grad: float32 [1536, 8960], P(('dp', 'ctx'))
- up_weight_grad: float32 [1536, 8960], P(('dp', 'ctx'))
- down_weight_grad: float32 [8960, 1536], P(('dp', 'ctx'))
Inputs may be any that keep to these rules, and one draw needn't show every extreme that they name: `segment_ids`: segment ids never fall along a sequence; each of the 4 documents of a sequence holds 1 to 512 tokens, and one holds exactly 512.
All inputs are finite; a program needn't handle non-finite values.
Results may differ from a plain program's by a relative error of at most 0.029.
The roundings to bfloat16 on the way count: a program that leaves them out, or rounds other values in their place, can miss the bound.
Values may be sent and summed in bfloat16 or wider, within the bound.
No kernel may reach another device: no remote copies, remote signals or barrier semaphores. Data moves between devices by JAX's collectives and lax.ppermute only.
A program may use at most 640 MiB of HBM per device.

v0:
```python
import math

import jax
import jax.numpy as jnp
from jax import lax
from jax.sharding import PartitionSpec as P

H = 12
KV = 2
HD = 128


EPS = 1e-06
THETA = 1000000.0
MASKED = -1e30


def rope_tables(positions):
    half_dim = jnp.arange(0, HD, 2).astype(jnp.float32) / HD
    inverse = THETA ** (-half_dim)
    angles = positions.astype(jnp.float32)[:, None] * inverse[None, :]
    angles = jnp.concatenate([angles, angles], axis=1)
    return (jnp.cos(angles), jnp.sin(angles))


def rotate(values, cos_table, sin_table):
    half_dim = values.shape[-1] // 2
    turned = jnp.concatenate([-values[..., half_dim:], values[..., :half_dim]], axis=-1)
    return values * cos_table[:, None, :] + turned * sin_table[:, None, :]


def rms_norm(values, gain):
    inv_rms = lax.rsqrt(jnp.mean(values * values, axis=-1, keepdims=True) + EPS)
    return (values * inv_rms * gain.astype(jnp.float32), inv_rms)


def norm_back(normed_grad, values, inv_rms, gain):
    normed = values * inv_rms
    gain_grad = jnp.sum(normed_grad * normed, axis=0)
    scaled_grad = normed_grad * gain.astype(jnp.float32)
    values_grad = inv_rms * (
        scaled_grad - normed * jnp.mean(scaled_grad * normed, axis=-1, keepdims=True)
    )
    return (values_grad, gain_grad)


def attend(queries, key_rows, value_rows, visible, scale_factor):
    per_group = queries.shape[1] // KV
    pieces = []
    totals = []
    for kv_group in range(KV):
        query_part = queries[:, kv_group * per_group : (kv_group + 1) * per_group, :]
        scores = (
            jnp.einsum(
                "tjd,nd->jtn",
                query_part,
                key_rows[:, kv_group, :],
                preferred_element_type=jnp.float32,
            )
            * scale_factor
        )
        scores = jnp.where(visible[None], scores, MASKED)
        row_max = jnp.max(scores, axis=-1, keepdims=True)
        row_sum = jnp.sum(jnp.exp(scores - row_max), axis=-1, keepdims=True)
        log_total = row_max + jnp.log(row_sum)
        weights = jnp.exp(scores - log_total).astype(jnp.bfloat16)
        mixed_part = jnp.einsum(
            "jtn,nd->tjd", weights, value_rows[:, kv_group, :], preferred_element_type=jnp.float32
        )
        pieces.append(mixed_part)
        totals.append(log_total)
    attended = jnp.concatenate(pieces, axis=1).astype(jnp.bfloat16)
    return (attended.reshape(queries.shape[0], -1), jnp.stack(totals))


def attend_back(
    queries, key_rows, value_rows, visible, attended, attended_grad, log_totals, scale_factor
):
    tokens = queries.shape[0]
    per_group = queries.shape[1] // KV
    attended_heads = attended.reshape(tokens, H, HD)
    grad_heads = attended_grad.reshape(tokens, H, HD)
    query_grads = []
    key_grads = []
    value_grads = []
    for kv_group in range(KV):
        part = slice(kv_group * per_group, (kv_group + 1) * per_group)
        query_part = queries[:, part, :]
        out_part = attended_heads[:, part, :]
        grad_part = grad_heads[:, part, :]
        key_part = key_rows[:, kv_group, :]
        value_part = value_rows[:, kv_group, :]
        scores = (
            jnp.einsum("tjd,nd->jtn", query_part, key_part, preferred_element_type=jnp.float32)
            * scale_factor
        )
        scores = jnp.where(visible[None], scores, MASKED)
        probs_full = jnp.exp(scores - log_totals[kv_group])
        probs_low = probs_full.astype(jnp.bfloat16)
        value_grads.append(
            jnp.einsum("jtn,tjd->nd", probs_low, grad_part, preferred_element_type=jnp.float32)
        )
        prob_grad = jnp.einsum(
            "tjd,nd->jtn", grad_part, value_part, preferred_element_type=jnp.float32
        )
        row_dot = jnp.sum(grad_part.astype(jnp.float32) * out_part.astype(jnp.float32), axis=-1).T
        score_grad = (probs_full * (prob_grad - row_dot[..., None]) * scale_factor).astype(
            jnp.bfloat16
        )
        query_grads.append(
            jnp.einsum("jtn,nd->tjd", score_grad, key_part, preferred_element_type=jnp.float32)
        )
        key_grads.append(
            jnp.einsum("jtn,tjd->nd", score_grad, query_part, preferred_element_type=jnp.float32)
        )
    return (
        jnp.concatenate(query_grads, axis=1),
        jnp.stack(key_grads, axis=1),
        jnp.stack(value_grads, axis=1),
    )


def on_device(
    inputs,
    cotangent,
    segment_ids,
    attn_gain,
    qkv_weight,
    qkv_bias,
    out_weight,
    mlp_gain,
    gate_weight,
    up_weight,
    down_weight,
):
    span_rows = inputs.shape[1]
    query_width = H * HD
    kv_width = KV * HD
    scale_factor = 1.0 / math.sqrt(HD)
    gain_one, full_qkv, bias_full, full_out = (
        lax.all_gather(attn_gain, ("dp", "ctx"), axis=0, tiled=True),
        lax.all_gather(qkv_weight, ("dp", "ctx"), axis=0, tiled=True),
        lax.all_gather(qkv_bias, ("dp", "ctx"), axis=0, tiled=True),
        lax.all_gather(out_weight, ("dp", "ctx"), axis=0, tiled=True),
    )
    gain_two, full_gate, full_up, full_down = (
        lax.all_gather(mlp_gain, ("dp", "ctx"), axis=0, tiled=True),
        lax.all_gather(gate_weight, ("dp", "ctx"), axis=0, tiled=True),
        lax.all_gather(up_weight, ("dp", "ctx"), axis=0, tiled=True),
        lax.all_gather(down_weight, ("dp", "ctx"), axis=0, tiled=True),
    )
    own_segments = segment_ids[0]
    all_segments = lax.all_gather(segment_ids, "ctx", axis=1, tiled=True)[0]
    length = all_segments.shape[0]
    offset = lax.axis_index("ctx") * span_rows
    query_index = offset + jnp.arange(span_rows, dtype=jnp.int32)
    key_index = jnp.arange(length, dtype=jnp.int32)
    doc_start = jnp.sum((all_segments[None, :] < own_segments[:, None]).astype(jnp.int32), axis=1)
    positions = query_index - doc_start
    visible = (key_index[None, :] <= query_index[:, None]) & (
        all_segments[None, :] == own_segments[:, None]
    )
    cos_table, sin_table = rope_tables(positions)
    resid_in = inputs[0].astype(jnp.float32)
    normed_one, inv_one = rms_norm(resid_in, gain_one)
    normed_low = normed_one.astype(jnp.bfloat16)
    projected = jnp.dot(
        normed_low, full_qkv, preferred_element_type=jnp.float32
    ) + bias_full.astype(jnp.float32)
    query_pre = projected[:, :query_width].reshape(span_rows, H, HD)
    key_pre = projected[:, query_width : query_width + kv_width].reshape(span_rows, KV, HD)
    value_rows = projected[:, query_width + kv_width :].astype(jnp.bfloat16)
    query_rot = rotate(query_pre, cos_table, sin_table).astype(jnp.bfloat16)
    key_rot = (
        rotate(key_pre, cos_table, sin_table).astype(jnp.bfloat16).reshape(span_rows, kv_width)
    )
    key_all, value_all = (
        lax.all_gather(key_rot, "ctx", axis=0, tiled=True),
        lax.all_gather(value_rows, "ctx", axis=0, tiled=True),
    )
    attended, log_totals = attend(
        query_rot,
        key_all.reshape(length, KV, HD),
        value_all.reshape(length, KV, HD),
        visible,
        scale_factor,
    )
    resid_mid = resid_in + jnp.dot(attended, full_out, preferred_element_type=jnp.float32)
    normed_two, inv_two = rms_norm(resid_mid, gain_two)
    normed_two_low = normed_two.astype(jnp.bfloat16)
    gate_pre = jnp.dot(normed_two_low, full_gate, preferred_element_type=jnp.float32)
    up_pre = jnp.dot(normed_two_low, full_up, preferred_element_type=jnp.float32)
    sigmoid_gate = jax.nn.sigmoid(gate_pre)
    silu_gate = gate_pre * sigmoid_gate
    hidden = (silu_gate * up_pre).astype(jnp.bfloat16)
    output = (resid_mid + jnp.dot(hidden, full_down, preferred_element_type=jnp.float32)).astype(
        jnp.bfloat16
    )
    grad_out = cotangent[0]
    gain_two, full_gate, full_up, full_down = (
        lax.all_gather(mlp_gain, ("dp", "ctx"), axis=0, tiled=True),
        lax.all_gather(gate_weight, ("dp", "ctx"), axis=0, tiled=True),
        lax.all_gather(up_weight, ("dp", "ctx"), axis=0, tiled=True),
        lax.all_gather(down_weight, ("dp", "ctx"), axis=0, tiled=True),
    )
    down_term = jnp.dot(hidden.T, grad_out, preferred_element_type=jnp.float32)
    down_grad = lax.psum_scatter(down_term, ("dp", "ctx"), scatter_dimension=0, tiled=True)
    hidden_grad = jnp.dot(grad_out, full_down.T, preferred_element_type=jnp.float32)
    gate_grad = (
        hidden_grad * up_pre * sigmoid_gate * (1.0 + gate_pre * (1.0 - sigmoid_gate))
    ).astype(jnp.bfloat16)
    up_grad = (hidden_grad * silu_gate).astype(jnp.bfloat16)
    normed_two_grad = jnp.dot(gate_grad, full_gate.T, preferred_element_type=jnp.float32) + jnp.dot(
        up_grad, full_up.T, preferred_element_type=jnp.float32
    )
    mid_norm_grad, gain_two_term = norm_back(normed_two_grad, resid_mid, inv_two, gain_two)
    gate_term = jnp.dot(normed_two_low.T, gate_grad, preferred_element_type=jnp.float32)
    up_term = jnp.dot(normed_two_low.T, up_grad, preferred_element_type=jnp.float32)
    gate_weight_grad, up_weight_grad, mlp_gain_grad = (
        lax.psum_scatter(gate_term, ("dp", "ctx"), scatter_dimension=0, tiled=True),
        lax.psum_scatter(up_term, ("dp", "ctx"), scatter_dimension=0, tiled=True),
        lax.psum_scatter(gain_two_term, ("dp", "ctx"), scatter_dimension=0, tiled=True),
    )
    mid_grad = grad_out.astype(jnp.float32) + mid_norm_grad
    mid_grad_low = mid_grad.astype(jnp.bfloat16)
    gain_one, full_qkv, bias_full, full_out = (
        lax.all_gather(attn_gain, ("dp", "ctx"), axis=0, tiled=True),
        lax.all_gather(qkv_weight, ("dp", "ctx"), axis=0, tiled=True),
        lax.all_gather(qkv_bias, ("dp", "ctx"), axis=0, tiled=True),
        lax.all_gather(out_weight, ("dp", "ctx"), axis=0, tiled=True),
    )
    attended_grad = jnp.dot(mid_grad_low, full_out.T, preferred_element_type=jnp.float32).astype(
        jnp.bfloat16
    )
    query_grad, key_grad_all, value_grad_all = attend_back(
        query_rot,
        key_all.reshape(length, KV, HD),
        value_all.reshape(length, KV, HD),
        visible,
        attended,
        attended_grad,
        log_totals,
        scale_factor,
    )
    key_grad, value_grad = (
        lax.psum_scatter(
            key_grad_all.reshape(length, kv_width).astype(jnp.bfloat16),
            "ctx",
            scatter_dimension=0,
            tiled=True,
        ).astype(jnp.float32),
        lax.psum_scatter(
            value_grad_all.reshape(length, kv_width).astype(jnp.bfloat16),
            "ctx",
            scatter_dimension=0,
            tiled=True,
        ).astype(jnp.float32),
    )
    query_grad_pre = rotate(query_grad, cos_table, -sin_table).reshape(span_rows, query_width)
    key_grad_pre = rotate(key_grad.reshape(span_rows, KV, HD), cos_table, -sin_table).reshape(
        span_rows, kv_width
    )
    proj_grad = jnp.concatenate([query_grad_pre, key_grad_pre, value_grad], axis=1)
    bias_term = jnp.sum(proj_grad, axis=0)
    proj_grad_low = proj_grad.astype(jnp.bfloat16)
    normed_one_grad = jnp.dot(proj_grad_low, full_qkv.T, preferred_element_type=jnp.float32)
    in_norm_grad, gain_one_term = norm_back(normed_one_grad, resid_in, inv_one, gain_one)
    input_grad = (mid_grad + in_norm_grad)[None]
    out_term = jnp.dot(attended.T, mid_grad_low, preferred_element_type=jnp.float32)
    qkv_term = jnp.dot(normed_low.T, proj_grad_low, preferred_element_type=jnp.float32)
    attn_gain_grad, qkv_weight_grad, qkv_bias_grad, out_weight_grad = (
        lax.psum_scatter(gain_one_term, ("dp", "ctx"), scatter_dimension=0, tiled=True),
        lax.psum_scatter(qkv_term, ("dp", "ctx"), scatter_dimension=0, tiled=True),
        lax.psum_scatter(bias_term, ("dp", "ctx"), scatter_dimension=0, tiled=True),
        lax.psum_scatter(out_term, ("dp", "ctx"), scatter_dimension=0, tiled=True),
    )
    return (
        output[None],
        input_grad,
        attn_gain_grad,
        qkv_weight_grad,
        qkv_bias_grad,
        out_weight_grad,
        mlp_gain_grad,
        gate_weight_grad,
        up_weight_grad,
        down_grad,
    )


def solution(mesh):
    return jax.shard_map(
        on_device,
        mesh=mesh,
        in_specs=(
            P("dp", "ctx", None),
            P("dp", "ctx", None),
            P("dp", "ctx"),
            P(("dp", "ctx")),
            P(("dp", "ctx"), None),
            P(("dp", "ctx")),
            P(("dp", "ctx"), None),
            P(("dp", "ctx")),
            P(("dp", "ctx"), None),
            P(("dp", "ctx"), None),
            P(("dp", "ctx"), None),
        ),
        out_specs=(
            P("dp", "ctx", None),
            P("dp", "ctx", None),
            P(("dp", "ctx")),
            P(("dp", "ctx"), None),
            P(("dp", "ctx")),
            P(("dp", "ctx"), None),
            P(("dp", "ctx")),
            P(("dp", "ctx"), None),
            P(("dp", "ctx"), None),
            P(("dp", "ctx"), None),
        ),
        check_vma=False,
    )
```

profile of v0, /device:TPU:25, one launch (start us, length us, event | category | flops | bytes accessed | tf_op | source)
XLA Modules:
  0.0 2478.0 jit_solution(7404797400683853180)
XLA Ops:
  13.2 39.1 %all-reduce.8 = (bf16[2048]{0:T(1024)(128)(2,1)S(1)}, bf16[1536]{0:T(1024)(128)(2,1)S(1)}, bf16[1536]{0:T(1024)(128)(2,1)S(1)}) all-reduce(bf16[2048]{0:T(1024)(128)(2,1)S(1)} %dynamic-update-slice.1, bf16[1536]{0:T(1024)(128)(2,1)S(1)} %dynamic-update-slice, ...), channel_id=1, replica_groups=mesh['dp'=8,'ctx'=4] {'dp','ctx'}, use_global_device_ids=true, to_apply=%add.1 | all-reduce | flops 5120 | bytes 20480
  61.8 18.3 all-gather.6.cloned.1.call-done
  86.1 8.8 all_gather.45
  101.3 9.3 all_gather.48
  124.2 22.0 all-gather.8.cloned.1.call-done
  150.2 162.3 %all-gather.10.cloned.1.call-done = bf16[1536,8960]{1,0:T(8,128)(2,1)} async-done(((bf16[48,8960]{1,0:T(8,128)(2,1)}), bf16[1536,8960]{1,0:T(8,128)(2,1)}) %all-gather.10.cloned.1.call-update) | async-done | bytes 27525136 | tf_op jit(solution)/shard_map/all_gather | solution.py:148
  312.5 15.2 fusion.75
  327.7 151.1 %all-gather.12.cloned.1.call-done = bf16[1536,8960]{1,0:T(8,128)(2,1)} async-done(((bf16[48,8960]{1,0:T(8,128)(2,1)}), bf16[1536,8960]{1,0:T(8,128)(2,1)}) %all-gather.12.cloned.1.call-update) | async-done | bytes 27525136 | tf_op jit(solution)/shard_map/all_gather | solution.py:149
  478.8 14.9 fusion.76
  493.7 151.4 %all-gather.14.cloned.1.call-done = bf16[8960,1536]{1,0:T(8,128)(2,1)} async-done(((bf16[280,1536]{1,0:T(8,128)(2,1)}), bf16[8960,1536]{1,0:T(8,128)(2,1)}) %all-gather.14.cloned.1.call-update) | async-done | bytes 27525136 | tf_op jit(solution)/shard_map/all_gather | solution.py:150
  645.1 21.5 multiply_convert_fusion
  666.6 14.8 fusion.77
  681.4 15.6 multiply_reduce_fusion
  749.3 21.2 reduce-scatter.12.cloned.1.call-done
  772.1 7.6 fusion.61
  779.7 26.3 %fusion.78 = f32[1536,8960]{1,0:T(8,128)} fusion(bf16[256,1536]{1,0:T(8,128)(2,1)} %copy-done.6, bf16[256,8960]{1,0:T(8,128)(2,1)} %get-tuple-element.25), kind=kOutput, calls=%fused_computation.142 | convolution fusion | flops 7046430720 | bytes 60424192 | tf_op jit(solution)/shard_map/dot_general | solution.py:217
  806.4 25.6 %fusion.79 = f32[1536,8960]{1,0:T(8,128)} fusion(bf16[256,1536]{1,0:T(8,128)(2,1)} %copy-done.6, bf16[256,8960]{1,0:T(8,128)(2,1)} %get-tuple-element.24), kind=kOutput, calls=%fused_computation.143 | convolution fusion | flops 7046430720 | bytes 60424192 | tf_op jit(solution)/shard_map/dot_general | solution.py:218
  832.0 23.2 fusion.43
  855.2 15.5 fusion.12
  877.1 38.4 %all-reduce.7 = (f32[1536]{0:T(1024)S(1)}, f32[2048]{0:T(1024)S(1)}, f32[1536]{0:T(1024)S(1)}) all-reduce(f32[1536]{0:T(1024)S(1)} %get-tuple-element.12, f32[2048]{0:T(1024)S(1)} %fusion.32, f32[1536]{0:T(1024)S(1)} %copy-done.33), channel_id=4, replica_groups=mesh['dp'=8,'ctx'=4] {'dp','ctx'}, use_global_device_ids=true, to_apply=%region_14.15.clone | all-reduce | flops 5120 | bytes 40960
  920.4 150.9 %reduce-scatter.14.cloned.1.call-done = f32[48,2048]{1,0:T(8,128)} async-done(((f32[1536,2048]{1,0:T(8,128)}), f32[48,2048]{1,0:T(8,128)}) %reduce-scatter.14.cloned.1.call-update) | async-done | bytes 393232 | tf_op jit(solution)/shard_map/reduce_scatter | solution.py:273
  1071.3 467.6 %reduce-scatter.18.cloned.1.call-done = f32[48,8960]{1,0:T(8,128)} async-done(((f32[1536,8960]{1,0:T(8,128)}), f32[48,8960]{1,0:T(8,128)}) %reduce-scatter.18.cloned.1.call-update) | async-done | bytes 1720336 | tf_op jit(solution)/shard_map/reduce_scatter | solution.py:220
  1538.9 466.0 %reduce-scatter.20.cloned.1.call-done = f32[48,8960]{1,0:T(8,128)} async-done(((f32[1536,8960]{1,0:T(8,128)}), f32[48,8960]{1,0:T(8,128)}) %reduce-scatter.20.cloned.1.call-update) | async-done | bytes 1720336 | tf_op jit(solution)/shard_map/reduce_scatter | solution.py:221
  2004.9 465.8 %reduce-scatter.22.cloned.1.call-done = f32[280,1536]{1,0:T(8,128)} async-done(((f32[8960,1536]{1,0:T(8,128)}), f32[280,1536]{1,0:T(8,128)}) %reduce-scatter.22.cloned.1.call-update) | async-done | bytes 1720336
  (186 shorter events, 110.3 us)
Async XLA Ops:
  7.2 53.6 %copy-start.32 = (s32[1,256]{1,0:T(1,128)S(1)}, s32[1,256]{1,0:T(1,128)}, u32[]{:S(2)}) copy-start(s32[1,256]{1,0:T(1,128)} %param.13) | copy-start | bytes 3076
  7.2 53.4 %copy-start.1 = (bf16[1,256,1536]{2,1,0:T(8,128)(2,1)S(1)}, bf16[1,256,1536]{2,1,0:T(8,128)(2,1)}, u32[]{:S(2)}) copy-start(bf16[1,256,1536]{2,1,0:T(8,128)(2,1)} %param.11) | copy-start | bytes 2359300
  7.2 72.9 %all-gather.6.cloned.1.call-start = ((), (), s32[]{:S(2)}) async-start(), calls=%async_computation.7 | async-start | bytes 6488064 | tf_op jit(solution)/shard_map/all_gather | solution.py:142
  7.9 138.3 %all-gather.8.cloned.1.call-start = ((), (), s32[]{:S(2)}) async-start(), calls=%async_computation.8 | async-start | bytes 4866048 | tf_op jit(solution)/shard_map/all_gather | solution.py:144
  8.7 303.8 %all-gather.10.cloned.1.call-start = ((), (), s32[]{:S(2)}) async-start(), calls=%async_computation.9 | async-start | bytes 28385280 | tf_op jit(solution)/shard_map/all_gather | solution.py:148
  9.4 469.4 %all-gather.12.cloned.1.call-start = ((), (), s32[]{:S(2)}) async-start(), calls=%async_computation.10 | async-start | bytes 28385280 | tf_op jit(solution)/shard_map/all_gather | solution.py:149
  10.0 635.1 %all-gather.14.cloned.1.call-start = ((), (), s32[]{:S(2)}) async-start(), calls=%async_computation.11 | async-start | bytes 28385280 | tf_op jit(solution)/shard_map/all_gather | solution.py:150
  10.6 732.5 %reduce-scatter.10.cloned.1.call-start = ((), (), s32[]{:S(2)}) async-start(), calls=%async_computation.12 | async-start | bytes 655360 | tf_op jit(solution)/shard_map/reduce_scatter | solution.py:246
  52.3 32.5 %copy-start.28 = (f32[1536]{0:T(1024)}, f32[1536]{0:T(1024)S(1)}, u32[]{:S(2)}) copy-start(f32[1536]{0:T(1024)S(1)} %convert_element_type.121) | copy-start | bytes 18436
  60.6 39.3 %copy-start.22 = (f32[256,128]{1,0:T(8,128)}, f32[256,128]{1,0:T(8,128)S(1)}, u32[]{:S(2)}) copy-start(f32[256,128]{1,0:T(8,128)S(1)} %get-tuple-element.38) | copy-start | bytes 393220
  60.8 19.3 copy-start.30
  150.0 531.4 %copy-start = (f32[256,1536]{1,0:T(8,128)}, f32[256,1536]{1,0:T(8,128)S(1)}, u32[]{:S(2)}) copy-start(f32[256,1536]{1,0:T(8,128)S(1)} %get-tuple-element.44) | copy-start | bytes 4718596
  150.2 328.6 %copy-start.6 = (bf16[256,1536]{1,0:T(8,128)(2,1)}, bf16[256,1536]{1,0:T(8,128)(2,1)S(1)}, u32[]{:S(2)}) copy-start(bf16[256,1536]{1,0:T(8,128)(2,1)S(1)} %multiply_convert_fusion.3) | copy-start | bytes 2359300
  681.4 17.5 slice-start
  681.4 17.5 slice-start.1
  717.3 53.1 %reduce-scatter.12.cloned.1.call-start = ((), (), s32[]{:S(2)}) async-start(), calls=%async_computation.13 | async-start | bytes 655360 | tf_op jit(solution)/shard_map/reduce_scatter | solution.py:252
  727.5 192.8 %reduce-scatter.16.cloned.1.call-start = ((), (), s32[]{:S(2)}) async-start(), calls=%async_computation.15 | async-start | bytes 9732096 | tf_op jit(solution)/shard_map/reduce_scatter | solution.py:275
  732.7 338.5 %reduce-scatter.14.cloned.1.call-start = ((), (), s32[]{:S(2)}) async-start(), calls=%async_computation.14 | async-start | bytes 12976128 | tf_op jit(solution)/shard_map/reduce_scatter | solution.py:273
  741.1 31.0 %copy-start.29 = (f32[1536]{0:T(1024)S(1)}, f32[1536]{0:T(1024)}, u32[]{:S(2)}) copy-start(f32[1536]{0:T(1024)} %copy-done.28) | copy-start | bytes 18436
  741.1 31.0 %copy-start.31 = (f32[256]{0:T(256)S(1)}, f32[256]{0:T(256)}, u32[]{:S(2)}) copy-start(f32[256]{0:T(256)} %copy-done.30) | copy-start | bytes 3076
  779.7 759.2 %reduce-scatter.18.cloned.1.call-start = ((), (), s32[]{:S(2)}) async-start(), calls=%async_computation.16 | async-start | bytes 56770560 | tf_op jit(solution)/shard_map/reduce_scatter | solution.py:220
  806.1 1198.8 %reduce-scatter.20.cloned.1.call-start = ((), (), s32[]{:S(2)}) async-start(), calls=%async_computation.17 | async-start | bytes 56770560 | tf_op jit(solution)/shard_map/reduce_scatter | solution.py:221
  832.0 1638.8 %reduce-scatter.22.cloned.1.call-start = ((), (), s32[]{:S(2)}) async-start(), calls=%async_computation.18 | async-start | bytes 56770560
  855.2 15.9 copy-start.2
  (29 other events, 108.1 us)
Sparse Core Ops, SparseCore 0:
  10.9 69.1 all-gather.5
  83.0 63.1 all-gather.7
  149.1 163.3 all-gather.9
  315.3 163.4 all-gather.11
  481.5 163.4 all-gather.13
  717.4 24.4 reduce-scatter.9
  745.3 25.0 reduce-scatter.11
  776.9 134.3 reduce-scatter.15
  917.9 153.3 reduce-scatter.13
  1078.1 460.7 reduce-scatter.17
  1545.9 458.9 reduce-scatter.19
  2011.7 458.9 reduce-scatter.21
where the time goes:
time: 2490 us; the launch traced here: 2480 us
  waiting for transfers between devices  2080 us (84%)
  matrix products  234 us (9%)
  blocking collectives  102 us (4%)
    unnamed x13, waiting for transfers between devices  469 us
    reduce_scatter x1, waiting for transfers between devices, on_device(): lax.psum_scatter(gate_term, ('dp', 'ctx'), scatter_dimension=0, tiled=True)  468 us
    reduce_scatter x1, waiting for transfers between devices, on_device(): lax.psum_scatter(up_term, ('dp', 'ctx'), scatter_dimension=0, tiled=True)  466 us
    all_gather x1, waiting for transfers between devices, on_device(): lax.all_gather(gate_weight, ('dp', 'ctx'), axis=0, tiled=True)  162 us
    all_gather x1, waiting for transfers between devices, on_device(): lax.all_gather(down_weight, ('dp', 'ctx'), axis=0, tiled=True)  151 us
    all_gather x1, waiting for transfers between devices, on_device(): lax.all_gather(up_weight, ('dp', 'ctx'), axis=0, tiled=True)  151 us
    reduce_scatter x1, waiting for transfers between devices, on_device(): lax.psum_scatter(qkv_term, ('dp', 'ctx'), scatter_dimension=0, tiled=True)  151 us
    unnamed x2, blocking collectives  77.4 us
  transfers between devices with their start and end apart: 12, of which 10 were waited for; matrix products, arithmetic and copies ran while one was open for 8% of the time, Pallas kernels for 0%

commit v1 on v0

v1 whole, which is shorter than its diff:
```python
import functools
import math

import jax
import jax.numpy as jnp
from jax import lax
from jax.sharding import PartitionSpec as P

H = 12
KV = 2
HD = 128
LANES = 128


EPS = 1e-06
THETA = 1000000.0
MASKED = -1e30
BF = jnp.bfloat16
F32 = jnp.float32
DP = ("far", "near")
ALL = ("far", "near", "ctx")


def rope_tables(positions):
    half_dim = jnp.arange(0, HD, 2).astype(F32) / HD
    inverse = THETA ** (-half_dim)
    angles = positions.astype(F32)[:, None] * inverse[None, :]
    angles = jnp.concatenate([angles, angles], axis=1)
    return (jnp.cos(angles), jnp.sin(angles))


def rotate(values, cos_table, sin_table):
    half_dim = values.shape[-1] // 2
    turned = jnp.concatenate([-values[..., half_dim:], values[..., :half_dim]], axis=-1)
    return values * cos_table[:, None, :] + turned * sin_table[:, None, :]


def inv_rms_of(values):
    return lax.rsqrt(jnp.mean(values * values, axis=-1, keepdims=True) + EPS)


def norm_back(normed_grad, values, inv_rms, gain):
    normed = values * inv_rms
    scaled_grad = normed_grad * gain
    return inv_rms * (scaled_grad - normed * jnp.mean(scaled_grad * normed, axis=-1, keepdims=True))


def dot(a, b):
    return jnp.dot(a, b, preferred_element_type=F32)


def dot_t(a, b):
    return lax.dot_general(a, b, (((1,), (1,)), ((), ())), preferred_element_type=F32)


def t_dot(a, b):
    return lax.dot_general(a, b, (((0,), (0,)), ((), ())), preferred_element_type=F32)


def attend(queries, key_rows, value_rows, visible, scale_factor):
    scores = jnp.einsum("tjd,nd->jtn", queries, key_rows, preferred_element_type=F32) * scale_factor
    scores = jnp.where(visible[None], scores, MASKED)
    row_max = jnp.max(scores, axis=-1, keepdims=True)
    row_sum = jnp.sum(jnp.exp(scores - row_max), axis=-1, keepdims=True)
    log_total = row_max + jnp.log(row_sum)
    weights = jnp.exp(scores - log_total).astype(BF)
    mixed = jnp.einsum("jtn,nd->tjd", weights, value_rows, preferred_element_type=F32)
    return mixed, log_total


def attend_back(
    queries, key_rows, value_rows, visible, attended, attended_grad, log_total, scale_factor
):
    scores = jnp.einsum("tjd,nd->jtn", queries, key_rows, preferred_element_type=F32) * scale_factor
    scores = jnp.where(visible[None], scores, MASKED)
    probs_full = jnp.exp(scores - log_total)
    probs_low = probs_full.astype(BF)
    value_grad = jnp.einsum("jtn,tjd->nd", probs_low, attended_grad, preferred_element_type=F32)
    prob_grad = jnp.einsum("tjd,nd->jtn", attended_grad, value_rows, preferred_element_type=F32)
    row_dot = jnp.sum(attended_grad.astype(F32) * attended.astype(F32), axis=-1).T
    score_grad = (probs_full * (prob_grad - row_dot[..., None]) * scale_factor).astype(BF)
    query_grad = jnp.einsum("jtn,nd->tjd", score_grad, key_rows, preferred_element_type=F32)
    key_grad = jnp.einsum("jtn,tjd->nd", score_grad, queries, preferred_element_type=F32)
    return query_grad, key_grad, value_grad


class Peers:
    def __init__(self, axis, size):
        self.axis = axis
        self.size = size
        self.paired = size & (size - 1) == 0
        self.me = lax.axis_index(axis)

    def to(self, index, step):
        return index ^ step if self.paired else (index + step) % self.size

    def source(self, step):
        return self.me ^ step if self.paired else (self.me - step + self.size) % self.size

    def spread(self, own):
        blocks = [own]
        for step in range(1, self.size):
            pairs = [(i, self.to(i, step)) for i in range(self.size)]
            blocks.append(lax.ppermute(own, self.axis, pairs))
        return blocks

    def exchange(self, parts):
        result = parts
        for step in range(1, self.size):
            source = self.source(step)
            pairs = [(self.to(i, step), i) for i in range(self.size)]
            got = lax.ppermute(lax.dynamic_index_in_dim(parts, source, 0), self.axis, pairs)
            target = source if self.paired else (self.me + step) % self.size
            result = lax.dynamic_update_slice_in_dim(result, got, target, 0)
        return result

    def shares(self, partial):
        return [partial(step).astype(BF) for step in range(self.size - 1, 0, -1)] + [partial(0)]

    def send(self, shares):
        received = shares[-1:]
        for step, share in zip(range(self.size - 1, 0, -1), shares):
            pairs = [(self.to(i, step), i) for i in range(self.size)]
            received.append(lax.ppermute(share, self.axis, pairs))
        return received

    def deliver(self, partial):
        return self.send(self.shares(partial))


def add_up(shares):
    return sum(share.astype(F32) for share in shares[1:]) + shares[0].astype(F32)


class Halves:
    def __init__(self, size):
        self.size = size

    def swap(self, own):
        return lax.ppermute(own, "far", [(i, self.size - 1 - i) for i in range(self.size)])


def pad_to(values, axis, size):
    widths = [(0, 0)] * values.ndim
    widths[axis] = (0, size - values.shape[axis])
    return jnp.pad(values, widths)


def round_up(value, unit):
    return -(-value // unit) * unit


class HeadSplit:
    def __init__(self, peers, dp_n, rows, bias_rows):
        self.peers = peers
        self.n = peers.size
        self.dp_n = dp_n
        self.rows = rows
        self.bias_rows = bias_rows
        self.share = self.n // KV
        self.heads = H // self.n
        self.q_cols = self.heads * HD
        self.cols = self.q_cols + 2 * HD
        self.bias_cols = -(-bias_rows // rows)
        self.width = self.cols + round_up(2 + self.bias_cols, LANES)

    @staticmethod
    def fits(n):
        return n % KV == 0 and H % n == 0

    def slices(self, values):
        rows = values.shape[0]
        query = values[:, : H * HD].reshape(rows, self.n, self.q_cols)
        both = values[:, H * HD :].reshape(rows, 2, KV, 1, HD)
        both = jnp.broadcast_to(both, (rows, 2, KV, self.share, HD)).reshape(rows, 2, self.n, HD)
        return jnp.concatenate([query, both[:, 0], both[:, 1]], axis=2)

    def gather(self, attn_gain, mlp_gain, qkv_weight, qkv_bias, out_weight):
        rows, n, dp_n = self.rows, self.n, self.dp_n
        bias = pad_to(qkv_bias, 0, self.bias_cols * rows).reshape(self.bias_cols, rows)
        extra = jnp.concatenate([attn_gain[None], mlp_gain[None], bias], axis=0).T
        extra = pad_to(extra, 1, self.width - self.cols)
        extra = jnp.broadcast_to(extra[:, None], (rows, n, extra.shape[1]))
        pack = jnp.concatenate([self.slices(qkv_weight), extra], axis=2).transpose(1, 0, 2)
        pack = lax.all_to_all(pack, "ctx", 0, 0, tiled=True).reshape(n * rows, self.width)
        moves = [(b, (b % dp_n) * n + b // dp_n) for b in range(dp_n * n)]
        out_block = lax.ppermute(out_weight, ALL, moves)
        self.out_rows, self.out_cols = out_weight.shape
        self.extra_rows = self.out_rows * self.out_cols // self.width
        pack = jnp.concatenate([pack, out_block.reshape(self.extra_rows, self.width)], axis=0)
        whole = lax.all_gather(pack, DP, axis=0, tiled=False)
        joint = whole[:, : n * rows].reshape(dp_n * n * rows, self.width)
        self.out_slice = whole[:, n * rows :].reshape(dp_n * self.out_rows, self.out_cols)
        self.qkv_slice = joint[:, : self.cols]
        bias = joint[:, self.cols + 2 : self.cols + 2 + self.bias_cols]
        bias = bias.reshape(dp_n * n, rows, self.bias_cols).transpose(0, 2, 1)
        bias = bias.reshape(dp_n * n, self.bias_cols * rows)[:, : self.bias_rows].reshape(-1)
        self.bias_slice = jnp.concatenate(
            [lax.dynamic_slice(bias, (start,), (size,)) for start, size in self.places()]
        ).astype(F32)
        return joint[:, self.cols].astype(F32), joint[:, self.cols + 1].astype(F32)

    def places(self):
        me = self.peers.me
        group = me // self.share
        return (
            (me * self.q_cols, self.q_cols),
            (H * HD + group * HD, HD),
            (H * HD + KV * HD + group * HD, HD),
        )

    def forward(self, blocks, segment_ids, gain, before):
        peers, n = self.peers, self.n
        span = blocks[0].shape[0]
        length = n * span
        starts = [peers.source(step) * span for step in range(n)]
        index = jnp.concatenate([start + jnp.arange(span, dtype=jnp.int32) for start in starts])
        segments = jnp.concatenate(peers.spread(segment_ids), axis=1)[0]
        doc_start = jnp.sum((segments[None, :] < segments[:, None]).astype(jnp.int32), axis=1)
        self.cos_table, self.sin_table = rope_tables(index - doc_start)
        self.visible = (index[None, :] <= index[:, None]) & (
            segments[None, :] == segments[:, None]
        )
        self.scale = 1.0 / math.sqrt(HD)
        self.resid = jnp.concatenate(blocks).astype(F32)
        self.inv = inv_rms_of(self.resid)
        self.normed = (self.resid * self.inv * gain).astype(BF)
        projected = dot(self.normed, self.qkv_slice) + self.bias_slice
        query_pre = projected[:, : self.q_cols].reshape(length, self.heads, HD)
        key_pre = projected[:, self.q_cols : self.q_cols + HD].reshape(length, 1, HD)
        self.values = projected[:, self.q_cols + HD :].astype(BF)
        self.query = rotate(query_pre, self.cos_table, self.sin_table).astype(BF)
        self.key = rotate(key_pre, self.cos_table, self.sin_table).astype(BF).reshape(length, HD)
        attended, self.log_total = attend(
            self.query, self.key, self.values, self.visible, self.scale
        )
        self.attended, before = lax.optimization_barrier((attended.astype(BF), before))
        flat = self.attended.reshape(length, self.q_cols)
        mixed = add_up(
            peers.deliver(lambda step: dot(flat[step * span : (step + 1) * span], self.out_slice))
        )
        return blocks[0].astype(F32) + mixed, before

    def backward(self, mid_grad, gain, gain_two_term, filler, after):
        peers, n, rows, dp_n = self.peers, self.n, self.rows, self.dp_n
        span = mid_grad.shape[0]
        blocks, filled = lax.optimization_barrier((peers.spread(mid_grad.astype(BF)), filler()))
        after = (after, filled)
        low = jnp.concatenate(blocks)
        length = low.shape[0]
        attended_grad = dot_t(low, self.out_slice).astype(BF).reshape(length, self.heads, HD)
        out_term = t_dot(self.attended.reshape(length, self.q_cols), low)
        query_grad, key_grad, value_grad = attend_back(
            self.query,
            self.key,
            self.values,
            self.visible,
            self.attended,
            attended_grad,
            self.log_total,
            self.scale,
        )
        query_grad = rotate(query_grad, self.cos_table, -self.sin_table).reshape(length, -1)
        key_grad = rotate(key_grad[:, None], self.cos_table, -self.sin_table).reshape(length, HD)
        proj_grad = jnp.concatenate([query_grad, key_grad, value_grad], axis=1)
        bias_term = jnp.sum(proj_grad, axis=0)
        low_grad = proj_grad.astype(BF)
        qkv_term = t_dot(self.normed, low_grad)
        gain_terms = []

        def share(step):
            part = slice(step * span, (step + 1) * span)
            normed_grad = dot_t(low_grad[part], self.qkv_slice)
            gain_terms.append(jnp.sum(normed_grad * (self.resid[part] * self.inv[part]), axis=0))
            return normed_grad

        normed_shares = peers.deliver(share)
        qkv_term, out_term = qkv_term.astype(BF), out_term.astype(BF)
        normed_grad = add_up(normed_shares)
        own = slice(0, span)
        input_grad = mid_grad + norm_back(normed_grad, self.resid[own], self.inv[own], gain)
        bias = jnp.zeros((dp_n * n * self.bias_rows,), F32)
        first = 0
        for start, size in self.places():
            bias = lax.dynamic_update_slice(bias, bias_term[first : first + size], (start,))
            first += size
        bias = pad_to(bias.reshape(dp_n * n, self.bias_rows), 1, self.bias_cols * rows)
        bias = bias.reshape(dp_n * n, self.bias_cols, rows).transpose(1, 0, 2)
        extra = jnp.concatenate(
            [sum(gain_terms)[None], gain_two_term[None], bias.reshape(self.bias_cols, -1)], axis=0
        ).T
        extra = pad_to(extra, 1, self.width - self.cols)
        joint = jnp.concatenate([qkv_term, extra.astype(BF)], axis=1)
        joint = joint.reshape(dp_n, n * rows, self.width)
        out_term = out_term.reshape(dp_n, self.extra_rows, self.width)
        pack, filled = lax.optimization_barrier((jnp.concatenate([joint, out_term], axis=1), after))
        mine = lax.psum_scatter(pack, DP, scatter_dimension=0, tiled=False)
        moves = [((b % dp_n) * n + b // dp_n, b) for b in range(dp_n * n)]
        out_grad = lax.ppermute(
            mine[n * rows :].reshape(self.out_rows, self.out_cols), ALL, moves
        ).astype(F32)
        parts = lax.all_to_all(
            mine[: n * rows].reshape(n, rows, self.width), "ctx", 0, 0, tiled=True
        ).astype(F32)
        query = parts[:, :, : self.q_cols].transpose(1, 0, 2).reshape(rows, -1)
        both = parts[:, :, self.q_cols : self.cols].reshape(KV, self.share, rows, 2, HD)
        both = jnp.sum(both, axis=1).transpose(1, 2, 0, 3).reshape(rows, -1)
        extra = jnp.sum(parts[:, :, self.cols :], axis=0)
        bias_grad = extra[:, 2 : 2 + self.bias_cols].T.reshape(-1)[: self.bias_rows]
        return (
            input_grad,
            extra[:, 0],
            jnp.concatenate([query, both], axis=1),
            bias_grad,
            out_grad,
            extra[:, 1],
        ), filled


class RowSplit:
    def __init__(self, peers):
        self.peers = peers

    def gather(self, attn_gain, mlp_gain, qkv_weight, qkv_bias, out_weight):
        gain_one, gain_two, self.qkv, bias, self.out = (
            lax.all_gather(part, ALL, axis=0, tiled=True)
            for part in (attn_gain, mlp_gain, qkv_weight, qkv_bias, out_weight)
        )
        self.bias = bias.astype(F32)
        return gain_one.astype(F32), gain_two.astype(F32)

    def forward(self, blocks, segment_ids, gain, before):
        own = blocks[0]
        span = own.shape[0]
        width = KV * HD
        segments = segment_ids[0]
        all_segments = lax.all_gather(segment_ids, "ctx", axis=1, tiled=True)[0]
        length = all_segments.shape[0]
        query_index = self.peers.me * span + jnp.arange(span, dtype=jnp.int32)
        key_index = jnp.arange(length, dtype=jnp.int32)
        doc_start = jnp.sum((all_segments[None] < segments[:, None]).astype(jnp.int32), axis=1)
        self.cos_table, self.sin_table = rope_tables(query_index - doc_start)
        self.visible = (key_index[None, :] <= query_index[:, None]) & (
            all_segments[None, :] == segments[:, None]
        )
        self.scale = 1.0 / math.sqrt(HD)
        self.resid = own.astype(F32)
        self.inv = inv_rms_of(self.resid)
        self.normed = (self.resid * self.inv * gain).astype(BF)
        projected = dot(self.normed, self.qkv) + self.bias
        query_pre = projected[:, : H * HD].reshape(span, H, HD)
        key_pre = projected[:, H * HD : H * HD + width].reshape(span, KV, HD)
        values = projected[:, H * HD + width :].astype(BF)
        self.query = rotate(query_pre, self.cos_table, self.sin_table).astype(BF)
        key_rot = rotate(key_pre, self.cos_table, self.sin_table).astype(BF).reshape(span, width)
        self.key, self.values = (
            lax.all_gather(part, "ctx", axis=0, tiled=True).reshape(length, KV, HD)
            for part in (key_rot, values)
        )
        pieces = [
            attend(
                self.query[:, self.part(group)],
                self.key[:, group],
                self.values[:, group],
                self.visible,
                self.scale,
            )
            for group in range(KV)
        ]
        self.attended = jnp.concatenate([piece[0] for piece in pieces], axis=1).astype(BF)
        self.log_totals = [piece[1] for piece in pieces]
        return self.resid + dot(self.attended.reshape(span, -1), self.out), before

    @staticmethod
    def part(group):
        return slice(group * (H // KV), (group + 1) * (H // KV))

    def backward(self, mid_grad, gain, gain_two_term, filler, after):
        span = mid_grad.shape[0]
        low = mid_grad.astype(BF)
        attended_grad = dot_t(low, self.out).astype(BF).reshape(span, H, HD)
        grads = [
            attend_back(
                self.query[:, self.part(group)],
                self.key[:, group],
                self.values[:, group],
                self.visible,
                self.attended[:, self.part(group)],
                attended_grad[:, self.part(group)],
                self.log_totals[group],
                self.scale,
            )
            for group in range(KV)
        ]
        query_grad = jnp.concatenate([grad[0] for grad in grads], axis=1)
        key_grad, value_grad = (
            lax.psum_scatter(
                jnp.concatenate([grad[place] for grad in grads], axis=1).astype(BF),
                "ctx",
                scatter_dimension=0,
                tiled=True,
            ).astype(F32)
            for place in (1, 2)
        )
        query_grad = rotate(query_grad, self.cos_table, -self.sin_table).reshape(span, -1)
        key_grad = rotate(key_grad.reshape(span, KV, HD), self.cos_table, -self.sin_table)
        proj_grad = jnp.concatenate([query_grad, key_grad.reshape(span, -1), value_grad], axis=1)
        low_grad = proj_grad.astype(BF)
        normed_grad = dot_t(low_grad, self.qkv)
        input_grad = mid_grad + norm_back(normed_grad, self.resid, self.inv, gain)
        gain_term = jnp.sum(normed_grad * (self.resid * self.inv), axis=0)
        terms = (
            gain_term,
            t_dot(self.normed, low_grad).astype(BF),
            jnp.sum(proj_grad, axis=0),
            t_dot(self.attended.reshape(span, -1), low).astype(BF),
            gain_two_term,
        )
        grads = (input_grad,) + tuple(
            lax.psum_scatter(term, ALL, scatter_dimension=0, tiled=True).astype(F32)
            for term in terms
        )
        return grads, (after, filler())


def on_device(
    inputs,
    cotangent,
    segment_ids,
    attn_gain,
    qkv_weight,
    qkv_bias,
    out_weight,
    mlp_gain,
    gate_weight,
    up_weight,
    down_weight,
    *,
    far_n,
    near_n,
    ctx_n,
):
    span, features = inputs.shape[1:]
    rows, hidden_width = gate_weight.shape
    n = ctx_n
    dp_n = far_n * near_n
    peers = Peers("ctx", n)
    halves = Halves(far_n)
    if HeadSplit.fits(n):
        attention = HeadSplit(peers, dp_n, rows, qkv_bias.shape[0])
        blocks = peers.spread(inputs[0])
    else:
        attention = RowSplit(peers)
        blocks = [inputs[0]]
    gain_one, gain_two = attention.gather(attn_gain, mlp_gain, qkv_weight, qkv_bias, out_weight)

    unit = hidden_width // (dp_n * n)
    width = near_n * unit
    wide = round_up(width, LANES)
    places = far_n * n

    def column_slices(weight):
        parts = weight.reshape(rows, far_n, near_n, n, unit).transpose(1, 3, 0, 2, 4)
        return pad_to(parts.reshape(places, rows, width), 2, wide)

    def weight_columns(values):
        parts = values.reshape(far_n, n, rows, near_n, unit).transpose(2, 0, 3, 1, 4)
        return parts.reshape(rows, hidden_width).astype(F32)

    joint = jnp.concatenate([column_slices(gate_weight), column_slices(up_weight)], axis=2)
    if far_n == 1:
        joint = peers.exchange(joint)
    else:
        joint = lax.all_to_all(joint, ("far", "ctx"), 0, 0, tiled=True)
    gate_up = lax.all_gather(joint.reshape(places * rows, 2 * wide), "near", axis=0, tiled=True)
    down = lax.all_gather(down_weight, "near", axis=0, tiled=True)

    def to_gathered(values):
        parts = values.reshape(span, far_n, near_n, -1).transpose(0, 2, 1, 3)
        return parts.reshape(span, features)

    def from_gathered(values):
        parts = values.reshape(span, near_n, far_n, -1).transpose(0, 2, 1, 3)
        return parts.reshape(span, features)

    def spread_wide(own):
        return sum([peers.spread(own if far == 0 else halves.swap(own)) for far in range(far_n)], [])

    def block(values, far, step):
        start = (far * n + step) * span
        return values[start : start + span]

    grad_out = spread_wide(cotangent[0])
    resid_mid, grad_out = attention.forward(blocks, segment_ids, gain_one, grad_out)
    inv_two = inv_rms_of(resid_mid)
    normed_own = (resid_mid * inv_two * gain_two).astype(BF)
    normed = jnp.concatenate(spread_wide(to_gathered(normed_own)))
    grad_out = jnp.concatenate(grad_out)
    pre = dot(normed, gate_up)
    gate_pre = pre[:, :width]
    up_pre = pre[:, wide : wide + width]
    sigmoid_gate = jax.nn.sigmoid(gate_pre)
    silu_gate = gate_pre * sigmoid_gate
    hidden = (silu_gate * up_pre).astype(BF)
    down_term = t_dot(hidden, grad_out).astype(BF)
    down_term, grad_out = lax.optimization_barrier((down_term, grad_out))
    down_grad = lax.psum_scatter(down_term, "near", scatter_dimension=0, tiled=True)
    hidden_grad = dot_t(grad_out, down)
    gate_grad = (
        hidden_grad * up_pre * sigmoid_gate * (1.0 + gate_pre * (1.0 - sigmoid_gate))
    ).astype(BF)
    up_grad = (hidden_grad * silu_gate).astype(BF)
    pre_grad = jnp.concatenate([pad_to(gate_grad, 1, wide), pad_to(up_grad, 1, wide)], axis=1)
    shares = [
        peers.deliver(lambda step: dot_t(block(pre_grad, far, step), gate_up))
        for far in range(far_n - 1, -1, -1)
    ]
    joint_term = t_dot(normed, pre_grad).astype(BF)
    shares, joint_term = lax.optimization_barrier((shares, joint_term))
    joint_term, down_grad = lax.optimization_barrier((joint_term, down_grad))
    joint_grad = lax.psum_scatter(joint_term, "near", scatter_dimension=0, tiled=True)
    def combine(shares):
        if far_n == 1:
            return add_up(shares[0])
        swapped = halves.swap(add_up(shares[0]).astype(BF))
        return add_up(shares[1] + [swapped])

    def output_shares():
        return [
            peers.shares(lambda step: dot(block(hidden, far, step), down))
            for far in range(far_n - 1, -1, -1)
        ]

    normed_two_grad = from_gathered(combine(shares))
    normed_two = resid_mid * inv_two
    gain_two_term = jnp.sum(normed_two_grad * normed_two, axis=0)
    mid_grad = cotangent[0].astype(F32) + norm_back(normed_two_grad, resid_mid, inv_two, gain_two)
    grads, (joint_grad, out_shares) = attention.backward(
        mid_grad, gain_one, gain_two_term, output_shares, joint_grad
    )
    joint_grad = lax.all_to_all(
        joint_grad.reshape(places, rows, 2 * wide), ("far", "ctx"), 0, 0, tiled=True
    )
    gate_weight_grad = weight_columns(joint_grad[:, :, :width])
    up_weight_grad = weight_columns(joint_grad[:, :, wide : wide + width])
    input_grad, attn_gain_grad, qkv_weight_grad, qkv_bias_grad, out_weight_grad, mlp_gain_grad = (
        grads
    )
    output = resid_mid + combine([peers.send(shares) for shares in out_shares])
    return (
        output.astype(BF)[None],
        input_grad[None],
        attn_gain_grad,
        qkv_weight_grad,
        qkv_bias_grad,
        out_weight_grad,
        mlp_gain_grad,
        gate_weight_grad,
        up_weight_grad,
        down_grad.astype(F32),
    )


def solution(mesh):
    dp_n, ctx_n = mesh.shape["dp"], mesh.shape["ctx"]
    far_n = 1
    split = jax.sharding.Mesh(mesh.devices.reshape(far_n, dp_n // far_n, ctx_n), ALL)
    body = functools.partial(on_device, far_n=far_n, near_n=dp_n // far_n, ctx_n=ctx_n)
    return jax.shard_map(
        body,
        mesh=split,
        in_specs=(
            P(DP, "ctx", None),
            P(DP, "ctx", None),
            P(DP, "ctx"),
            P(ALL),
            P(ALL, None),
            P(ALL),
            P(ALL, None),
            P(ALL),
            P(ALL, None),
            P(ALL, None),
            P(ALL, None),
        ),
        out_specs=(
            P(DP, "ctx", None),
            P(DP, "ctx", None),
            P(ALL),
            P(ALL, None),
            P(ALL),
            P(ALL, None),
            P(ALL),
            P(ALL, None),
            P(ALL, None),
            P(ALL, None),
        ),
        check_vma=False,
    )
```

time: 2490 us -> 618 us (0.25)
  the two profiles are of different devices: /device:TPU:25 before, /device:TPU:0 now
where the time goes in v1:
time: 618 us; the launch traced here: 610 us
  waiting for transfers between devices  219 us (35%)
  matrix products  176 us (28%)
  local copies, waits for them, and re-layouts  78.2 us (13%)
  starting transfers between devices  62.3 us (10%)
  other arithmetic  58.2 us (9%)
  between operations  15.9 us (3%)
    ppermute x15, waiting for transfers between devices, spread(): blocks.append(lax.ppermute(own, self.axis, pairs))  81.2 us
    dot_general x10, matrix products, dot_t(): lax.dot_general(a, b, (((1,), (1,)), ((), ())), preferred_element_type=F32)  75.4 us
    ppermute x12, waiting for transfers between devices, send(): received.append(lax.ppermute(share, self.axis, pairs))  73.4 us
    dot_general x10, matrix products, dot(): return jnp.dot(a, b, preferred_element_type=F32)  40.9 us
    dot_general x4, matrix products, t_dot(): lax.dot_general(a, b, (((0,), (0,)), ((), ())), preferred_element_type=F32)  38 us
    ppermute x3, waiting for transfers between devices, exchange(): lax.ppermute(lax.dynamic_index_in_dim(parts, source, 0), self.axis, pairs)  26.7 us
    ppermute x15, starting transfers between devices, spread(): blocks.append(lax.ppermute(own, self.axis, pairs))  19.4 us
    unnamed x144, local copies, waits for them, and re-layouts  19 us
  transfers between devices with their start and end apart: 41, of which 20 were waited for; matrix products, arithmetic and copies ran while one was open for 47% of the time, Pallas kernels for 0%

profile of v1, /device:TPU:0, one launch (start us, length us, event | category | flops | bytes accessed | tf_op | source)
XLA Modules:
  0.0 609.6 jit_solution(8701064157352462139)
XLA Ops:
  41.0 9.8 %collective-permute-done.16 = bf16[1,48,4608]{2,1,0:T(8,128)(2,1)} collective-permute-done((bf16[1,48,4608]{2,1,0:T(8,128)(2,1)S(1)}, bf16[1,48,4608]{2,1,0:T(8,128)(2,1)}, u32[]{:S(2)}, u32[]{:S(2)}) %collective-permute-start.16) | collective-permute-done | bytes 442400 | tf_op jit(solution)/shard_map/ppermute | solution.py:112
  55.5 17.0 %collective-permute-done.17 = bf16[1,48,4608]{2,1,0:T(8,128)(2,1)S(1)} collective-permute-done((bf16[1,48,4608]{2,1,0:T(8,128)(2,1)S(1)}, bf16[1,48,4608]{2,1,0:T(8,128)(2,1)S(1)}, u32[]{:S(2)}, u32[]{:S(2)}) %collective-permute-start.17) | collective-permute-done | bytes 442400 | tf_op jit(solution)/shard_map/ppermute | solution.py:112
  80.2 11.5 %collective-permute-done.4 = s32[1,256]{1,0:T(1,128)S(1)} collective-permute-done((s32[1,256]{1,0:T(1,128)S(1)}, s32[1,256]{1,0:T(1,128)S(1)}, u32[]{:S(2)}, u32[]{:S(2)}) %collective-permute-start.4) | collective-permute-done | bytes 1056 | tf_op jit(solution)/shard_map/ppermute | solution.py:104
  100.7 12.4 %collective-permute-done.2 = bf16[256,1536]{1,0:T(8,128)(2,1)S(1)} collective-permute-done((bf16[256,1536]{1,0:T(8,128)(2,1)S(1)}, bf16[256,1536]{1,0:T(8,128)(2,1)S(1)}, u32[]{:S(2)}, u32[]{:S(2)}) %collective-permute-start.2) | collective-permute-done | bytes 786464 | tf_op jit(solution)/shard_map/ppermute | solution.py:104
  155.8 15.2 %collective-permute-done.10 = bf16[256,1536]{1,0:T(8,128)(2,1)S(1)} collective-permute-done((bf16[256,1536]{1,0:T(8,128)(2,1)S(1)}, bf16[256,1536]{1,0:T(8,128)(2,1)S(1)}, u32[]{:S(2)}, u32[]{:S(2)}) %collective-permute-start.10) | collective-permute-done | bytes 786464 | tf_op jit(solution)/shard_map/ppermute | solution.py:124
  171.1 13.0 %collective-permute-done.11 = bf16[256,1536]{1,0:T(8,128)(2,1)S(1)} collective-permute-done((bf16[256,1536]{1,0:T(8,128)(2,1)S(1)}, bf16[256,1536]{1,0:T(8,128)(2,1)S(1)}, u32[]{:S(2)}, u32[]{:S(2)}) %collective-permute-start.11) | collective-permute-done | bytes 786464 | tf_op jit(solution)/shard_map/ppermute | solution.py:124
  193.7 12.1 %collective-permute-done.13 = bf16[256,1536]{1,0:T(8,128)(2,1)S(1)} collective-permute-done((bf16[256,1536]{1,0:T(8,128)(2,1)S(1)}, bf16[256,1536]{1,0:T(8,128)(2,1)S(1)}, u32[]{:S(2)}, u32[]{:S(2)}) %collective-permute-start.13) | collective-permute-done | bytes 786464 | tf_op jit(solution)/shard_map/ppermute | solution.py:104
  205.8 15.2 %collective-permute-done.14 = bf16[256,1536]{1,0:T(8,128)(2,1)S(1)} collective-permute-done((bf16[256,1536]{1,0:T(8,128)(2,1)S(1)}, bf16[256,1536]{1,0:T(8,128)(2,1)S(1)}, u32[]{:S(2)}, u32[]{:S(2)}) %collective-permute-start.14) | collective-permute-done | bytes 786464 | tf_op jit(solution)/shard_map/ppermute | solution.py:104
  222.8 17.8 %fusion.47 = f32[1024,4608]{1,0:T(8,128)S(1)} fusion(bf16[1536,4608]{1,0:T(8,128)(2,1)} %all-gather.5.cloned.1.call-done, bf16[256,1536]{1,0:T(8,128)(2,1)} %collective-permute-done.15, bf16[256,1536]{1,0:T(8,128)(2,1)S(1)} %collective-permute-done.14, bf16[256,1536]{1,0:T(8,128)(2,1)S(1)} %collective-permute-done.13, ...), kind=kOutput, calls=%fused_computation.118 | convolution fusion | flops 14508097536 | bytes 36175872 | tf_op jit(solution)/shard_map/dot_general | solution.py:49
  250.3 9.5 %convolution_convert_fusion.1 = bf16[2240,1536]{1,0:T(8,128)(2,1)} fusion(bf16[1024,2240]{1,0:T(8,128)(2,1)S(1)} %multiply_convert_fusion.2, bf16[1024,1536]{1,0:T(8,128)(2,1)S(1)} %copy-done.50), kind=kOutput, calls=%fused_computation.12 | convolution fusion | flops 7049871360 | bytes 14614528 | tf_op jit(solution)/shard_map/dot_general | solution.py:57
  259.8 13.8 %all-gather.7.cloned.1.call-done = bf16[2240,1536]{1,0:T(8,128)(2,1)} async-done(((bf16[280,1536]{1,0:T(8,128)(2,1)}), bf16[2240,1536]{1,0:T(8,128)(2,1)}) %all-gather.7.cloned.1.call-update) | async-done | bytes 6881296 | tf_op jit(solution)/shard_map/all_gather | solution.py:476
  273.6 18.6 %multiply_convert_fusion.1 = (bf16[1024,2240]{1,0:T(8,128)(2,1)}, bf16[1024,2240]{1,0:T(8,128)(2,1)}) fusion(f32[1024,4608]{1,0:T(8,128)} %copy-done.7, bf16[1024,1536]{1,0:T(8,128)(2,1)} %copy-done.49, bf16[2240,1536]{1,0:T(8,128)(2,1)} %all-gather.7.cloned.1.call-done), kind=kOutput, calls=%fused_computation.16 | convolution fusion | flops 7076249600 | bytes 37552128 | tf_op jit(solution)/shard_map/dot_general | solution.py:53
  292.2 9.0 %fusion.6 = bf16[1024,4608]{1,0:T(8,128)(2,1)} fusion(bf16[1024,2240]{1,0:T(8,128)(2,1)} %get-tuple-element.81, bf16[1024,2240]{1,0:T(8,128)(2,1)} %get-tuple-element.80), kind=kLoop, calls=%fused_computation.14 | loop fusion | flops 37748736 | bytes 18612224 | tf_op jit(solution)/shard_map/concatenate | solution.py:513
  301.2 10.6 %convolution_convert_fusion.7 = bf16[256,1536]{1,0:T(8,128)(2,1)} fusion(bf16[1536,4608]{1,0:T(8,128)(2,1)} %all-gather.5.cloned.1.call-done, bf16[1024,4608]{1,0:T(8,128)(2,1)} %fusion.6), kind=kOutput, calls=%fused_computation.40 | convolution fusion | flops 3624271872 | bytes 17301504 | tf_op jit(solution)/shard_map/dot_general | solution.py:53
  313.3 10.6 %convolution_convert_fusion.8 = bf16[256,1536]{1,0:T(8,128)(2,1)} fusion(bf16[1536,4608]{1,0:T(8,128)(2,1)} %all-gather.5.cloned.1.call-done, bf16[1024,4608]{1,0:T(8,128)(2,1)} %fusion.6), kind=kOutput, calls=%fused_computation.41 | convolution fusion | flops 3624271872 | bytes 17301504 | tf_op jit(solution)/shard_map/dot_general | solution.py:53
  325.4 10.6 %convolution_convert_fusion.9 = bf16[256,1536]{1,0:T(8,128)(2,1)} fusion(bf16[1536,4608]{1,0:T(8,128)(2,1)} %all-gather.5.cloned.1.call-done, bf16[1024,4608]{1,0:T(8,128)(2,1)} %fusion.6), kind=kOutput, calls=%fused_computation.42 | convolution fusion | flops 3624271872 | bytes 17301504 | tf_op jit(solution)/shard_map/dot_general | solution.py:53
  336.6 21.4 %convolution_convert_fusion = bf16[1536,4608]{1,0:T(8,128)(2,1)} fusion(bf16[256,1536]{1,0:T(8,128)(2,1)} %collective-permute-done.15, bf16[256,1536]{1,0:T(8,128)(2,1)S(1)} %collective-permute-done.14, bf16[256,1536]{1,0:T(8,128)(2,1)S(1)} %collective-permute-done.13, bf16[256,1536]{1,0:T(8,128)(2,1)S(1)} %multiply_convert_fusion.4, ...), kind=kOutput, calls=%fused_computation | convolution fusion | flops 14552924160 | bytes 26476544 | tf_op jit(solution)/shard_map/dot_general | solution.py:57
  358.0 10.7 %fusion.16 = f32[256,1536]{1,0:T(8,128)} fusion(bf16[1536,4608]{1,0:T(8,128)(2,1)} %all-gather.5.cloned.1.call-done, bf16[1024,4608]{1,0:T(8,128)(2,1)} %fusion.6), kind=kOutput, calls=%fused_computation.50 | convolution fusion | flops 3623878656 | bytes 18087936 | tf_op jit(solution)/shard_map/dot_general | solution.py:53
  398.2 11.1 %collective-permute-done.22 = bf16[256,1536]{1,0:T(8,128)(2,1)S(1)} collective-permute-done((bf16[256,1536]{1,0:T(8,128)(2,1)S(1)}, bf16[256,1536]{1,0:T(8,128)(2,1)S(1)}, u32[]{:S(2)}, u32[]{:S(2)}) %collective-permute-start.22) | collective-permute-done | bytes 786464 | tf_op jit(solution)/shard_map/ppermute | solution.py:104
  409.4 17.0 %collective-permute-done.23 = bf16[256,1536]{1,0:T(8,128)(2,1)S(1)} collective-permute-done((bf16[256,1536]{1,0:T(8,128)(2,1)S(1)}, bf16[256,1536]{1,0:T(8,128)(2,1)S(1)}, u32[]{:S(2)}, u32[]{:S(2)}) %collective-permute-start.23) | collective-permute-done | bytes 786464 | tf_op jit(solution)/shard_map/ppermute | solution.py:104
  473.1 14.5 %collective-permute-done.29 = bf16[256,1536]{1,0:T(8,128)(2,1)} collective-permute-done((bf16[256,1536]{1,0:T(8,128)(2,1)}, bf16[256,1536]{1,0:T(8,128)(2,1)}, u32[]{:S(2)}, u32[]{:S(2)}) %collective-permute-start.29) | collective-permute-done | bytes 786464 | tf_op jit(solution)/shard_map/ppermute | solution.py:124
  522.3 11.0 %collective-permute-done.25 = bf16[256,1536]{1,0:T(8,128)(2,1)} collective-permute-done((bf16[256,1536]{1,0:T(8,128)(2,1)}, bf16[256,1536]{1,0:T(8,128)(2,1)}, u32[]{:S(2)}, u32[]{:S(2)}) %collective-permute-start.25) | collective-permute-done | bytes 786464 | tf_op jit(solution)/shard_map/ppermute | solution.py:124
  533.3 16.9 %collective-permute-done.26 = bf16[256,1536]{1,0:T(8,128)(2,1)} collective-permute-done((bf16[256,1536]{1,0:T(8,128)(2,1)}, bf16[256,1536]{1,0:T(8,128)(2,1)}, u32[]{:S(2)}, u32[]{:S(2)}) %collective-permute-start.26) | collective-permute-done | bytes 786464 | tf_op jit(solution)/shard_map/ppermute | solution.py:124
  559.7 12.0 %all-to-all-done.2 = bf16[4,48,4608]{2,1,0:T(8,128)(2,1)} async-done(((bf16[4,48,4608]{2,1,0:T(8,128)(2,1)}), bf16[4,48,4608]{2,1,0:T(8,128)(2,1)}, u32[]{:S(2)}, u32[]{:S(2)}) %all-to-all-start.2) | async-done | bytes 1769504 | tf_op jit(solution)/shard_map/all_to_all | solution.py:541
  (364 shorter events, 272.1 us)
Async XLA Ops:
  16.9 97.0 %all-gather.9.cloned.1.call-start = ((), (), s32[]{:S(2)}) async-start(), calls=%async_computation.11 | async-start | bytes 3981312 | tf_op jit(solution)/shard_map/all_gather | solution.py:191
  23.3 199.5 %all-gather.5.cloned.1.call-start = ((), (), s32[]{:S(2)}) async-start(), calls=%async_computation.6 | async-start | bytes 15925248 | tf_op jit(solution)/shard_map/all_gather | solution.py:475
  73.8 199.8 %all-gather.7.cloned.1.call-start = ((), (), s32[]{:S(2)}) async-start(), calls=%async_computation.7 | async-start | bytes 7741440 | tf_op jit(solution)/shard_map/all_gather | solution.py:476
  80.0 288.7 %reduce-scatter.4.cloned.1.call-start = ((), (), s32[]{:S(2)}) async-start(), calls=%async_computation.8 | async-start | bytes 7741440 | tf_op jit(solution)/shard_map/reduce_scatter | solution.py:507
  94.2 50.5 %collective-permute-start.7 = (bf16[256,1536]{1,0:T(8,128)(2,1)}, bf16[256,1536]{1,0:T(8,128)(2,1)}, u32[]{:S(2)}, u32[]{:S(2)}) collective-permute-start(bf16[256,1536]{1,0:T(8,128)(2,1)} %bitcast.25), channel_id=1, source_target_pairs={{0,1},{1,0},{2,3},{3,2},{4,5},{5,4},{6,7},{7,6},{8,9},{9,8},{10,11... | collective-permute-start | bytes 2359304 | tf_op jit(solution)/shard_map/ppermute | solution.py:104
  96.4 48.4 %collective-permute-start.8 = (bf16[256,1536]{1,0:T(8,128)(2,1)}, bf16[256,1536]{1,0:T(8,128)(2,1)}, u32[]{:S(2)}, u32[]{:S(2)}) collective-permute-start(bf16[256,1536]{1,0:T(8,128)(2,1)} %bitcast.25), channel_id=1, source_target_pairs={{0,2},{1,3},{2,0},{3,1},{4,6},{5,7},{6,4},{7,5},{8,10},{9,11},{10,... | collective-permute-start | bytes 2359304 | tf_op jit(solution)/shard_map/ppermute | solution.py:104
  99.1 45.6 %collective-permute-start.9 = (bf16[256,1536]{1,0:T(8,128)(2,1)}, bf16[256,1536]{1,0:T(8,128)(2,1)}, u32[]{:S(2)}, u32[]{:S(2)}) collective-permute-start(bf16[256,1536]{1,0:T(8,128)(2,1)} %bitcast.25), channel_id=1, source_target_pairs={{0,3},{1,2},{2,1},{3,0},{4,7},{5,6},{6,5},{7,4},{8,11},{9,10},{10,... | collective-permute-start | bytes 2359304 | tf_op jit(solution)/shard_map/ppermute | solution.py:104
  152.8 31.2 %collective-permute-start.11 = (bf16[256,1536]{1,0:T(8,128)(2,1)S(1)}, bf16[256,1536]{1,0:T(8,128)(2,1)S(1)}, u32[]{:S(2)}, u32[]{:S(2)}) collective-permute-start(bf16[256,1536]{1,0:T(8,128)(2,1)S(1)} %convolution_convert_fusion.11), channel_id=1, source_target_pairs={{2,0},{3,1},{0,2},{1,3},{6,4},{7,5},{4,6},{5,7},{10,8},{11,9},{8,1... | collective-permute-start | bytes 2359304 | tf_op jit(solution)/shard_map/ppermute | solution.py:124
  154.4 29.7 %collective-permute-start.12 = (bf16[256,1536]{1,0:T(8,128)(2,1)S(1)}, bf16[256,1536]{1,0:T(8,128)(2,1)S(1)}, u32[]{:S(2)}, u32[]{:S(2)}) collective-permute-start(bf16[256,1536]{1,0:T(8,128)(2,1)S(1)} %convolution_convert_fusion.10), channel_id=1, source_target_pairs={{1,0},{0,1},{3,2},{2,3},{5,4},{4,5},{7,6},{6,7},{9,8},{8,9},{11,10... | collective-permute-start | bytes 2359304 | tf_op jit(solution)/shard_map/ppermute | solution.py:124
  185.9 35.1 %collective-permute-start.14 = (bf16[256,1536]{1,0:T(8,128)(2,1)S(1)}, bf16[256,1536]{1,0:T(8,128)(2,1)S(1)}, u32[]{:S(2)}, u32[]{:S(2)}) collective-permute-start(bf16[256,1536]{1,0:T(8,128)(2,1)S(1)} %multiply_convert_fusion.4), channel_id=1, source_target_pairs={{0,2},{1,3},{2,0},{3,1},{4,6},{5,7},{6,4},{7,5},{8,10},{9,11},{10,... | collective-permute-start | bytes 2359304 | tf_op jit(solution)/shard_map/ppermute | solution.py:104
  187.4 35.4 %collective-permute-start.15 = (bf16[256,1536]{1,0:T(8,128)(2,1)S(1)}, bf16[256,1536]{1,0:T(8,128)(2,1)}, u32[]{:S(2)}, u32[]{:S(2)}) collective-permute-start(bf16[256,1536]{1,0:T(8,128)(2,1)S(1)} %multiply_convert_fusion.4), channel_id=1, source_target_pairs={{0,3},{1,2},{2,1},{3,0},{4,7},{5,6},{6,5},{7,4},{8,11},{9,10},{10,... | collective-permute-start | bytes 2359304 | tf_op jit(solution)/shard_map/ppermute | solution.py:104
  259.7 251.8 %reduce-scatter.6.cloned.1.call-start = ((), (), s32[]{:S(2)}) async-start(), calls=%async_computation.9 | async-start | bytes 15925248 | tf_op jit(solution)/shard_map/reduce_scatter | solution.py:521
  311.9 56.9 %collective-permute-start.21 = (bf16[256,1536]{1,0:T(8,128)(2,1)}, bf16[256,1536]{1,0:T(8,128)(2,1)}, u32[]{:S(2)}, u32[]{:S(2)}) collective-permute-start(bf16[256,1536]{1,0:T(8,128)(2,1)} %convolution_convert_fusion.7), channel_id=1, source_target_pairs={{1,0},{0,1},{3,2},{2,3},{5,4},{4,5},{7,6},{6,7},{9,8},{8,9},{11,10... | collective-permute-start | bytes 2359304 | tf_op jit(solution)/shard_map/ppermute | solution.py:124
  323.9 44.8 %collective-permute-start.20 = (bf16[256,1536]{1,0:T(8,128)(2,1)}, bf16[256,1536]{1,0:T(8,128)(2,1)}, u32[]{:S(2)}, u32[]{:S(2)}) collective-permute-start(bf16[256,1536]{1,0:T(8,128)(2,1)} %convolution_convert_fusion.8), channel_id=1, source_target_pairs={{2,0},{3,1},{0,2},{1,3},{6,4},{7,5},{4,6},{5,7},{10,8},{11,9},{8,1... | collective-permute-start | bytes 2359304 | tf_op jit(solution)/shard_map/ppermute | solution.py:124
  336.0 32.7 %collective-permute-start.19 = (bf16[256,1536]{1,0:T(8,128)(2,1)}, bf16[256,1536]{1,0:T(8,128)(2,1)}, u32[]{:S(2)}, u32[]{:S(2)}) collective-permute-start(bf16[256,1536]{1,0:T(8,128)(2,1)} %convolution_convert_fusion.9), channel_id=1, source_target_pairs={{3,0},{2,1},{1,2},{0,3},{7,4},{6,5},{5,6},{4,7},{11,8},{10,9},{9,1... | collective-permute-start | bytes 2359304 | tf_op jit(solution)/shard_map/ppermute | solution.py:124
  368.8 187.6 %reduce-scatter.8.cloned.1.call-start = ((), (), s32[]{:S(2)}) async-start(), calls=%async_computation.10 | async-start | bytes 3981312 | tf_op jit(solution)/shard_map/reduce_scatter | solution.py:297
  390.6 35.8 %collective-permute-start.23 = (bf16[256,1536]{1,0:T(8,128)(2,1)S(1)}, bf16[256,1536]{1,0:T(8,128)(2,1)S(1)}, u32[]{:S(2)}, u32[]{:S(2)}) collective-permute-start(bf16[256,1536]{1,0:T(8,128)(2,1)S(1)} %fusion.68), channel_id=1, source_target_pairs={{0,2},{1,3},{2,0},{3,1},{4,6},{5,7},{6,4},{7,5},{8,10},{9,11},{10,... | collective-permute-start | bytes 2359304 | tf_op jit(solution)/shard_map/ppermute | solution.py:104
  392.1 34.3 %collective-permute-start.24 = (bf16[256,1536]{1,0:T(8,128)(2,1)S(1)}, bf16[256,1536]{1,0:T(8,128)(2,1)S(1)}, u32[]{:S(2)}, u32[]{:S(2)}) collective-permute-start(bf16[256,1536]{1,0:T(8,128)(2,1)S(1)} %fusion.68), channel_id=1, source_target_pairs={{0,3},{1,2},{2,1},{3,0},{4,7},{5,6},{6,5},{7,4},{8,11},{9,10},{10,... | collective-permute-start | bytes 2359304 | tf_op jit(solution)/shard_map/ppermute | solution.py:104
  455.0 32.6 %collective-permute-start.29 = (bf16[256,1536]{1,0:T(8,128)(2,1)}, bf16[256,1536]{1,0:T(8,128)(2,1)}, u32[]{:S(2)}, u32[]{:S(2)}) collective-permute-start(bf16[256,1536]{1,0:T(8,128)(2,1)} %get-tuple-element.119), channel_id=1, source_target_pairs={{2,0},{3,1},{0,2},{1,3},{6,4},{7,5},{4,6},{5,7},{10,8},{11,9},{8,1... | collective-permute-start | bytes 2359304 | tf_op jit(solution)/shard_map/ppermute | solution.py:124
  458.5 29.2 %collective-permute-start.30 = (bf16[256,1536]{1,0:T(8,128)(2,1)}, bf16[256,1536]{1,0:T(8,128)(2,1)}, u32[]{:S(2)}, u32[]{:S(2)}) collective-permute-start(bf16[256,1536]{1,0:T(8,128)(2,1)} %get-tuple-element.117), channel_id=1, source_target_pairs={{1,0},{0,1},{3,2},{2,3},{5,4},{4,5},{7,6},{6,7},{9,8},{8,9},{11,10... | collective-permute-start | bytes 2359304 | tf_op jit(solution)/shard_map/ppermute | solution.py:124
  514.0 36.2 %collective-permute-start.26 = (bf16[256,1536]{1,0:T(8,128)(2,1)}, bf16[256,1536]{1,0:T(8,128)(2,1)}, u32[]{:S(2)}, u32[]{:S(2)}) collective-permute-start(bf16[256,1536]{1,0:T(8,128)(2,1)} %convolution_convert_fusion.5), channel_id=1, source_target_pairs={{2,0},{3,1},{0,2},{1,3},{6,4},{7,5},{4,6},{5,7},{10,8},{11,9},{8,1... | collective-permute-start | bytes 2359304 | tf_op jit(solution)/shard_map/ppermute | solution.py:124
  514.6 35.6 %collective-permute-start.27 = (bf16[256,1536]{1,0:T(8,128)(2,1)}, bf16[256,1536]{1,0:T(8,128)(2,1)}, u32[]{:S(2)}, u32[]{:S(2)}) collective-permute-start(bf16[256,1536]{1,0:T(8,128)(2,1)} %convolution_convert_fusion.4), channel_id=1, source_target_pairs={{1,0},{0,1},{3,2},{2,3},{5,4},{4,5},{7,6},{6,7},{9,8},{8,9},{11,10... | collective-permute-start | bytes 2359304 | tf_op jit(solution)/shard_map/ppermute | solution.py:124
  515.1 56.6 %all-to-all-start.2 = ((bf16[4,48,4608]{2,1,0:T(8,128)(2,1)}), bf16[4,48,4608]{2,1,0:T(8,128)(2,1)}, u32[]{:S(2)}, u32[]{:S(2)}) async-start(bf16[4,48,4608]{2,1,0:T(8,128)(2,1)} %bitcast.198), calls=%async_computation.5 | async-start | bytes 3538944 | tf_op jit(solution)/shard_map/all_to_all | solution.py:541
  557.4 41.4 %collective-permute-start.31 = (bf16[48,1536]{1,0:T(8,128)(2,1)S(1)}, bf16[48,1536]{1,0:T(8,128)(2,1)S(1)}, u32[]{:S(2)}, u32[]{:S(2)}) collective-permute-start(bf16[48,1536]{1,0:T(8,128)(2,1)S(1)} %reshape.466), channel_id=1, source_target_pairs={{0,0},{4,1},{8,2},{12,3},{16,4},{20,5},{24,6},{28,7},{1,8},{5,9},{... | collective-permute-start | bytes 442376 | tf_op jit(solution)/shard_map/ppermute | solution.py:299
  (85 other events, 1088.4 us)
Sparse Core Ops, SparseCore 0:
  23.5 47.7 all-gather.8
  73.9 130.1 all-gather.4
  205.8 67.7 all-gather.6
  275.7 73.8 reduce-scatter.3
  368.9 142.5 reduce-scatter.5
  513.7 42.1 reduce-scatter.7

commit v2 on v1

--- a/solution.py
+++ b/solution.py
@@ -17,8 +17,7 @@
 MASKED = -1e30
 BF = jnp.bfloat16
 F32 = jnp.float32
-DP = ("far", "near")
-ALL = ("far", "near", "ctx")
+ALL = ("dp", "ctx")
 
 
 def rope_tables(positions):
@@ -114,30 +113,18 @@
             result = lax.dynamic_update_slice_in_dim(result, got, target, 0)
         return result
 
-    def shares(self, partial):
-        return [partial(step).astype(BF) for step in range(self.size - 1, 0, -1)] + [partial(0)]
-
-    def send(self, shares):
-        received = shares[-1:]
-        for step, share in zip(range(self.size - 1, 0, -1), shares):
+    def deliver(self, partial):
+        span = partial.shape[0] // self.size
+        received = [partial[:span]]
+        for step in range(self.size - 1, 0, -1):
             pairs = [(self.to(i, step), i) for i in range(self.size)]
+            share = partial[step * span : (step + 1) * span]
             received.append(lax.ppermute(share, self.axis, pairs))
         return received
 
-    def deliver(self, partial):
-        return self.send(self.shares(partial))
-
 
 def add_up(shares):
     return sum(share.astype(F32) for share in shares[1:]) + shares[0].astype(F32)
-
-
-class Halves:
-    def __init__(self, size):
-        self.size = size
-
-    def swap(self, own):
-        return lax.ppermute(own, "far", [(i, self.size - 1 - i) for i in range(self.size)])
 
 
 def pad_to(values, axis, size):
@@ -188,10 +175,10 @@
         self.out_rows, self.out_cols = out_weight.shape
         self.extra_rows = self.out_rows * self.out_cols // self.width
         pack = jnp.concatenate([pack, out_block.reshape(self.extra_rows, self.width)], axis=0)
-        whole = lax.all_gather(pack, DP, axis=0, tiled=False)
+        whole = lax.all_gather(pack, "dp", axis=0, tiled=False)
         joint = whole[:, : n * rows].reshape(dp_n * n * rows, self.width)
         self.out_slice = whole[:, n * rows :].reshape(dp_n * self.out_rows, self.out_cols)
-        self.qkv_slice = joint[:, : self.cols]
+        self.joint = joint
         bias = joint[:, self.cols + 2 : self.cols + 2 + self.bias_cols]
         bias = bias.reshape(dp_n * n, rows, self.bias_cols).transpose(0, 2, 1)
         bias = bias.reshape(dp_n * n, self.bias_cols * rows)[:, : self.bias_rows].reshape(-1)
@@ -225,10 +212,10 @@
         self.resid = jnp.concatenate(blocks).astype(F32)
         self.inv = inv_rms_of(self.resid)
         self.normed = (self.resid * self.inv * gain).astype(BF)
-        projected = dot(self.normed, self.qkv_slice) + self.bias_slice
+        projected = dot(self.normed, self.joint)[:, : self.cols] + self.bias_slice
         query_pre = projected[:, : self.q_cols].reshape(length, self.heads, HD)
         key_pre = projected[:, self.q_cols : self.q_cols + HD].reshape(length, 1, HD)
-        self.values = projected[:, self.q_cols + HD :].astype(BF)
+        self.values = projected[:, self.q_cols + HD : self.cols].astype(BF)
         self.query = rotate(query_pre, self.cos_table, self.sin_table).astype(BF)
         self.key = rotate(key_pre, self.cos_table, self.sin_table).astype(BF).reshape(length, HD)
         attended, self.log_total = attend(
@@ -236,16 +223,14 @@
         )
         self.attended, before = lax.optimization_barrier((attended.astype(BF), before))
         flat = self.attended.reshape(length, self.q_cols)
-        mixed = add_up(
-            peers.deliver(lambda step: dot(flat[step * span : (step + 1) * span], self.out_slice))
-        )
+        mixed = add_up(peers.deliver(dot(flat, self.out_slice).astype(BF)))
         return blocks[0].astype(F32) + mixed, before
 
-    def backward(self, mid_grad, gain, gain_two_term, filler, after):
+    def backward(self, mid_grad, gain, gain_two_term, filled, joint_grad, finish):
         peers, n, rows, dp_n = self.peers, self.n, self.rows, self.dp_n
         span = mid_grad.shape[0]
-        blocks, filled = lax.optimization_barrier((peers.spread(mid_grad.astype(BF)), filler()))
-        after = (after, filled)
+        blocks, filled = lax.optimization_barrier((peers.spread(mid_grad.astype(BF)), filled))
+        filled = peers.deliver(filled)
         low = jnp.concatenate(blocks)
         length = low.shape[0]
         attended_grad = dot_t(low, self.out_slice).astype(BF).reshape(length, self.heads, HD)
@@ -264,21 +249,12 @@
         key_grad = rotate(key_grad[:, None], self.cos_table, -self.sin_table).reshape(length, HD)
         proj_grad = jnp.concatenate([query_grad, key_grad, value_grad], axis=1)
         bias_term = jnp.sum(proj_grad, axis=0)
-        low_grad = proj_grad.astype(BF)
+        low_grad = pad_to(proj_grad.astype(BF), 1, self.width)
+        partial = dot_t(low_grad, self.joint).astype(BF)
+        partial, filled = lax.optimization_barrier((partial, filled))
+        normed_shares = peers.deliver(partial)
+        gain_term = jnp.sum(partial.astype(F32) * (self.resid * self.inv), axis=0)
         qkv_term = t_dot(self.normed, low_grad)
-        gain_terms = []
-
-        def share(step):
-            part = slice(step * span, (step + 1) * span)
-            normed_grad = dot_t(low_grad[part], self.qkv_slice)
-            gain_terms.append(jnp.sum(normed_grad * (self.resid[part] * self.inv[part]), axis=0))
-            return normed_grad
-
-        normed_shares = peers.deliver(share)
-        qkv_term, out_term = qkv_term.astype(BF), out_term.astype(BF)
-        normed_grad = add_up(normed_shares)
-        own = slice(0, span)
-        input_grad = mid_grad + norm_back(normed_grad, self.resid[own], self.inv[own], gain)
         bias = jnp.zeros((dp_n * n * self.bias_rows,), F32)
         first = 0
         for start, size in self.places():
@@ -287,14 +263,19 @@
         bias = pad_to(bias.reshape(dp_n * n, self.bias_rows), 1, self.bias_cols * rows)
         bias = bias.reshape(dp_n * n, self.bias_cols, rows).transpose(1, 0, 2)
         extra = jnp.concatenate(
-            [sum(gain_terms)[None], gain_two_term[None], bias.reshape(self.bias_cols, -1)], axis=0
+            [gain_term[None], gain_two_term[None], bias.reshape(self.bias_cols, -1)], axis=0
         ).T
-        extra = pad_to(extra, 1, self.width - self.cols)
-        joint = jnp.concatenate([qkv_term, extra.astype(BF)], axis=1)
-        joint = joint.reshape(dp_n, n * rows, self.width)
-        out_term = out_term.reshape(dp_n, self.extra_rows, self.width)
-        pack, filled = lax.optimization_barrier((jnp.concatenate([joint, out_term], axis=1), after))
-        mine = lax.psum_scatter(pack, DP, scatter_dimension=0, tiled=False)
+        extra = jnp.pad(extra, ((0, 0), (self.cols, self.width - self.cols - extra.shape[1])))
+        joint = (qkv_term + extra).astype(BF).reshape(dp_n, n * rows, self.width)
+        out_term = out_term.astype(BF).reshape(dp_n, self.extra_rows, self.width)
+        pack, joint_grad, normed_shares = lax.optimization_barrier(
+            (jnp.concatenate([joint, out_term], axis=1), joint_grad, normed_shares)
+        )
+        mine = lax.psum_scatter(pack, "dp", scatter_dimension=0, tiled=False)
+        own = slice(0, span)
+        normed_grad = add_up(normed_shares)
+        input_grad = mid_grad + norm_back(normed_grad, self.resid[own], self.inv[own], gain)
+        mine, output, finished = lax.optimization_barrier((mine, *finish(filled, joint_grad)))
         moves = [((b % dp_n) * n + b // dp_n, b) for b in range(dp_n * n)]
         out_grad = lax.ppermute(
             mine[n * rows :].reshape(self.out_rows, self.out_cols), ALL, moves
@@ -314,7 +295,7 @@
             bias_grad,
             out_grad,
             extra[:, 1],
-        ), filled
+        ), output, finished
 
 
 class RowSplit:
@@ -375,7 +356,7 @@
     def part(group):
         return slice(group * (H // KV), (group + 1) * (H // KV))
 
-    def backward(self, mid_grad, gain, gain_two_term, filler, after):
+    def backward(self, mid_grad, gain, gain_two_term, filled, joint_grad, finish):
         span = mid_grad.shape[0]
         low = mid_grad.astype(BF)
         attended_grad = dot_t(low, self.out).astype(BF).reshape(span, H, HD)
@@ -420,7 +401,7 @@
             lax.psum_scatter(term, ALL, scatter_dimension=0, tiled=True).astype(F32)
             for term in terms
         )
-        return grads, (after, filler())
+        return grads, *finish(self.peers.deliver(filled), joint_grad)
 
 
 def on_device(
@@ -436,16 +417,12 @@
     up_weight,
     down_weight,
     *,
-    far_n,
-    near_n,
+    dp_n,
     ctx_n,
 ):
-    span, features = inputs.shape[1:]
     rows, hidden_width = gate_weight.shape
     n = ctx_n
-    dp_n = far_n * near_n
     peers = Peers("ctx", n)
-    halves = Halves(far_n)
     if HeadSplit.fits(n):
         attention = HeadSplit(peers, dp_n, rows, qkv_bias.shape[0])
         blocks = peers.spread(inputs[0])
@@ -455,100 +432,68 @@
     gain_one, gain_two = attention.gather(attn_gain, mlp_gain, qkv_weight, qkv_bias, out_weight)
 
     unit = hidden_width // (dp_n * n)
-    width = near_n * unit
-    wide = round_up(width, LANES)
-    places = far_n * n
+    padded = round_up(unit, LANES // math.gcd(LANES, dp_n))
+    wide = dp_n * padded
 
     def column_slices(weight):
-        parts = weight.reshape(rows, far_n, near_n, n, unit).transpose(1, 3, 0, 2, 4)
-        return pad_to(parts.reshape(places, rows, width), 2, wide)
+        parts = pad_to(weight.reshape(rows, dp_n, n, unit), 3, padded)
+        return parts.transpose(2, 0, 1, 3).reshape(n, rows, wide)
 
     def weight_columns(values):
-        parts = values.reshape(far_n, n, rows, near_n, unit).transpose(2, 0, 3, 1, 4)
+        parts = values.reshape(n, rows, dp_n, padded)[..., :unit].transpose(1, 2, 0, 3)
         return parts.reshape(rows, hidden_width).astype(F32)
 
     joint = jnp.concatenate([column_slices(gate_weight), column_slices(up_weight)], axis=2)
-    if far_n == 1:
-        joint = peers.exchange(joint)
-    else:
-        joint = lax.all_to_all(joint, ("far", "ctx"), 0, 0, tiled=True)
-    gate_up = lax.all_gather(joint.reshape(places * rows, 2 * wide), "near", axis=0, tiled=True)
-    down = lax.all_gather(down_weight, "near", axis=0, tiled=True)
-
-    def to_gathered(values):
-        parts = values.reshape(span, far_n, near_n, -1).transpose(0, 2, 1, 3)
-        return parts.reshape(span, features)
-
-    def from_gathered(values):
-        parts = values.reshape(span, near_n, far_n, -1).transpose(0, 2, 1, 3)
-        return parts.reshape(span, features)
-
-    def spread_wide(own):
-        return sum([peers.spread(own if far == 0 else halves.swap(own)) for far in range(far_n)], [])
-
-    def block(values, far, step):
-        start = (far * n + step) * span
-        return values[start : start + span]
-
-    grad_out = spread_wide(cotangent[0])
+    joint = peers.exchange(joint).reshape(n * rows, 2 * wide)
+    gate_up = lax.all_gather(joint, "dp", axis=0, tiled=True)
+    down = lax.all_gather(pad_to(down_weight, 0, padded), "dp", axis=0, tiled=True)
+
+    blocks, own_cotangent = lax.optimization_barrier((blocks, cotangent[0]))
+    grad_out = peers.spread(own_cotangent)
     resid_mid, grad_out = attention.forward(blocks, segment_ids, gain_one, grad_out)
     inv_two = inv_rms_of(resid_mid)
     normed_own = (resid_mid * inv_two * gain_two).astype(BF)
-    normed = jnp.concatenate(spread_wide(to_gathered(normed_own)))
+    normed = jnp.concatenate(peers.spread(normed_own))
     grad_out = jnp.concatenate(grad_out)
     pre = dot(normed, gate_up)
-    gate_pre = pre[:, :width]
-    up_pre = pre[:, wide : wide + width]
+    gate_pre = pre[:, :wide]
+    up_pre = pre[:, wide:]
     sigmoid_gate = jax.nn.sigmoid(gate_pre)
     silu_gate = gate_pre * sigmoid_gate
     hidden = (silu_gate * up_pre).astype(BF)
     down_term = t_dot(hidden, grad_out).astype(BF)
     down_term, grad_out = lax.optimization_barrier((down_term, grad_out))
-    down_grad = lax.psum_scatter(down_term, "near", scatter_dimension=0, tiled=True)
+    down_grad = lax.psum_scatter(down_term, "dp", scatter_dimension=0, tiled=True)
     hidden_grad = dot_t(grad_out, down)
     gate_grad = (
         hidden_grad * up_pre * sigmoid_gate * (1.0 + gate_pre * (1.0 - sigmoid_gate))
     ).astype(BF)
     up_grad = (hidden_grad * silu_gate).astype(BF)
-    pre_grad = jnp.concatenate([pad_to(gate_grad, 1, wide), pad_to(up_grad, 1, wide)], axis=1)
-    shares = [
-        peers.deliver(lambda step: dot_t(block(pre_grad, far, step), gate_up))
-        for far in range(far_n - 1, -1, -1)
-    ]
+    pre_grad = jnp.concatenate([gate_grad, up_grad], axis=1)
+    shares = peers.deliver(dot_t(pre_grad, gate_up).astype(BF))
     joint_term = t_dot(normed, pre_grad).astype(BF)
     shares, joint_term = lax.optimization_barrier((shares, joint_term))
     joint_term, down_grad = lax.optimization_barrier((joint_term, down_grad))
-    joint_grad = lax.psum_scatter(joint_term, "near", scatter_dimension=0, tiled=True)
-    def combine(shares):
-        if far_n == 1:
-            return add_up(shares[0])
-        swapped = halves.swap(add_up(shares[0]).astype(BF))
-        return add_up(shares[1] + [swapped])
-
-    def output_shares():
-        return [
-            peers.shares(lambda step: dot(block(hidden, far, step), down))
-            for far in range(far_n - 1, -1, -1)
-        ]
-
-    normed_two_grad = from_gathered(combine(shares))
-    normed_two = resid_mid * inv_two
-    gain_two_term = jnp.sum(normed_two_grad * normed_two, axis=0)
+    joint_grad = lax.psum_scatter(joint_term, "dp", scatter_dimension=0, tiled=True)
+
+    normed_two_grad = add_up(shares)
+    gain_two_term = jnp.sum(normed_two_grad * (resid_mid * inv_two), axis=0)
     mid_grad = cotangent[0].astype(F32) + norm_back(normed_two_grad, resid_mid, inv_two, gain_two)
-    grads, (joint_grad, out_shares) = attention.backward(
-        mid_grad, gain_one, gain_two_term, output_shares, joint_grad
+
+    def finish(output_shares, joint_grad):
+        output = resid_mid + add_up(output_shares)
+        parts = peers.exchange(joint_grad.reshape(n, rows, 2 * wide))
+        grads = (weight_columns(parts[:, :, :wide]), weight_columns(parts[:, :, wide:]))
+        return output.astype(BF), grads
+
+    grads, output, (gate_weight_grad, up_weight_grad) = attention.backward(
+        mid_grad, gain_one, gain_two_term, dot(hidden, down).astype(BF), joint_grad, finish
     )
-    joint_grad = lax.all_to_all(
-        joint_grad.reshape(places, rows, 2 * wide), ("far", "ctx"), 0, 0, tiled=True
-    )
-    gate_weight_grad = weight_columns(joint_grad[:, :, :width])
-    up_weight_grad = weight_columns(joint_grad[:, :, wide : wide + width])
     input_grad, attn_gain_grad, qkv_weight_grad, qkv_bias_grad, out_weight_grad, mlp_gain_grad = (
         grads
     )
-    output = resid_mid + combine([peers.send(shares) for shares in out_shares])
     return (
-        output.astype(BF)[None],
+        output[None],
         input_grad[None],
         attn_gain_grad,
         qkv_weight_grad,
@@ -557,22 +502,19 @@
         mlp_gain_grad,
         gate_weight_grad,
         up_weight_grad,
-        down_grad.astype(F32),
+        down_grad[:unit].astype(F32),
     )
 
 
 def solution(mesh):
-    dp_n, ctx_n = mesh.shape["dp"], mesh.shape["ctx"]
-    far_n = 1
-    split = jax.sharding.Mesh(mesh.devices.reshape(far_n, dp_n // far_n, ctx_n), ALL)
-    body = functools.partial(on_device, far_n=far_n, near_n=dp_n // far_n, ctx_n=ctx_n)
+    body = functools.partial(on_device, dp_n=mesh.shape["dp"], ctx_n=mesh.shape["ctx"])
     return jax.shard_map(
         body,
-        mesh=split,
+        mesh=mesh,
         in_specs=(
-            P(DP, "ctx", None),
-            P(DP, "ctx", None),
-            P(DP, "ctx"),
+            P("dp", "ctx", None),
+            P("dp", "ctx", None),
+            P("dp", "ctx"),
             P(ALL),
             P(ALL, None),
             P(ALL),
@@ -583,8 +525,8 @@
             P(ALL, None),
         ),
         out_specs=(
-            P(DP, "ctx", None),
-            P(DP, "ctx", None),
+            P("dp", "ctx", None),
+            P("dp", "ctx", None),
             P(ALL),
             P(ALL, None),
             P(ALL),

time: 618 us -> 590 us (0.955)
  the two profiles are of different devices: /device:TPU:0 before, /device:TPU:25 now
where the time goes in v2:
time: 590 us; the launch traced here: 582 us
  waiting for transfers between devices  252 us (43%)
  matrix products  142 us (24%)
  local copies, waits for them, and re-layouts  76 us (13%)
  other arithmetic  54 us (9%)
  starting transfers between devices  42.1 us (7%)
  between operations  15.9 us (3%)
    ppermute x12, waiting for transfers between devices, deliver(): received.append(lax.ppermute(share, self.axis, pairs))  79.7 us
    ppermute x15, waiting for transfers between devices, spread(): blocks.append(lax.ppermute(own, self.axis, pairs))  76.4 us
    ppermute x6, waiting for transfers between devices, exchange(): lax.ppermute(lax.dynamic_index_in_dim(parts, source, 0), self.axis, pairs)  54.3 us
    dot_general x4, matrix products, dot_t(): lax.dot_general(a, b, (((1,), (1,)), ((), ())), preferred_element_type=F32)  45.2 us
    dot_general x4, matrix products, dot(): return jnp.dot(a, b, preferred_element_type=F32)  37.9 us
    dot_general x4, matrix products, t_dot(): lax.dot_general(a, b, (((0,), (0,)), ((), ())), preferred_element_type=F32)  37.5 us
    unnamed x153, local copies, waits for them, and re-layouts  20 us
    reduce_scatter x1, waiting for transfers between devices, on_device(): lax.psum_scatter(joint_term, 'dp', scatter_dimension=0, tiled=True)  12 us
  transfers between devices with their start and end apart: 43, of which 21 were waited for; matrix products, arithmetic and copies ran while one was open for 42% of the time, Pallas kernels for 0%

profile of v2, /device:TPU:25, one launch (start us, length us, event | category | flops | bytes accessed | tf_op | source)
XLA Modules:
  0.0 581.6 jit_solution(18171800249995184925)
XLA Ops:
  20.4 6.1 %collective-permute-done.3 = bf16[48,1536]{1,0:T(8,128)(2,1)S(1)} collective-permute-done((bf16[48,1536]{1,0:T(8,128)(2,1)}, bf16[48,1536]{1,0:T(8,128)(2,1)S(1)}, u32[]{:S(2)}, u32[]{:S(2)}) %collective-permute-start.3) | collective-permute-done | bytes 147488 | tf_op jit(solution)/shard_map/ppermute | solution.py:174
  37.5 11.4 %collective-permute-done.16 = bf16[1,48,4608]{2,1,0:T(8,128)(2,1)} collective-permute-done((bf16[1,48,4608]{2,1,0:T(8,128)(2,1)}, bf16[1,48,4608]{2,1,0:T(8,128)(2,1)}, u32[]{:S(2)}, u32[]{:S(2)}) %collective-permute-start.16) | collective-permute-done | bytes 442400 | tf_op jit(solution)/shard_map/ppermute | solution.py:111
  50.6 20.1 %collective-permute-done.17 = bf16[1,48,4608]{2,1,0:T(8,128)(2,1)S(1)} collective-permute-done((bf16[1,48,4608]{2,1,0:T(8,128)(2,1)S(1)}, bf16[1,48,4608]{2,1,0:T(8,128)(2,1)S(1)}, u32[]{:S(2)}, u32[]{:S(2)}) %collective-permute-start.17) | collective-permute-done | bytes 442400 | tf_op jit(solution)/shard_map/ppermute | solution.py:111
  76.7 13.2 %collective-permute-done.4 = s32[1,256]{1,0:T(1,128)S(1)} collective-permute-done((s32[1,256]{1,0:T(1,128)S(1)}, s32[1,256]{1,0:T(1,128)S(1)}, u32[]{:S(2)}, u32[]{:S(2)}) %collective-permute-start.4) | collective-permute-done | bytes 1056 | tf_op jit(solution)/shard_map/ppermute | solution.py:103
  93.2 14.3 %collective-permute-done.2 = bf16[256,1536]{1,0:T(8,128)(2,1)S(1)} collective-permute-done((bf16[256,1536]{1,0:T(8,128)(2,1)S(1)}, bf16[256,1536]{1,0:T(8,128)(2,1)S(1)}, u32[]{:S(2)}, u32[]{:S(2)}) %collective-permute-start.2) | collective-permute-done | bytes 786464 | tf_op jit(solution)/shard_map/ppermute | solution.py:103
  151.0 13.0 %collective-permute-done.10 = bf16[256,1536]{1,0:T(8,128)(2,1)S(1)} collective-permute-done((bf16[256,1536]{1,0:T(8,128)(2,1)S(1)}, bf16[256,1536]{1,0:T(8,128)(2,1)S(1)}, u32[]{:S(2)}, u32[]{:S(2)}) %collective-permute-start.10) | collective-permute-done | bytes 786464 | tf_op jit(solution)/shard_map/ppermute | solution.py:122
  164.1 21.3 %collective-permute-done.11 = bf16[256,1536]{1,0:T(8,128)(2,1)S(1)} collective-permute-done((bf16[256,1536]{1,0:T(8,128)(2,1)S(1)}, bf16[256,1536]{1,0:T(8,128)(2,1)S(1)}, u32[]{:S(2)}, u32[]{:S(2)}) %collective-permute-start.11) | collective-permute-done | bytes 786464 | tf_op jit(solution)/shard_map/ppermute | solution.py:122
  192.7 12.3 %collective-permute-done.13 = bf16[256,1536]{1,0:T(8,128)(2,1)S(1)} collective-permute-done((bf16[256,1536]{1,0:T(8,128)(2,1)S(1)}, bf16[256,1536]{1,0:T(8,128)(2,1)S(1)}, u32[]{:S(2)}, u32[]{:S(2)}) %collective-permute-start.13) | collective-permute-done | bytes 786464 | tf_op jit(solution)/shard_map/ppermute | solution.py:103
  206.7 14.9 %collective-permute-done.15 = bf16[256,1536]{1,0:T(8,128)(2,1)} collective-permute-done((bf16[256,1536]{1,0:T(8,128)(2,1)S(1)}, bf16[256,1536]{1,0:T(8,128)(2,1)}, u32[]{:S(2)}, u32[]{:S(2)}) %collective-permute-start.15) | collective-permute-done | bytes 786464 | tf_op jit(solution)/shard_map/ppermute | solution.py:103
  221.6 18.3 %fusion.22 = f32[1024,4608]{1,0:T(8,128)S(1)} fusion(bf16[1536,4608]{1,0:T(8,128)(2,1)} %all-gather.5.cloned.1.call-done, bf16[256,1536]{1,0:T(8,128)(2,1)} %collective-permute-done.15, bf16[256,1536]{1,0:T(8,128)(2,1)} %copy-done.67, bf16[256,1536]{1,0:T(8,128)(2,1)} %copy-done.66, bf16[256,1536]{1,0:T(8,128)(2,1)S(1)} %multiply_convert_fusion.4), kind=kOutput, calls=%fused_computation.78 | convolution fusion | flops 14508097536 | bytes 36175872 | tf_op jit(solution)/shard_map/dot_general | solution.py:48
  249.6 9.4 %convolution_convert_fusion.1 = bf16[2304,1536]{1,0:T(8,128)(2,1)} fusion(bf16[1024,2304]{1,0:T(8,128)(2,1)S(1)} %multiply_convert_fusion.2, bf16[1024,1536]{1,0:T(8,128)(2,1)S(1)} %copy-done.58), kind=kOutput, calls=%fused_computation.8 | convolution fusion | flops 7251296256 | bytes 14942208 | tf_op jit(solution)/shard_map/dot_general | solution.py:56
  259.1 11.5 %all-gather.7.cloned.1.call-done = bf16[2304,1536]{1,0:T(8,128)(2,1)} async-done(((bf16[288,1536]{1,0:T(8,128)(2,1)}), bf16[2304,1536]{1,0:T(8,128)(2,1)}) %all-gather.7.cloned.1.call-update) | async-done | bytes 7077904 | tf_op jit(solution)/shard_map/all_gather | solution.py:449
  270.6 20.3 %multiply_convert_fusion.1 = (bf16[1024,2304]{1,0:T(8,128)(2,1)}, bf16[1024,2304]{1,0:T(8,128)(2,1)}) fusion(f32[1024,4608]{1,0:T(8,128)} %copy-done, bf16[1024,1536]{1,0:T(8,128)(2,1)} %copy-done.57, bf16[2304,1536]{1,0:T(8,128)(2,1)} %all-gather.7.cloned.1.call-done), kind=kOutput, calls=%fused_computation.12 | convolution fusion | flops 7278428160 | bytes 38535168 | tf_op jit(solution)/shard_map/dot_general | solution.py:52
  290.9 20.5 %fusion.7 = bf16[1024,1536]{1,0:T(8,128)(2,1)S(1)} fusion(bf16[1536,4608]{1,0:T(8,128)(2,1)} %all-gather.5.cloned.1.call-done, bf16[1024,2304]{1,0:T(8,128)(2,1)} %get-tuple-element.99, bf16[1024,2304]{1,0:T(8,128)(2,1)} %get-tuple-element.98), kind=kOutput, calls=%fused_computation.24 | convolution fusion | flops 14515961856 | bytes 26738688 | tf_op jit(solution)/shard_map/dot_general | solution.py:52
  315.5 22.6 %convolution_convert_fusion = bf16[1536,4608]{1,0:T(8,128)(2,1)} fusion(bf16[1024,2304]{1,0:T(8,128)(2,1)} %get-tuple-element.99, bf16[1024,2304]{1,0:T(8,128)(2,1)} %get-tuple-element.98, bf16[256,1536]{1,0:T(8,128)(2,1)} %collective-permute-done.15, bf16[256,1536]{1,0:T(8,128)(2,1)} %copy-done.67, bf16[256,1536]{1,0:T(8,128)(2,1)} %copy-done.66, ...), kind=kOutput, calls=%fused_computation | convolution fusion | flops 14534049792 | bytes 26738688 | tf_op jit(solution)/shard_map/dot_general | solution.py:56
  338.0 12.3 %collective-permute-done.20 = bf16[256,1536]{1,0:T(8,128)(2,1)} collective-permute-done((bf16[256,1536]{1,0:T(8,128)(2,1)}, bf16[256,1536]{1,0:T(8,128)(2,1)}, u32[]{:S(2)}, u32[]{:S(2)}) %collective-permute-start.20) | collective-permute-done | bytes 786464 | tf_op jit(solution)/shard_map/ppermute | solution.py:122
  359.2 12.1 %convolution_convert_fusion.3 = bf16[1024,1536]{1,0:T(8,128)(2,1)S(1)} fusion(bf16[1024,2304]{1,0:T(8,128)(2,1)} %copy-done.29, bf16[2304,1536]{1,0:T(8,128)(2,1)} %all-gather.7.cloned.1.call-done), kind=kOutput, calls=%fused_computation.26 | convolution fusion | flops 7249330176 | bytes 14942208 | tf_op jit(solution)/shard_map/dot_general | solution.py:48
  376.4 16.8 %collective-permute-done.24 = bf16[256,1536]{1,0:T(8,128)(2,1)S(1)} collective-permute-done((bf16[256,1536]{1,0:T(8,128)(2,1)S(1)}, bf16[256,1536]{1,0:T(8,128)(2,1)S(1)}, u32[]{:S(2)}, u32[]{:S(2)}) %collective-permute-start.24) | collective-permute-done | bytes 786464 | tf_op jit(solution)/shard_map/ppermute | solution.py:103
  450.9 12.0 %collective-permute-done.28 = bf16[256,1536]{1,0:T(8,128)(2,1)} collective-permute-done((bf16[256,1536]{1,0:T(8,128)(2,1)}, bf16[256,1536]{1,0:T(8,128)(2,1)}, u32[]{:S(2)}, u32[]{:S(2)}) %collective-permute-start.28) | collective-permute-done | bytes 786464 | tf_op jit(solution)/shard_map/ppermute | solution.py:122
  463.0 17.7 %collective-permute-done.29 = bf16[256,1536]{1,0:T(8,128)(2,1)} collective-permute-done((bf16[256,1536]{1,0:T(8,128)(2,1)}, bf16[256,1536]{1,0:T(8,128)(2,1)}, u32[]{:S(2)}, u32[]{:S(2)}) %collective-permute-start.29) | collective-permute-done | bytes 786464 | tf_op jit(solution)/shard_map/ppermute | solution.py:122
  480.6 12.0 %reduce-scatter.6.cloned.1.call-done = bf16[192,4608]{1,0:T(8,128)(2,1)} async-done(((bf16[1536,4608]{1,0:T(8,128)(2,1)}), bf16[192,4608]{1,0:T(8,128)(2,1)}) %reduce-scatter.6.cloned.1.call-update) | async-done | bytes 1769488 | tf_op jit(solution)/shard_map/reduce_scatter | solution.py:477
  503.0 8.1 %collective-permute-done.31 = bf16[1,48,4608]{2,1,0:T(8,128)(2,1)S(1)} collective-permute-done((bf16[1,48,4608]{2,1,0:T(8,128)(2,1)S(1)}, bf16[1,48,4608]{2,1,0:T(8,128)(2,1)S(1)}, u32[]{:S(2)}, u32[]{:S(2)}) %collective-permute-start.31) | collective-permute-done | bytes 442400 | tf_op jit(solution)/shard_map/ppermute | solution.py:111
  516.4 14.7 %collective-permute-done.32 = bf16[1,48,4608]{2,1,0:T(8,128)(2,1)S(1)} collective-permute-done((bf16[1,48,4608]{2,1,0:T(8,128)(2,1)S(1)}, bf16[1,48,4608]{2,1,0:T(8,128)(2,1)S(1)}, u32[]{:S(2)}, u32[]{:S(2)}) %collective-permute-start.32) | collective-permute-done | bytes 442400 | tf_op jit(solution)/shard_map/ppermute | solution.py:111
  559.5 11.6 %collective-permute-done.34 = bf16[48,1536]{1,0:T(8,128)(2,1)S(1)} collective-permute-done((bf16[48,1536]{1,0:T(8,128)(2,1)S(1)}, bf16[48,1536]{1,0:T(8,128)(2,1)S(1)}, u32[]{:S(2)}, u32[]{:S(2)}) %collective-permute-start.34) | collective-permute-done | bytes 147488 | tf_op jit(solution)/shard_map/ppermute | solution.py:280
  (373 shorter events, 219.3 us)
Async XLA Ops:
  15.2 95.7 %all-gather.9.cloned.1.call-start = ((), (), s32[]{:S(2)}) async-start(), calls=%async_computation.10 | async-start | bytes 3981312 | tf_op jit(solution)/shard_map/all_gather | solution.py:178
  27.4 194.2 %all-gather.5.cloned.1.call-start = ((), (), s32[]{:S(2)}) async-start(), calls=%async_computation.5 | async-start | bytes 15925248 | tf_op jit(solution)/shard_map/all_gather | solution.py:448
  72.0 198.5 %all-gather.7.cloned.1.call-start = ((), (), s32[]{:S(2)}) async-start(), calls=%async_computation.6 | async-start | bytes 7962624 | tf_op jit(solution)/shard_map/all_gather | solution.py:449
  72.1 21.1 %collective-permute-start = (bf16[256,1536]{1,0:T(8,128)(2,1)S(1)}, bf16[256,1536]{1,0:T(8,128)(2,1)S(1)}, u32[]{:S(2)}, u32[]{:S(2)}) collective-permute-start(bf16[256,1536]{1,0:T(8,128)(2,1)S(1)} %bitcast.146), channel_id=1, source_target_pairs={{0,1},{1,0},{2,3},{3,2},{4,5},{5,4},{6,7},{7,6},{8,9},{9,8},{10,11... | collective-permute-start | bytes 2359304 | tf_op jit(solution)/shard_map/ppermute | solution.py:103
  72.2 21.0 %collective-permute-start.1 = (bf16[256,1536]{1,0:T(8,128)(2,1)S(1)}, bf16[256,1536]{1,0:T(8,128)(2,1)S(1)}, u32[]{:S(2)}, u32[]{:S(2)}) collective-permute-start(bf16[256,1536]{1,0:T(8,128)(2,1)S(1)} %bitcast.147), channel_id=1, source_target_pairs={{0,2},{1,3},{2,0},{3,1},{4,6},{5,7},{6,4},{7,5},{8,10},{9,11},{10,... | collective-permute-start | bytes 2359304 | tf_op jit(solution)/shard_map/ppermute | solution.py:103
  76.6 273.8 %reduce-scatter.4.cloned.1.call-start = ((), (), s32[]{:S(2)}) async-start(), calls=%async_computation.7 | async-start | bytes 7962624 | tf_op jit(solution)/shard_map/reduce_scatter | solution.py:466
  107.4 34.8 %collective-permute-start.7 = (bf16[256,1536]{1,0:T(8,128)(2,1)}, bf16[256,1536]{1,0:T(8,128)(2,1)}, u32[]{:S(2)}, u32[]{:S(2)}) collective-permute-start(bf16[256,1536]{1,0:T(8,128)(2,1)} %bitcast.167), channel_id=1, source_target_pairs={{0,1},{1,0},{2,3},{3,2},{4,5},{5,4},{6,7},{7,6},{8,9},{9,8},{10,11... | collective-permute-start | bytes 2359304 | tf_op jit(solution)/shard_map/ppermute | solution.py:103
  108.3 33.9 %collective-permute-start.8 = (bf16[256,1536]{1,0:T(8,128)(2,1)}, bf16[256,1536]{1,0:T(8,128)(2,1)}, u32[]{:S(2)}, u32[]{:S(2)}) collective-permute-start(bf16[256,1536]{1,0:T(8,128)(2,1)} %bitcast.168), channel_id=1, source_target_pairs={{0,2},{1,3},{2,0},{3,1},{4,6},{5,7},{6,4},{7,5},{8,10},{9,11},{10,... | collective-permute-start | bytes 2359304 | tf_op jit(solution)/shard_map/ppermute | solution.py:103
  108.6 33.6 %collective-permute-start.9 = (bf16[256,1536]{1,0:T(8,128)(2,1)}, bf16[256,1536]{1,0:T(8,128)(2,1)}, u32[]{:S(2)}, u32[]{:S(2)}) collective-permute-start(bf16[256,1536]{1,0:T(8,128)(2,1)} %bitcast.169), channel_id=1, source_target_pairs={{0,3},{1,2},{2,1},{3,0},{4,7},{5,6},{6,5},{7,4},{8,11},{9,10},{10,... | collective-permute-start | bytes 2359304 | tf_op jit(solution)/shard_map/ppermute | solution.py:103
  149.1 36.3 %collective-permute-start.11 = (bf16[256,1536]{1,0:T(8,128)(2,1)S(1)}, bf16[256,1536]{1,0:T(8,128)(2,1)S(1)}, u32[]{:S(2)}, u32[]{:S(2)}) collective-permute-start(bf16[256,1536]{1,0:T(8,128)(2,1)S(1)} %get-tuple-element.114), channel_id=1, source_target_pairs={{2,0},{3,1},{0,2},{1,3},{6,4},{7,5},{4,6},{5,7},{10,8},{11,9},{8,1... | collective-permute-start | bytes 2359304 | tf_op jit(solution)/shard_map/ppermute | solution.py:122
  150.3 35.0 %collective-permute-start.12 = (bf16[256,1536]{1,0:T(8,128)(2,1)S(1)}, bf16[256,1536]{1,0:T(8,128)(2,1)S(1)}, u32[]{:S(2)}, u32[]{:S(2)}) collective-permute-start(bf16[256,1536]{1,0:T(8,128)(2,1)S(1)} %get-tuple-element.113), channel_id=1, source_target_pairs={{1,0},{0,1},{3,2},{2,3},{5,4},{4,5},{7,6},{6,7},{9,8},{8,9},{11,10... | collective-permute-start | bytes 2359304 | tf_op jit(solution)/shard_map/ppermute | solution.py:122
  187.7 33.9 %collective-permute-start.15 = (bf16[256,1536]{1,0:T(8,128)(2,1)S(1)}, bf16[256,1536]{1,0:T(8,128)(2,1)}, u32[]{:S(2)}, u32[]{:S(2)}) collective-permute-start(bf16[256,1536]{1,0:T(8,128)(2,1)S(1)} %multiply_convert_fusion.4), channel_id=1, source_target_pairs={{0,3},{1,2},{2,1},{3,0},{4,7},{5,6},{6,5},{7,4},{8,11},{9,10},{10,... | collective-permute-start | bytes 2359304 | tf_op jit(solution)/shard_map/ppermute | solution.py:103
  259.1 233.6 %reduce-scatter.6.cloned.1.call-start = ((), (), s32[]{:S(2)}) async-start(), calls=%async_computation.8 | async-start | bytes 15925248 | tf_op jit(solution)/shard_map/reduce_scatter | solution.py:477
  312.8 25.2 %collective-permute-start.19 = (bf16[256,1536]{1,0:T(8,128)(2,1)}, bf16[256,1536]{1,0:T(8,128)(2,1)}, u32[]{:S(2)}, u32[]{:S(2)}) collective-permute-start(bf16[256,1536]{1,0:T(8,128)(2,1)} %get-tuple-element.110), channel_id=1, source_target_pairs={{3,0},{2,1},{1,2},{0,3},{7,4},{6,5},{5,6},{4,7},{11,8},{10,9},{9,1... | collective-permute-start | bytes 2359304 | tf_op jit(solution)/shard_map/ppermute | solution.py:122
  315.2 35.2 %collective-permute-start.20 = (bf16[256,1536]{1,0:T(8,128)(2,1)}, bf16[256,1536]{1,0:T(8,128)(2,1)}, u32[]{:S(2)}, u32[]{:S(2)}) collective-permute-start(bf16[256,1536]{1,0:T(8,128)(2,1)} %get-tuple-element.109), channel_id=1, source_target_pairs={{2,0},{3,1},{0,2},{1,3},{6,4},{7,5},{4,6},{5,7},{10,8},{11,9},{8,1... | collective-permute-start | bytes 2359304 | tf_op jit(solution)/shard_map/ppermute | solution.py:122
  315.4 34.9 %collective-permute-start.21 = (bf16[256,1536]{1,0:T(8,128)(2,1)}, bf16[256,1536]{1,0:T(8,128)(2,1)}, u32[]{:S(2)}, u32[]{:S(2)}) collective-permute-start(bf16[256,1536]{1,0:T(8,128)(2,1)} %get-tuple-element.108), channel_id=1, source_target_pairs={{1,0},{0,1},{3,2},{2,3},{5,4},{4,5},{7,6},{6,7},{9,8},{8,9},{11,10... | collective-permute-start | bytes 2359304 | tf_op jit(solution)/shard_map/ppermute | solution.py:122
  350.4 196.3 %reduce-scatter.8.cloned.1.call-start = ((), (), s32[]{:S(2)}) async-start(), calls=%async_computation.9 | async-start | bytes 3981312 | tf_op jit(solution)/shard_map/reduce_scatter | solution.py:274
  358.0 35.2 %collective-permute-start.24 = (bf16[256,1536]{1,0:T(8,128)(2,1)S(1)}, bf16[256,1536]{1,0:T(8,128)(2,1)S(1)}, u32[]{:S(2)}, u32[]{:S(2)}) collective-permute-start(bf16[256,1536]{1,0:T(8,128)(2,1)S(1)} %get-tuple-element.64), channel_id=1, source_target_pairs={{0,3},{1,2},{2,1},{3,0},{4,7},{5,6},{6,5},{7,4},{8,11},{9,10},{10,... | collective-permute-start | bytes 2359304 | tf_op jit(solution)/shard_map/ppermute | solution.py:103
  394.9 34.2 %collective-permute-start.25 = (bf16[256,1536]{1,0:T(8,128)(2,1)}, bf16[256,1536]{1,0:T(8,128)(2,1)}, u32[]{:S(2)}, u32[]{:S(2)}) collective-permute-start(bf16[256,1536]{1,0:T(8,128)(2,1)} %get-tuple-element.106), channel_id=1, source_target_pairs={{3,0},{2,1},{1,2},{0,3},{7,4},{6,5},{5,6},{4,7},{11,8},{10,9},{9,1... | collective-permute-start | bytes 2359304 | tf_op jit(solution)/shard_map/ppermute | solution.py:122
  396.0 36.4 %collective-permute-start.26 = (bf16[256,1536]{1,0:T(8,128)(2,1)}, bf16[256,1536]{1,0:T(8,128)(2,1)}, u32[]{:S(2)}, u32[]{:S(2)}) collective-permute-start(bf16[256,1536]{1,0:T(8,128)(2,1)} %get-tuple-element.105), channel_id=1, source_target_pairs={{2,0},{3,1},{0,2},{1,3},{6,4},{7,5},{4,6},{5,7},{10,8},{11,9},{8,1... | collective-permute-start | bytes 2359304 | tf_op jit(solution)/shard_map/ppermute | solution.py:122
  396.0 36.4 %collective-permute-start.27 = (bf16[256,1536]{1,0:T(8,128)(2,1)}, bf16[256,1536]{1,0:T(8,128)(2,1)}, u32[]{:S(2)}, u32[]{:S(2)}) collective-permute-start(bf16[256,1536]{1,0:T(8,128)(2,1)} %get-tuple-element.104), channel_id=1, source_target_pairs={{1,0},{0,1},{3,2},{2,3},{5,4},{4,5},{7,6},{6,7},{9,8},{8,9},{11,10... | collective-permute-start | bytes 2359304 | tf_op jit(solution)/shard_map/ppermute | solution.py:122
  444.3 36.4 %collective-permute-start.29 = (bf16[256,1536]{1,0:T(8,128)(2,1)}, bf16[256,1536]{1,0:T(8,128)(2,1)}, u32[]{:S(2)}, u32[]{:S(2)}) collective-permute-start(bf16[256,1536]{1,0:T(8,128)(2,1)} %get-tuple-element.101), channel_id=1, source_target_pairs={{2,0},{3,1},{0,2},{1,3},{6,4},{7,5},{4,6},{5,7},{10,8},{11,9},{8,1... | collective-permute-start | bytes 2359304 | tf_op jit(solution)/shard_map/ppermute | solution.py:122
  444.3 36.4 %collective-permute-start.30 = (bf16[256,1536]{1,0:T(8,128)(2,1)}, bf16[256,1536]{1,0:T(8,128)(2,1)}, u32[]{:S(2)}, u32[]{:S(2)}) collective-permute-start(bf16[256,1536]{1,0:T(8,128)(2,1)} %get-tuple-element.100), channel_id=1, source_target_pairs={{1,0},{0,1},{3,2},{2,3},{5,4},{4,5},{7,6},{6,7},{9,8},{8,9},{11,10... | collective-permute-start | bytes 2359304 | tf_op jit(solution)/shard_map/ppermute | solution.py:122
  549.4 22.4 %all-to-all-start.1 = ((bf16[4,48,768]{2,1,0:T(8,128)(2,1)}), bf16[4,48,768]{2,1,0:T(8,128)(2,1)S(1)}, u32[]{:S(2)}, u32[]{:S(2)}) async-start(bf16[4,48,768]{2,1,0:T(8,128)(2,1)} %bitcast.51), calls=%async_computation.4 | async-start | bytes 589824 | tf_op jit(solution)/shard_map/all_to_all | solution.py:283
  (90 other events, 1045.6 us)
Sparse Core Ops, SparseCore 0:
  27.5 40.2 all-gather.8
  72.1 126.9 all-gather.4
  200.8 69.7 all-gather.6
  272.7 75.2 reduce-scatter.3
  350.5 142.0 reduce-scatter.5
  494.9 43.0 reduce-scatter.7

commit v3 on v2

--- a/solution.py
+++ b/solution.py
@@ -104,14 +104,16 @@
         return blocks
 
     def exchange(self, parts):
-        result = parts
+        received = []
         for step in range(1, self.size):
-            source = self.source(step)
             pairs = [(self.to(i, step), i) for i in range(self.size)]
-            got = lax.ppermute(lax.dynamic_index_in_dim(parts, source, 0), self.axis, pairs)
-            target = source if self.paired else (self.me + step) % self.size
-            result = lax.dynamic_update_slice_in_dim(result, got, target, 0)
-        return result
+            block = lax.dynamic_index_in_dim(parts, self.source(step), 0)
+            received.append(lax.ppermute(block, self.axis, pairs))
+        parts, received = lax.optimization_barrier((parts, received))
+        for step, block in enumerate(received, 1):
+            target = self.source(step) if self.paired else (self.me + step) % self.size
+            parts = lax.dynamic_update_slice_in_dim(parts, block, target, 0)
+        return parts
 
     def deliver(self, partial):
         span = partial.shape[0] // self.size
@@ -275,7 +277,9 @@
         own = slice(0, span)
         normed_grad = add_up(normed_shares)
         input_grad = mid_grad + norm_back(normed_grad, self.resid[own], self.inv[own], gain)
-        mine, output, finished = lax.optimization_barrier((mine, *finish(filled, joint_grad)))
+        mine, input_grad, output, finished = lax.optimization_barrier(
+            (mine, input_grad, *finish(filled, joint_grad))
+        )
         moves = [((b % dp_n) * n + b // dp_n, b) for b in range(dp_n * n)]
         out_grad = lax.ppermute(
             mine[n * rows :].reshape(self.out_rows, self.out_cols), ALL, moves

time: 590 us -> 577 us (0.978)
  waiting for transfers between devices: 252 us -> 241 us
    ppermute x6, waiting for transfers between devices: 54.3 us -> 30.8 us  [exchange(): received.append(lax.ppermute(block, self.axis, pairs))]
    all_gather x1, waiting for transfers between devices: 11.5 us -> 21.8 us  [on_device(): lax.all_gather(pad_to(down_weight, 0, padded), 'dp', axis=0, tiled=True)]
  transfers between devices with their start and end apart: 43 -> 43, of which waited for: 21 -> 26; matrix products, arithmetic and copies ran while one was open for 42% -> 42% of each run, Pallas kernels for 0% -> 0%
where the time goes in v3:
time: 577 us; the launch traced here: 568 us
  waiting for transfers between devices  241 us (42%)
  matrix products  142 us (25%)
  local copies, waits for them, and re-layouts  71.4 us (12%)
  other arithmetic  51.2 us (9%)
  starting transfers between devices  47.1 us (8%)
  between operations  15.9 us (3%)
    ppermute x12, waiting for transfers between devices, deliver(): received.append(lax.ppermute(share, self.axis, pairs))  80 us
    ppermute x15, waiting for transfers between devices, spread(): blocks.append(lax.ppermute(own, self.axis, pairs))  75.6 us
    dot_general x4, matrix products, dot_t(): lax.dot_general(a, b, (((1,), (1,)), ((), ())), preferred_element_type=F32)  45.1 us
    dot_general x4, matrix products, dot(): return jnp.dot(a, b, preferred_element_type=F32)  37.9 us
    dot_general x4, matrix products, t_dot(): lax.dot_general(a, b, (((0,), (0,)), ((), ())), preferred_element_type=F32)  37.5 us
    ppermute x6, waiting for transfers between devices, exchange(): received.append(lax.ppermute(block, self.axis, pairs))  30.8 us
    all_gather x1, waiting for transfers between devices, on_device(): lax.all_gather(pad_to(down_weight, 0, padded), 'dp', axis=0, tiled=True)  21.8 us
    unnamed x153, local copies, waits for them, and re-layouts  19.1 us
  transfers between devices with their start and end apart: 43, of which 26 were waited for; matrix products, arithmetic and copies ran while one was open for 42% of the time, Pallas kernels for 0%

profile of v3, /device:TPU:25, one launch (start us, length us, event | category | flops | bytes accessed | tf_op | source)
XLA Modules:
  0.0 568.3 jit_solution(5792812786757524366)
XLA Ops:
  20.4 6.1 %collective-permute-done.3 = bf16[48,1536]{1,0:T(8,128)(2,1)S(1)} collective-permute-done((bf16[48,1536]{1,0:T(8,128)(2,1)}, bf16[48,1536]{1,0:T(8,128)(2,1)S(1)}, u32[]{:S(2)}, u32[]{:S(2)}) %collective-permute-start.3) | collective-permute-done | bytes 147488 | tf_op jit(solution)/shard_map/ppermute | solution.py:176
  39.6 8.6 %collective-permute-done.16 = bf16[1,48,4608]{2,1,0:T(8,128)(2,1)S(1)} collective-permute-done((bf16[1,48,4608]{2,1,0:T(8,128)(2,1)S(1)}, bf16[1,48,4608]{2,1,0:T(8,128)(2,1)S(1)}, u32[]{:S(2)}, u32[]{:S(2)}) %collective-permute-start.16) | collective-permute-done | bytes 442400 | tf_op jit(solution)/shard_map/ppermute | solution.py:111
  48.1 9.0 %collective-permute-done.18 = bf16[1,48,4608]{2,1,0:T(8,128)(2,1)S(1)} collective-permute-done((bf16[1,48,4608]{2,1,0:T(8,128)(2,1)S(1)}, bf16[1,48,4608]{2,1,0:T(8,128)(2,1)S(1)}, u32[]{:S(2)}, u32[]{:S(2)}) %collective-permute-start.18) | collective-permute-done | bytes 442400 | tf_op jit(solution)/shard_map/ppermute | solution.py:111
  64.2 11.9 %collective-permute-done.4 = s32[1,256]{1,0:T(1,128)S(1)} collective-permute-done((s32[1,256]{1,0:T(1,128)S(1)}, s32[1,256]{1,0:T(1,128)S(1)}, u32[]{:S(2)}, u32[]{:S(2)}) %collective-permute-start.4) | collective-permute-done | bytes 1056 | tf_op jit(solution)/shard_map/ppermute | solution.py:103
  80.3 13.3 %collective-permute-done.2 = bf16[256,1536]{1,0:T(8,128)(2,1)S(1)} collective-permute-done((bf16[256,1536]{1,0:T(8,128)(2,1)S(1)}, bf16[256,1536]{1,0:T(8,128)(2,1)S(1)}, u32[]{:S(2)}, u32[]{:S(2)}) %collective-permute-start.2) | collective-permute-done | bytes 786464 | tf_op jit(solution)/shard_map/ppermute | solution.py:103
  137.9 10.9 %collective-permute-done.10 = bf16[256,1536]{1,0:T(8,128)(2,1)S(1)} collective-permute-done((bf16[256,1536]{1,0:T(8,128)(2,1)S(1)}, bf16[256,1536]{1,0:T(8,128)(2,1)S(1)}, u32[]{:S(2)}, u32[]{:S(2)}) %collective-permute-start.10) | collective-permute-done | bytes 786464 | tf_op jit(solution)/shard_map/ppermute | solution.py:124
  148.8 23.7 %collective-permute-done.11 = bf16[256,1536]{1,0:T(8,128)(2,1)S(1)} collective-permute-done((bf16[256,1536]{1,0:T(8,128)(2,1)S(1)}, bf16[256,1536]{1,0:T(8,128)(2,1)S(1)}, u32[]{:S(2)}, u32[]{:S(2)}) %collective-permute-start.11) | collective-permute-done | bytes 786464 | tf_op jit(solution)/shard_map/ppermute | solution.py:124
  179.8 12.1 %collective-permute-done.13 = bf16[256,1536]{1,0:T(8,128)(2,1)S(1)} collective-permute-done((bf16[256,1536]{1,0:T(8,128)(2,1)S(1)}, bf16[256,1536]{1,0:T(8,128)(2,1)S(1)}, u32[]{:S(2)}, u32[]{:S(2)}) %collective-permute-start.13) | collective-permute-done | bytes 786464 | tf_op jit(solution)/shard_map/ppermute | solution.py:103
  194.4 14.6 %collective-permute-done.15 = bf16[256,1536]{1,0:T(8,128)(2,1)} collective-permute-done((bf16[256,1536]{1,0:T(8,128)(2,1)S(1)}, bf16[256,1536]{1,0:T(8,128)(2,1)}, u32[]{:S(2)}, u32[]{:S(2)}) %collective-permute-start.15) | collective-permute-done | bytes 786464 | tf_op jit(solution)/shard_map/ppermute | solution.py:103
  209.0 18.4 %fusion.22 = f32[1024,4608]{1,0:T(8,128)S(1)} fusion(bf16[1536,4608]{1,0:T(8,128)(2,1)} %all-gather.5.cloned.1.call-done, bf16[256,1536]{1,0:T(8,128)(2,1)} %collective-permute-done.15, bf16[256,1536]{1,0:T(8,128)(2,1)} %copy-done.67, bf16[256,1536]{1,0:T(8,128)(2,1)} %copy-done.66, bf16[256,1536]{1,0:T(8,128)(2,1)S(1)} %multiply_convert_fusion.4), kind=kOutput, calls=%fused_computation.78 | convolution fusion | flops 14508097536 | bytes 36175872 | tf_op jit(solution)/shard_map/dot_general | solution.py:48
  237.1 9.4 %convolution_convert_fusion.1 = bf16[2304,1536]{1,0:T(8,128)(2,1)} fusion(bf16[1024,2304]{1,0:T(8,128)(2,1)S(1)} %multiply_convert_fusion.2, bf16[1024,1536]{1,0:T(8,128)(2,1)S(1)} %copy-done.58), kind=kOutput, calls=%fused_computation.8 | convolution fusion | flops 7251296256 | bytes 14942208 | tf_op jit(solution)/shard_map/dot_general | solution.py:56
  246.6 21.8 %all-gather.7.cloned.1.call-done = bf16[2304,1536]{1,0:T(8,128)(2,1)} async-done(((bf16[288,1536]{1,0:T(8,128)(2,1)}), bf16[2304,1536]{1,0:T(8,128)(2,1)}) %all-gather.7.cloned.1.call-update) | async-done | bytes 7077904 | tf_op jit(solution)/shard_map/all_gather | solution.py:453
  268.4 20.2 %multiply_convert_fusion.1 = (bf16[1024,2304]{1,0:T(8,128)(2,1)}, bf16[1024,2304]{1,0:T(8,128)(2,1)}) fusion(f32[1024,4608]{1,0:T(8,128)} %copy-done, bf16[1024,1536]{1,0:T(8,128)(2,1)} %copy-done.57, bf16[2304,1536]{1,0:T(8,128)(2,1)} %all-gather.7.cloned.1.call-done), kind=kOutput, calls=%fused_computation.12 | convolution fusion | flops 7278428160 | bytes 38535168 | tf_op jit(solution)/shard_map/dot_general | solution.py:52
  288.6 20.5 %fusion.7 = bf16[1024,1536]{1,0:T(8,128)(2,1)S(1)} fusion(bf16[1536,4608]{1,0:T(8,128)(2,1)} %all-gather.5.cloned.1.call-done, bf16[1024,2304]{1,0:T(8,128)(2,1)} %get-tuple-element.117, bf16[1024,2304]{1,0:T(8,128)(2,1)} %get-tuple-element.116), kind=kOutput, calls=%fused_computation.24 | convolution fusion | flops 14515961856 | bytes 26738688 | tf_op jit(solution)/shard_map/dot_general | solution.py:52
  313.2 22.6 %convolution_convert_fusion = bf16[1536,4608]{1,0:T(8,128)(2,1)} fusion(bf16[1024,2304]{1,0:T(8,128)(2,1)} %get-tuple-element.117, bf16[1024,2304]{1,0:T(8,128)(2,1)} %get-tuple-element.116, bf16[256,1536]{1,0:T(8,128)(2,1)} %collective-permute-done.15, bf16[256,1536]{1,0:T(8,128)(2,1)} %copy-done.67, bf16[256,1536]{1,0:T(8,128)(2,1)} %copy-done.66, ...), kind=kOutput, calls=%fused_computation | convolution fusion | flops 14534049792 | bytes 26738688 | tf_op jit(solution)/shard_map/dot_general | solution.py:56
  335.8 12.3 %collective-permute-done.20 = bf16[256,1536]{1,0:T(8,128)(2,1)} collective-permute-done((bf16[256,1536]{1,0:T(8,128)(2,1)}, bf16[256,1536]{1,0:T(8,128)(2,1)}, u32[]{:S(2)}, u32[]{:S(2)}) %collective-permute-start.20) | collective-permute-done | bytes 786464 | tf_op jit(solution)/shard_map/ppermute | solution.py:124
  357.0 12.2 %convolution_convert_fusion.3 = bf16[1024,1536]{1,0:T(8,128)(2,1)S(1)} fusion(bf16[1024,2304]{1,0:T(8,128)(2,1)} %copy-done.29, bf16[2304,1536]{1,0:T(8,128)(2,1)} %all-gather.7.cloned.1.call-done), kind=kOutput, calls=%fused_computation.26 | convolution fusion | flops 7249330176 | bytes 14942208 | tf_op jit(solution)/shard_map/dot_general | solution.py:48
  374.1 16.8 %collective-permute-done.24 = bf16[256,1536]{1,0:T(8,128)(2,1)S(1)} collective-permute-done((bf16[256,1536]{1,0:T(8,128)(2,1)S(1)}, bf16[256,1536]{1,0:T(8,128)(2,1)S(1)}, u32[]{:S(2)}, u32[]{:S(2)}) %collective-permute-start.24) | collective-permute-done | bytes 786464 | tf_op jit(solution)/shard_map/ppermute | solution.py:103
  398.2 6.0 %fusion.2 = bf16[3,1024,1024]{1,2,0:T(8,128)(2,1)S(1)} fusion(f32[1024,1024,3]{1,0,2:T(8,128)S(1)} %bitcast.144, f32[3,1024]{1,0:T(4,128)S(1)} %bitcast.192, f32[3,1024]{1,0:T(4,128)S(1)} %copy-done.64, pred[1024,1024]{0,1:T(8,128)(4,1)S(1)} %copy-done.31, bf16[1024,3,128]{0,2,1:T(8,128)(2,1)S(1)} %bitcast.178, f32[1024,640]{0,1:T(8,128)} %copy-done.22), kind=kOutput, calls=%fused_computation.4 | convolution fusion | flops 827326464 | bytes 20996096 | tf_op jit(solution)/shard_map/tjd,nd->jtn/dot_general | solution.py:78
  448.7 12.0 %collective-permute-done.28 = bf16[256,1536]{1,0:T(8,128)(2,1)} collective-permute-done((bf16[256,1536]{1,0:T(8,128)(2,1)}, bf16[256,1536]{1,0:T(8,128)(2,1)}, u32[]{:S(2)}, u32[]{:S(2)}) %collective-permute-start.28) | collective-permute-done | bytes 786464 | tf_op jit(solution)/shard_map/ppermute | solution.py:124
  460.8 17.7 %collective-permute-done.29 = bf16[256,1536]{1,0:T(8,128)(2,1)} collective-permute-done((bf16[256,1536]{1,0:T(8,128)(2,1)}, bf16[256,1536]{1,0:T(8,128)(2,1)}, u32[]{:S(2)}, u32[]{:S(2)}) %collective-permute-start.29) | collective-permute-done | bytes 786464 | tf_op jit(solution)/shard_map/ppermute | solution.py:124
  478.4 12.0 %reduce-scatter.6.cloned.1.call-done = bf16[192,4608]{1,0:T(8,128)(2,1)} async-done(((bf16[1536,4608]{1,0:T(8,128)(2,1)}), bf16[192,4608]{1,0:T(8,128)(2,1)}) %reduce-scatter.6.cloned.1.call-update) | async-done | bytes 1769488 | tf_op jit(solution)/shard_map/reduce_scatter | solution.py:481
  508.4 9.4 %collective-permute-done.33 = bf16[1,48,4608]{2,1,0:T(8,128)(2,1)S(1)} collective-permute-done((bf16[1,48,4608]{2,1,0:T(8,128)(2,1)S(1)}, bf16[1,48,4608]{2,1,0:T(8,128)(2,1)S(1)}, u32[]{:S(2)}, u32[]{:S(2)}) %collective-permute-start.33) | collective-permute-done | bytes 442400 | tf_op jit(solution)/shard_map/ppermute | solution.py:111
  547.5 10.3 %collective-permute-done.34 = bf16[48,1536]{1,0:T(8,128)(2,1)S(1)} collective-permute-done((bf16[48,1536]{1,0:T(8,128)(2,1)S(1)}, bf16[48,1536]{1,0:T(8,128)(2,1)S(1)}, u32[]{:S(2)}, u32[]{:S(2)}) %collective-permute-start.34) | collective-permute-done | bytes 147488 | tf_op jit(solution)/shard_map/ppermute | solution.py:284
  (372 shorter events, 220.7 us)
Async XLA Ops:
  15.2 82.7 %all-gather.9.cloned.1.call-start = ((), (), s32[]{:S(2)}) async-start(), calls=%async_computation.10 | async-start | bytes 3981312 | tf_op jit(solution)/shard_map/all_gather | solution.py:180
  27.4 181.6 %all-gather.5.cloned.1.call-start = ((), (), s32[]{:S(2)}) async-start(), calls=%async_computation.5 | async-start | bytes 15925248 | tf_op jit(solution)/shard_map/all_gather | solution.py:452
  58.5 209.9 %all-gather.7.cloned.1.call-start = ((), (), s32[]{:S(2)}) async-start(), calls=%async_computation.6 | async-start | bytes 7962624 | tf_op jit(solution)/shard_map/all_gather | solution.py:453
  58.5 21.7 %collective-permute-start = (bf16[256,1536]{1,0:T(8,128)(2,1)S(1)}, bf16[256,1536]{1,0:T(8,128)(2,1)S(1)}, u32[]{:S(2)}, u32[]{:S(2)}) collective-permute-start(bf16[256,1536]{1,0:T(8,128)(2,1)S(1)} %bitcast.145), channel_id=1, source_target_pairs={{0,1},{1,0},{2,3},{3,2},{4,5},{5,4},{6,7},{7,6},{8,9},{9,8},{10,11... | collective-permute-start | bytes 2359304 | tf_op jit(solution)/shard_map/ppermute | solution.py:103
  60.2 20.0 %collective-permute-start.1 = (bf16[256,1536]{1,0:T(8,128)(2,1)S(1)}, bf16[256,1536]{1,0:T(8,128)(2,1)S(1)}, u32[]{:S(2)}, u32[]{:S(2)}) collective-permute-start(bf16[256,1536]{1,0:T(8,128)(2,1)S(1)} %bitcast.146), channel_id=1, source_target_pairs={{0,2},{1,3},{2,0},{3,1},{4,6},{5,7},{6,4},{7,5},{8,10},{9,11},{10,... | collective-permute-start | bytes 2359304 | tf_op jit(solution)/shard_map/ppermute | solution.py:103
  64.1 284.1 %reduce-scatter.4.cloned.1.call-start = ((), (), s32[]{:S(2)}) async-start(), calls=%async_computation.7 | async-start | bytes 7962624 | tf_op jit(solution)/shard_map/reduce_scatter | solution.py:470
  93.6 35.4 %collective-permute-start.7 = (bf16[256,1536]{1,0:T(8,128)(2,1)}, bf16[256,1536]{1,0:T(8,128)(2,1)}, u32[]{:S(2)}, u32[]{:S(2)}) collective-permute-start(bf16[256,1536]{1,0:T(8,128)(2,1)} %bitcast.166), channel_id=1, source_target_pairs={{0,1},{1,0},{2,3},{3,2},{4,5},{5,4},{6,7},{7,6},{8,9},{9,8},{10,11... | collective-permute-start | bytes 2359304 | tf_op jit(solution)/shard_map/ppermute | solution.py:103
  95.2 33.8 %collective-permute-start.8 = (bf16[256,1536]{1,0:T(8,128)(2,1)}, bf16[256,1536]{1,0:T(8,128)(2,1)}, u32[]{:S(2)}, u32[]{:S(2)}) collective-permute-start(bf16[256,1536]{1,0:T(8,128)(2,1)} %bitcast.167), channel_id=1, source_target_pairs={{0,2},{1,3},{2,0},{3,1},{4,6},{5,7},{6,4},{7,5},{8,10},{9,11},{10,... | collective-permute-start | bytes 2359304 | tf_op jit(solution)/shard_map/ppermute | solution.py:103
  95.9 33.1 %collective-permute-start.9 = (bf16[256,1536]{1,0:T(8,128)(2,1)}, bf16[256,1536]{1,0:T(8,128)(2,1)}, u32[]{:S(2)}, u32[]{:S(2)}) collective-permute-start(bf16[256,1536]{1,0:T(8,128)(2,1)} %bitcast.168), channel_id=1, source_target_pairs={{0,3},{1,2},{2,1},{3,0},{4,7},{5,6},{6,5},{7,4},{8,11},{9,10},{10,... | collective-permute-start | bytes 2359304 | tf_op jit(solution)/shard_map/ppermute | solution.py:103
  136.4 36.1 %collective-permute-start.11 = (bf16[256,1536]{1,0:T(8,128)(2,1)S(1)}, bf16[256,1536]{1,0:T(8,128)(2,1)S(1)}, u32[]{:S(2)}, u32[]{:S(2)}) collective-permute-start(bf16[256,1536]{1,0:T(8,128)(2,1)S(1)} %get-tuple-element.132), channel_id=1, source_target_pairs={{2,0},{3,1},{0,2},{1,3},{6,4},{7,5},{4,6},{5,7},{10,8},{11,9},{8,1... | collective-permute-start | bytes 2359304 | tf_op jit(solution)/shard_map/ppermute | solution.py:124
  137.1 35.4 %collective-permute-start.12 = (bf16[256,1536]{1,0:T(8,128)(2,1)S(1)}, bf16[256,1536]{1,0:T(8,128)(2,1)S(1)}, u32[]{:S(2)}, u32[]{:S(2)}) collective-permute-start(bf16[256,1536]{1,0:T(8,128)(2,1)S(1)} %get-tuple-element.131), channel_id=1, source_target_pairs={{1,0},{0,1},{3,2},{2,3},{5,4},{4,5},{7,6},{6,7},{9,8},{8,9},{11,10... | collective-permute-start | bytes 2359304 | tf_op jit(solution)/shard_map/ppermute | solution.py:124
  175.0 34.0 %collective-permute-start.15 = (bf16[256,1536]{1,0:T(8,128)(2,1)S(1)}, bf16[256,1536]{1,0:T(8,128)(2,1)}, u32[]{:S(2)}, u32[]{:S(2)}) collective-permute-start(bf16[256,1536]{1,0:T(8,128)(2,1)S(1)} %multiply_convert_fusion.4), channel_id=1, source_target_pairs={{0,3},{1,2},{2,1},{3,0},{4,7},{5,6},{6,5},{7,4},{8,11},{9,10},{10,... | collective-permute-start | bytes 2359304 | tf_op jit(solution)/shard_map/ppermute | solution.py:103
  246.6 243.9 %reduce-scatter.6.cloned.1.call-start = ((), (), s32[]{:S(2)}) async-start(), calls=%async_computation.8 | async-start | bytes 15925248 | tf_op jit(solution)/shard_map/reduce_scatter | solution.py:481
  310.6 25.2 %collective-permute-start.19 = (bf16[256,1536]{1,0:T(8,128)(2,1)}, bf16[256,1536]{1,0:T(8,128)(2,1)}, u32[]{:S(2)}, u32[]{:S(2)}) collective-permute-start(bf16[256,1536]{1,0:T(8,128)(2,1)} %get-tuple-element.128), channel_id=1, source_target_pairs={{3,0},{2,1},{1,2},{0,3},{7,4},{6,5},{5,6},{4,7},{11,8},{10,9},{9,1... | collective-permute-start | bytes 2359304 | tf_op jit(solution)/shard_map/ppermute | solution.py:124
  312.9 35.2 %collective-permute-start.20 = (bf16[256,1536]{1,0:T(8,128)(2,1)}, bf16[256,1536]{1,0:T(8,128)(2,1)}, u32[]{:S(2)}, u32[]{:S(2)}) collective-permute-start(bf16[256,1536]{1,0:T(8,128)(2,1)} %get-tuple-element.127), channel_id=1, source_target_pairs={{2,0},{3,1},{0,2},{1,3},{6,4},{7,5},{4,6},{5,7},{10,8},{11,9},{8,1... | collective-permute-start | bytes 2359304 | tf_op jit(solution)/shard_map/ppermute | solution.py:124
  313.2 35.0 %collective-permute-start.21 = (bf16[256,1536]{1,0:T(8,128)(2,1)}, bf16[256,1536]{1,0:T(8,128)(2,1)}, u32[]{:S(2)}, u32[]{:S(2)}) collective-permute-start(bf16[256,1536]{1,0:T(8,128)(2,1)} %get-tuple-element.126), channel_id=1, source_target_pairs={{1,0},{0,1},{3,2},{2,3},{5,4},{4,5},{7,6},{6,7},{9,8},{8,9},{11,10... | collective-permute-start | bytes 2359304 | tf_op jit(solution)/shard_map/ppermute | solution.py:124
  348.2 187.6 %reduce-scatter.8.cloned.1.call-start = ((), (), s32[]{:S(2)}) async-start(), calls=%async_computation.9 | async-start | bytes 3981312 | tf_op jit(solution)/shard_map/reduce_scatter | solution.py:276
  355.8 35.2 %collective-permute-start.24 = (bf16[256,1536]{1,0:T(8,128)(2,1)S(1)}, bf16[256,1536]{1,0:T(8,128)(2,1)S(1)}, u32[]{:S(2)}, u32[]{:S(2)}) collective-permute-start(bf16[256,1536]{1,0:T(8,128)(2,1)S(1)} %get-tuple-element.77), channel_id=1, source_target_pairs={{0,3},{1,2},{2,1},{3,0},{4,7},{5,6},{6,5},{7,4},{8,11},{9,10},{10,... | collective-permute-start | bytes 2359304 | tf_op jit(solution)/shard_map/ppermute | solution.py:103
  392.7 34.1 %collective-permute-start.25 = (bf16[256,1536]{1,0:T(8,128)(2,1)}, bf16[256,1536]{1,0:T(8,128)(2,1)}, u32[]{:S(2)}, u32[]{:S(2)}) collective-permute-start(bf16[256,1536]{1,0:T(8,128)(2,1)} %get-tuple-element.124), channel_id=1, source_target_pairs={{3,0},{2,1},{1,2},{0,3},{7,4},{6,5},{5,6},{4,7},{11,8},{10,9},{9,1... | collective-permute-start | bytes 2359304 | tf_op jit(solution)/shard_map/ppermute | solution.py:124
  393.8 36.4 %collective-permute-start.26 = (bf16[256,1536]{1,0:T(8,128)(2,1)}, bf16[256,1536]{1,0:T(8,128)(2,1)}, u32[]{:S(2)}, u32[]{:S(2)}) collective-permute-start(bf16[256,1536]{1,0:T(8,128)(2,1)} %get-tuple-element.123), channel_id=1, source_target_pairs={{2,0},{3,1},{0,2},{1,3},{6,4},{7,5},{4,6},{5,7},{10,8},{11,9},{8,1... | collective-permute-start | bytes 2359304 | tf_op jit(solution)/shard_map/ppermute | solution.py:124
  393.8 36.4 %collective-permute-start.27 = (bf16[256,1536]{1,0:T(8,128)(2,1)}, bf16[256,1536]{1,0:T(8,128)(2,1)}, u32[]{:S(2)}, u32[]{:S(2)}) collective-permute-start(bf16[256,1536]{1,0:T(8,128)(2,1)} %get-tuple-element.122), channel_id=1, source_target_pairs={{1,0},{0,1},{3,2},{2,3},{5,4},{4,5},{7,6},{6,7},{9,8},{8,9},{11,10... | collective-permute-start | bytes 2359304 | tf_op jit(solution)/shard_map/ppermute | solution.py:124
  442.1 36.4 %collective-permute-start.29 = (bf16[256,1536]{1,0:T(8,128)(2,1)}, bf16[256,1536]{1,0:T(8,128)(2,1)}, u32[]{:S(2)}, u32[]{:S(2)}) collective-permute-start(bf16[256,1536]{1,0:T(8,128)(2,1)} %get-tuple-element.119), channel_id=1, source_target_pairs={{2,0},{3,1},{0,2},{1,3},{6,4},{7,5},{4,6},{5,7},{10,8},{11,9},{8,1... | collective-permute-start | bytes 2359304 | tf_op jit(solution)/shard_map/ppermute | solution.py:124
  442.1 36.4 %collective-permute-start.30 = (bf16[256,1536]{1,0:T(8,128)(2,1)}, bf16[256,1536]{1,0:T(8,128)(2,1)}, u32[]{:S(2)}, u32[]{:S(2)}) collective-permute-start(bf16[256,1536]{1,0:T(8,128)(2,1)} %get-tuple-element.118), channel_id=1, source_target_pairs={{1,0},{0,1},{3,2},{2,3},{5,4},{4,5},{7,6},{6,7},{9,8},{8,9},{11,10... | collective-permute-start | bytes 2359304 | tf_op jit(solution)/shard_map/ppermute | solution.py:124
  538.4 20.1 %all-to-all-start.1 = ((bf16[4,48,768]{2,1,0:T(8,128)(2,1)}), bf16[4,48,768]{2,1,0:T(8,128)(2,1)S(1)}, u32[]{:S(2)}, u32[]{:S(2)}) async-start(bf16[4,48,768]{2,1,0:T(8,128)(2,1)} %bitcast.51), calls=%async_computation.4 | async-start | bytes 589824 | tf_op jit(solution)/shard_map/all_to_all | solution.py:287
  (90 other events, 983.9 us)
Sparse Core Ops, SparseCore 0:
  27.5 40.2 all-gather.8
  69.5 127.4 all-gather.4
  198.6 69.7 all-gather.6
  270.6 75.2 reduce-scatter.3
  348.3 142.1 reduce-scatter.5
  492.7 43.0 reduce-scatter.7

commit v4 on v3

--- a/solution.py
+++ b/solution.py
@@ -154,8 +154,8 @@
         self.width = self.cols + round_up(2 + self.bias_cols, LANES)
 
     @staticmethod
-    def fits(n):
-        return n % KV == 0 and H % n == 0
+    def fits(n, dp_n):
+        return n % KV == 0 and H % n == 0 and dp_n % n == 0
 
     def slices(self, values):
         rows = values.shape[0]
@@ -169,17 +169,23 @@
         bias = pad_to(qkv_bias, 0, self.bias_cols * rows).reshape(self.bias_cols, rows)
         extra = jnp.concatenate([attn_gain[None], mlp_gain[None], bias], axis=0).T
         extra = pad_to(extra, 1, self.width - self.cols)
-        extra = jnp.broadcast_to(extra[:, None], (rows, n, extra.shape[1]))
-        pack = jnp.concatenate([self.slices(qkv_weight), extra], axis=2).transpose(1, 0, 2)
-        pack = lax.all_to_all(pack, "ctx", 0, 0, tiled=True).reshape(n * rows, self.width)
-        moves = [(b, (b % dp_n) * n + b // dp_n) for b in range(dp_n * n)]
-        out_block = lax.ppermute(out_weight, ALL, moves)
+        own = jnp.concatenate([qkv_weight, extra, out_weight], axis=1)
+        whole = lax.all_gather(own, "dp", axis=0, tiled=False)
+        qkv_cols, out_first = qkv_weight.shape[1], qkv_weight.shape[1] + extra.shape[1]
+        qkv = whole[:, :, :qkv_cols].reshape(dp_n * rows, qkv_cols)
+        extra = whole[:, :, qkv_cols:out_first].reshape(dp_n * rows, 1, -1)
+        extra = jnp.broadcast_to(extra, (dp_n * rows, n, extra.shape[2]))
+        parts = jnp.concatenate([self.slices(qkv), extra], axis=2).transpose(1, 0, 2)
+        blocks = whole[:, :, out_first:]
+        parts, blocks = lax.optimization_barrier((self.peers.exchange(parts), blocks))
+        parts = parts.reshape(n, dp_n, rows, self.width)
+        joint = parts.transpose(1, 0, 2, 3).reshape(dp_n * n * rows, self.width)
         self.out_rows, self.out_cols = out_weight.shape
         self.extra_rows = self.out_rows * self.out_cols // self.width
-        pack = jnp.concatenate([pack, out_block.reshape(self.extra_rows, self.width)], axis=0)
-        whole = lax.all_gather(pack, "dp", axis=0, tiled=False)
-        joint = whole[:, : n * rows].reshape(dp_n * n * rows, self.width)
-        self.out_slice = whole[:, n * rows :].reshape(dp_n * self.out_rows, self.out_cols)
+        run = dp_n // n
+        blocks = blocks.reshape(n, run, rows, self.out_cols)
+        blocks = self.peers.exchange(blocks).transpose(1, 0, 2, 3)
+        self.out_slice = blocks.reshape(dp_n * rows, self.out_cols)
         self.joint = joint
         bias = joint[:, self.cols + 2 : self.cols + 2 + self.bias_cols]
         bias = bias.reshape(dp_n * n, rows, self.bias_cols).transpose(0, 2, 1)
@@ -188,6 +194,10 @@
             [lax.dynamic_slice(bias, (start,), (size,)) for start, size in self.places()]
         ).astype(F32)
         return joint[:, self.cols].astype(F32), joint[:, self.cols + 1].astype(F32)
+
+    def hold(self, values):
+        self.joint, values = lax.optimization_barrier((self.joint, values))
+        return values
 
     def places(self):
         me = self.peers.me
@@ -355,6 +365,9 @@
         self.attended = jnp.concatenate([piece[0] for piece in pieces], axis=1).astype(BF)
         self.log_totals = [piece[1] for piece in pieces]
         return self.resid + dot(self.attended.reshape(span, -1), self.out), before
+
+    def hold(self, values):
+        return values
 
     @staticmethod
     def part(group):
@@ -427,7 +440,7 @@
     rows, hidden_width = gate_weight.shape
     n = ctx_n
     peers = Peers("ctx", n)
-    if HeadSplit.fits(n):
+    if HeadSplit.fits(n, dp_n) and out_weight.shape[0] == rows:
         attention = HeadSplit(peers, dp_n, rows, qkv_bias.shape[0])
         blocks = peers.spread(inputs[0])
     else:
@@ -453,7 +466,7 @@
     down = lax.all_gather(pad_to(down_weight, 0, padded), "dp", axis=0, tiled=True)
 
     blocks, own_cotangent = lax.optimization_barrier((blocks, cotangent[0]))
-    grad_out = peers.spread(own_cotangent)
+    grad_out = peers.spread(attention.hold(own_cotangent))
     resid_mid, grad_out = attention.forward(blocks, segment_ids, gain_one, grad_out)
     inv_two = inv_rms_of(resid_mid)
     normed_own = (resid_mid * inv_two * gain_two).astype(BF)

time: 577 us -> 588 us (1.019)
  waiting for transfers between devices: 241 us -> 250 us
  local copies, waits for them, and re-layouts: 71.4 us -> 79.4 us
    ppermute x6 -> x12, waiting for transfers between devices: 30.8 us -> 76 us  [exchange(): received.append(lax.ppermute(block, self.axis, pairs))]
    all_gather x1, waiting for transfers between devices: 21.8 us -> 0.02 us  [on_device(): lax.all_gather(pad_to(down_weight, 0, padded), 'dp', axis=0, tiled=True)]
    ppermute x15, waiting for transfers between devices: 75.6 us -> 65.7 us  [spread(): blocks.append(lax.ppermute(own, self.axis, pairs))]
    ppermute x1 -> x0, waiting for transfers between devices: 6.11 us -> none  [gather(): out_block = lax.ppermute(out_weight, ALL, moves)]
    ppermute x6 -> x12, starting transfers between devices: 5.42 us -> 11.4 us  [exchange(): received.append(lax.ppermute(block, self.axis, pairs))]
    unnamed x153 -> x141, local copies, waits for them, and re-layouts: 19.1 us -> 21.6 us
  transfers between devices with their start and end apart: 43 -> 47, of which waited for: 26 -> 27; matrix products, arithmetic and copies ran while one was open for 42% -> 43% of each run, Pallas kernels for 0% -> 0%
where the time goes in v4:
time: 588 us; the launch traced here: 580 us
  waiting for transfers between devices  250 us (43%)
  matrix products  140 us (24%)
  local copies, waits for them, and re-layouts  79.4 us (14%)
  other arithmetic  50.5 us (9%)
  starting transfers between devices  43.7 us (7%)
  between operations  16.1 us (3%)
    ppermute x12, waiting for transfers between devices, deliver(): received.append(lax.ppermute(share, self.axis, pairs))  77.8 us
    ppermute x12, waiting for transfers between devices, exchange(): received.append(lax.ppermute(block, self.axis, pairs))  76 us
    ppermute x15, waiting for transfers between devices, spread(): blocks.append(lax.ppermute(own, self.axis, pairs))  65.7 us
    dot_general x4, matrix products, dot_t(): lax.dot_general(a, b, (((1,), (1,)), ((), ())), preferred_element_type=F32)  44.8 us
    dot_general x4, matrix products, t_dot(): lax.dot_general(a, b, (((0,), (0,)), ((), ())), preferred_element_type=F32)  39.2 us
    dot_general x4, matrix products, dot(): return jnp.dot(a, b, preferred_element_type=F32)  35.8 us
    unnamed x141, local copies, waits for them, and re-layouts  21.6 us
    reduce_scatter x1, waiting for transfers between devices, on_device(): lax.psum_scatter(joint_term, 'dp', scatter_dimension=0, tiled=True)  16.1 us
  transfers between devices with their start and end apart: 47, of which 27 were waited for; matrix products, arithmetic and copies ran while one was open for 43% of the time, Pallas kernels for 0%

profile of v4, /device:TPU:25, one launch (start us, length us, event | category | flops | bytes accessed | tf_op | source)
XLA Modules:
  0.0 580.3 jit_solution(10006842681922912131)
XLA Ops:
  24.4 8.6 %collective-permute-done.21 = bf16[1,48,4608]{2,1,0:T(8,128)(2,1)S(1)} collective-permute-done((bf16[1,48,4608]{2,1,0:T(8,128)(2,1)S(1)}, bf16[1,48,4608]{2,1,0:T(8,128)(2,1)S(1)}, u32[]{:S(2)}, u32[]{:S(2)}) %collective-permute-start.21) | collective-permute-done | bytes 442400 | tf_op jit(solution)/shard_map/ppermute | solution.py:111
  33.9 9.5 %collective-permute-done.23 = bf16[1,48,4608]{2,1,0:T(8,128)(2,1)S(1)} collective-permute-done((bf16[1,48,4608]{2,1,0:T(8,128)(2,1)S(1)}, bf16[1,48,4608]{2,1,0:T(8,128)(2,1)S(1)}, u32[]{:S(2)}, u32[]{:S(2)}) %collective-permute-start.23) | collective-permute-done | bytes 442400 | tf_op jit(solution)/shard_map/ppermute | solution.py:111
  50.2 12.3 %collective-permute-done.6 = s32[1,256]{1,0:T(1,128)S(1)} collective-permute-done((s32[1,256]{1,0:T(1,128)S(1)}, s32[1,256]{1,0:T(1,128)S(1)}, u32[]{:S(2)}, u32[]{:S(2)}) %collective-permute-start.6) | collective-permute-done | bytes 1056 | tf_op jit(solution)/shard_map/ppermute | solution.py:103
  84.6 7.2 %collective-permute-done.3 = bf16[1,384,768]{1,2,0:T(8,128)(2,1)S(1)} collective-permute-done((bf16[1,384,768]{1,2,0:T(8,128)(2,1)S(1)}, bf16[1,384,768]{1,2,0:T(8,128)(2,1)S(1)}, u32[]{:S(2)}, u32[]{:S(2)}) %collective-permute-start.3) | collective-permute-done | bytes 589856 | tf_op jit(solution)/shard_map/ppermute | solution.py:111
  91.8 6.6 %collective-permute-done.4 = bf16[1,384,768]{1,2,0:T(8,128)(2,1)S(1)} collective-permute-done((bf16[1,384,768]{1,2,0:T(8,128)(2,1)S(1)}, bf16[1,384,768]{1,2,0:T(8,128)(2,1)S(1)}, u32[]{:S(2)}, u32[]{:S(2)}) %collective-permute-start.4) | collective-permute-done | bytes 589856 | tf_op jit(solution)/shard_map/ppermute | solution.py:111
  98.4 7.1 %collective-permute-done.5 = bf16[1,384,768]{1,2,0:T(8,128)(2,1)S(1)} collective-permute-done((bf16[1,384,768]{1,2,0:T(8,128)(2,1)S(1)}, bf16[1,384,768]{1,2,0:T(8,128)(2,1)S(1)}, u32[]{:S(2)}, u32[]{:S(2)}) %collective-permute-start.5) | collective-permute-done | bytes 589856 | tf_op jit(solution)/shard_map/ppermute | solution.py:111
  135.9 22.3 %collective-permute-done.12 = bf16[1,2,48,1536]{3,2,1,0:T(8,128)(2,1)} collective-permute-done((bf16[1,2,48,1536]{3,2,1,0:T(8,128)(2,1)}, bf16[1,2,48,1536]{3,2,1,0:T(8,128)(2,1)}, u32[]{:S(2)}, u32[]{:S(2)}) %collective-permute-start.12) | collective-permute-done | bytes 294944 | tf_op jit(solution)/shard_map/ppermute | solution.py:111
  172.4 12.9 %collective-permute-done.15 = bf16[256,1536]{1,0:T(8,128)(2,1)S(1)} collective-permute-done((bf16[256,1536]{1,0:T(8,128)(2,1)S(1)}, bf16[256,1536]{1,0:T(8,128)(2,1)S(1)}, u32[]{:S(2)}, u32[]{:S(2)}) %collective-permute-start.15) | collective-permute-done | bytes 786464 | tf_op jit(solution)/shard_map/ppermute | solution.py:124
  185.2 21.8 %collective-permute-done.16 = bf16[256,1536]{1,0:T(8,128)(2,1)S(1)} collective-permute-done((bf16[256,1536]{1,0:T(8,128)(2,1)S(1)}, bf16[256,1536]{1,0:T(8,128)(2,1)S(1)}, u32[]{:S(2)}, u32[]{:S(2)}) %collective-permute-start.16) | collective-permute-done | bytes 786464 | tf_op jit(solution)/shard_map/ppermute | solution.py:124
  215.5 11.4 %collective-permute-done.18 = bf16[256,1536]{1,0:T(8,128)(2,1)S(1)} collective-permute-done((bf16[256,1536]{1,0:T(8,128)(2,1)S(1)}, bf16[256,1536]{1,0:T(8,128)(2,1)S(1)}, u32[]{:S(2)}, u32[]{:S(2)}) %collective-permute-start.18) | collective-permute-done | bytes 786464 | tf_op jit(solution)/shard_map/ppermute | solution.py:103
  228.6 15.9 %collective-permute-done.20 = bf16[256,1536]{1,0:T(8,128)(2,1)} collective-permute-done((bf16[256,1536]{1,0:T(8,128)(2,1)S(1)}, bf16[256,1536]{1,0:T(8,128)(2,1)}, u32[]{:S(2)}, u32[]{:S(2)}) %collective-permute-start.20) | collective-permute-done | bytes 786464 | tf_op jit(solution)/shard_map/ppermute | solution.py:103
  244.5 18.0 %fusion.24 = f32[1024,4608]{1,0:T(8,128)S(1)} fusion(bf16[1536,4608]{1,0:T(8,128)(2,1)} %all-gather.5.cloned.1.call-done, bf16[256,1536]{1,0:T(8,128)(2,1)} %collective-permute-done.20, bf16[256,1536]{1,0:T(8,128)(2,1)} %copy-done.61, bf16[256,1536]{1,0:T(8,128)(2,1)S(1)} %collective-permute-done.18, bf16[256,1536]{1,0:T(8,128)(2,1)S(1)} %multiply_convert_fusion.4), kind=kOutput, calls=%fused_computation.86 | convolution fusion | flops 14508097536 | bytes 36175872 | tf_op jit(solution)/shard_map/dot_general | solution.py:48
  272.1 9.4 %convolution_convert_fusion.1 = bf16[2304,1536]{1,0:T(8,128)(2,1)} fusion(bf16[1024,2304]{1,0:T(8,128)(2,1)S(1)} %multiply_convert_fusion.2, bf16[1024,1536]{1,0:T(8,128)(2,1)S(1)} %copy-done.52), kind=kOutput, calls=%fused_computation.8 | convolution fusion | flops 7251296256 | bytes 14942208 | tf_op jit(solution)/shard_map/dot_general | solution.py:56
  281.6 20.0 %multiply_convert_fusion.1 = (bf16[1024,2304]{1,0:T(8,128)(2,1)}, bf16[1024,2304]{1,0:T(8,128)(2,1)}) fusion(f32[1024,4608]{1,0:T(8,128)} %copy-done, bf16[1024,1536]{1,0:T(8,128)(2,1)} %copy-done.51, bf16[2304,1536]{1,0:T(8,128)(2,1)} %all-gather.7.cloned.1.call-done), kind=kOutput, calls=%fused_computation.12 | convolution fusion | flops 7278428160 | bytes 38535168 | tf_op jit(solution)/shard_map/dot_general | solution.py:52
  301.6 20.5 %fusion.7 = bf16[1024,1536]{1,0:T(8,128)(2,1)S(1)} fusion(bf16[1536,4608]{1,0:T(8,128)(2,1)} %all-gather.5.cloned.1.call-done, bf16[1024,2304]{1,0:T(8,128)(2,1)} %get-tuple-element.141, bf16[1024,2304]{1,0:T(8,128)(2,1)} %get-tuple-element.140), kind=kOutput, calls=%fused_computation.24 | convolution fusion | flops 14515961856 | bytes 26738688 | tf_op jit(solution)/shard_map/dot_general | solution.py:52
  326.2 22.7 %convolution_convert_fusion = bf16[1536,4608]{1,0:T(8,128)(2,1)} fusion(bf16[1024,2304]{1,0:T(8,128)(2,1)} %get-tuple-element.141, bf16[1024,2304]{1,0:T(8,128)(2,1)} %get-tuple-element.140, bf16[256,1536]{1,0:T(8,128)(2,1)} %collective-permute-done.20, bf16[256,1536]{1,0:T(8,128)(2,1)} %copy-done.61, bf16[256,1536]{1,0:T(8,128)(2,1)} %copy-done.60, ...), kind=kOutput, calls=%fused_computation | convolution fusion | flops 14534049792 | bytes 26738688 | tf_op jit(solution)/shard_map/dot_general | solution.py:56
  348.9 12.2 %collective-permute-done.25 = bf16[256,1536]{1,0:T(8,128)(2,1)} collective-permute-done((bf16[256,1536]{1,0:T(8,128)(2,1)}, bf16[256,1536]{1,0:T(8,128)(2,1)}, u32[]{:S(2)}, u32[]{:S(2)}) %collective-permute-start.25) | collective-permute-done | bytes 786464 | tf_op jit(solution)/shard_map/ppermute | solution.py:124
  369.7 11.9 %convolution_convert_fusion.3 = bf16[1024,1536]{1,0:T(8,128)(2,1)S(1)} fusion(bf16[1024,2304]{1,0:T(8,128)(2,1)} %copy-done.23, bf16[2304,1536]{1,0:T(8,128)(2,1)} %all-gather.7.cloned.1.call-done), kind=kOutput, calls=%fused_computation.26 | convolution fusion | flops 7249330176 | bytes 14942208 | tf_op jit(solution)/shard_map/dot_general | solution.py:48
  385.8 16.4 %collective-permute-done.29 = bf16[256,1536]{1,0:T(8,128)(2,1)S(1)} collective-permute-done((bf16[256,1536]{1,0:T(8,128)(2,1)S(1)}, bf16[256,1536]{1,0:T(8,128)(2,1)S(1)}, u32[]{:S(2)}, u32[]{:S(2)}) %collective-permute-start.29) | collective-permute-done | bytes 786464 | tf_op jit(solution)/shard_map/ppermute | solution.py:103
  458.2 10.0 %collective-permute-done.33 = bf16[256,1536]{1,0:T(8,128)(2,1)} collective-permute-done((bf16[256,1536]{1,0:T(8,128)(2,1)}, bf16[256,1536]{1,0:T(8,128)(2,1)}, u32[]{:S(2)}, u32[]{:S(2)}) %collective-permute-start.33) | collective-permute-done | bytes 786464 | tf_op jit(solution)/shard_map/ppermute | solution.py:124
  468.1 18.1 %collective-permute-done.34 = bf16[256,1536]{1,0:T(8,128)(2,1)} collective-permute-done((bf16[256,1536]{1,0:T(8,128)(2,1)}, bf16[256,1536]{1,0:T(8,128)(2,1)}, u32[]{:S(2)}, u32[]{:S(2)}) %collective-permute-start.34) | collective-permute-done | bytes 786464 | tf_op jit(solution)/shard_map/ppermute | solution.py:124
  486.2 16.1 %reduce-scatter.6.cloned.1.call-done = bf16[192,4608]{1,0:T(8,128)(2,1)} async-done(((bf16[1536,4608]{1,0:T(8,128)(2,1)}), bf16[192,4608]{1,0:T(8,128)(2,1)}) %reduce-scatter.6.cloned.1.call-update) | async-done | bytes 1769488 | tf_op jit(solution)/shard_map/reduce_scatter | solution.py:494
  520.3 9.4 %collective-permute-done.38 = bf16[1,48,4608]{2,1,0:T(8,128)(2,1)S(1)} collective-permute-done((bf16[1,48,4608]{2,1,0:T(8,128)(2,1)S(1)}, bf16[1,48,4608]{2,1,0:T(8,128)(2,1)S(1)}, u32[]{:S(2)}, u32[]{:S(2)}) %collective-permute-start.38) | collective-permute-done | bytes 442400 | tf_op jit(solution)/shard_map/ppermute | solution.py:111
  559.3 10.2 %collective-permute-done.39 = bf16[48,1536]{1,0:T(8,128)(2,1)S(1)} collective-permute-done((bf16[48,1536]{1,0:T(8,128)(2,1)S(1)}, bf16[48,1536]{1,0:T(8,128)(2,1)S(1)}, u32[]{:S(2)}, u32[]{:S(2)}) %collective-permute-start.39) | collective-permute-done | bytes 147488 | tf_op jit(solution)/shard_map/ppermute | solution.py:294
  (376 shorter events, 233.9 us)
Async XLA Ops:
  7.2 59.2 %all-gather.9.cloned.1.call-start = ((), (), s32[]{:S(2)}) async-start(), calls=%async_computation.9 | async-start | bytes 3207168 | tf_op jit(solution)/shard_map/all_gather | solution.py:173
  10.5 233.9 %all-gather.5.cloned.1.call-start = ((), (), s32[]{:S(2)}) async-start(), calls=%async_computation.4 | async-start | bytes 15925248 | tf_op jit(solution)/shard_map/all_gather | solution.py:465
  44.8 236.8 %all-gather.7.cloned.1.call-start = ((), (), s32[]{:S(2)}) async-start(), calls=%async_computation.5 | async-start | bytes 7962624 | tf_op jit(solution)/shard_map/all_gather | solution.py:466
  46.1 29.3 %collective-permute-start.1 = (bf16[256,1536]{1,0:T(8,128)(2,1)S(1)}, bf16[256,1536]{1,0:T(8,128)(2,1)}, u32[]{:S(2)}, u32[]{:S(2)}) collective-permute-start(bf16[256,1536]{1,0:T(8,128)(2,1)S(1)} %bitcast.161), channel_id=1, source_target_pairs={{0,2},{1,3},{2,0},{3,1},{4,6},{5,7},{6,4},{7,5},{8,10},{9,11},{10,... | collective-permute-start | bytes 2359304 | tf_op jit(solution)/shard_map/ppermute | solution.py:103
  50.1 311.0 %reduce-scatter.4.cloned.1.call-start = ((), (), s32[]{:S(2)}) async-start(), calls=%async_computation.6 | async-start | bytes 7962624 | tf_op jit(solution)/shard_map/reduce_scatter | solution.py:483
  74.2 31.3 %collective-permute-start.5 = (bf16[1,384,768]{1,2,0:T(8,128)(2,1)S(1)}, bf16[1,384,768]{1,2,0:T(8,128)(2,1)S(1)}, u32[]{:S(2)}, u32[]{:S(2)}) collective-permute-start(bf16[1,384,768]{1,2,0:T(8,128)(2,1)S(1)} %get-tuple-element.157), channel_id=1, source_target_pairs={{3,0},{2,1},{1,2},{0,3},{7,4},{6,5},{5,6},{4,7},{11,8},{10,9},{9,1... | collective-permute-start | bytes 1769480 | tf_op jit(solution)/shard_map/ppermute | solution.py:111
  117.7 49.8 %collective-permute-start.10 = (bf16[256,1536]{1,0:T(8,128)(2,1)}, bf16[256,1536]{1,0:T(8,128)(2,1)}, u32[]{:S(2)}, u32[]{:S(2)}) collective-permute-start(bf16[256,1536]{1,0:T(8,128)(2,1)} %bitcast.1), channel_id=1, source_target_pairs={{0,2},{1,3},{2,0},{3,1},{4,6},{5,7},{6,4},{7,5},{8,10},{9,11},{10,... | collective-permute-start | bytes 2359304 | tf_op jit(solution)/shard_map/ppermute | solution.py:103
  118.1 49.5 %collective-permute-start.11 = (bf16[256,1536]{1,0:T(8,128)(2,1)}, bf16[256,1536]{1,0:T(8,128)(2,1)}, u32[]{:S(2)}, u32[]{:S(2)}) collective-permute-start(bf16[256,1536]{1,0:T(8,128)(2,1)} %bitcast.1), channel_id=1, source_target_pairs={{0,3},{1,2},{2,1},{3,0},{4,7},{5,6},{6,5},{7,4},{8,11},{9,10},{10,... | collective-permute-start | bytes 2359304 | tf_op jit(solution)/shard_map/ppermute | solution.py:103
  120.6 47.0 %collective-permute-start.9 = (bf16[256,1536]{1,0:T(8,128)(2,1)}, bf16[256,1536]{1,0:T(8,128)(2,1)}, u32[]{:S(2)}, u32[]{:S(2)}) collective-permute-start(bf16[256,1536]{1,0:T(8,128)(2,1)} %bitcast.1), channel_id=1, source_target_pairs={{0,1},{1,0},{2,3},{3,2},{4,5},{5,4},{6,7},{7,6},{8,9},{9,8},{10,11... | collective-permute-start | bytes 2359304 | tf_op jit(solution)/shard_map/ppermute | solution.py:103
  121.8 36.4 %collective-permute-start.12 = (bf16[1,2,48,1536]{3,2,1,0:T(8,128)(2,1)}, bf16[1,2,48,1536]{3,2,1,0:T(8,128)(2,1)}, u32[]{:S(2)}, u32[]{:S(2)}) collective-permute-start(bf16[1,2,48,1536]{3,2,1,0:T(8,128)(2,1)} %get-tuple-element.176), channel_id=1, source_target_pairs={{1,0},{0,1},{3,2},{2,3},{5,4},{4,5},{7,6},{6,7},{9,8},{8,9},{11,10... | collective-permute-start | bytes 884744 | tf_op jit(solution)/shard_map/ppermute | solution.py:111
  123.2 41.6 %collective-permute-start.13 = (bf16[1,2,48,1536]{3,2,1,0:T(8,128)(2,1)}, bf16[1,2,48,1536]{3,2,1,0:T(8,128)(2,1)}, u32[]{:S(2)}, u32[]{:S(2)}) collective-permute-start(bf16[1,2,48,1536]{3,2,1,0:T(8,128)(2,1)} %get-tuple-element.175), channel_id=1, source_target_pairs={{2,0},{3,1},{0,2},{1,3},{6,4},{7,5},{4,6},{5,7},{10,8},{11,9},{8,1... | collective-permute-start | bytes 884744 | tf_op jit(solution)/shard_map/ppermute | solution.py:111
  172.0 35.0 %collective-permute-start.16 = (bf16[256,1536]{1,0:T(8,128)(2,1)S(1)}, bf16[256,1536]{1,0:T(8,128)(2,1)S(1)}, u32[]{:S(2)}, u32[]{:S(2)}) collective-permute-start(bf16[256,1536]{1,0:T(8,128)(2,1)S(1)} %get-tuple-element.156), channel_id=1, source_target_pairs={{2,0},{3,1},{0,2},{1,3},{6,4},{7,5},{4,6},{5,7},{10,8},{11,9},{8,1... | collective-permute-start | bytes 2359304 | tf_op jit(solution)/shard_map/ppermute | solution.py:124
  172.2 34.8 %collective-permute-start.17 = (bf16[256,1536]{1,0:T(8,128)(2,1)S(1)}, bf16[256,1536]{1,0:T(8,128)(2,1)S(1)}, u32[]{:S(2)}, u32[]{:S(2)}) collective-permute-start(bf16[256,1536]{1,0:T(8,128)(2,1)S(1)} %get-tuple-element.155), channel_id=1, source_target_pairs={{1,0},{0,1},{3,2},{2,3},{5,4},{4,5},{7,6},{6,7},{9,8},{8,9},{11,10... | collective-permute-start | bytes 2359304 | tf_op jit(solution)/shard_map/ppermute | solution.py:124
  209.3 35.2 %collective-permute-start.20 = (bf16[256,1536]{1,0:T(8,128)(2,1)S(1)}, bf16[256,1536]{1,0:T(8,128)(2,1)}, u32[]{:S(2)}, u32[]{:S(2)}) collective-permute-start(bf16[256,1536]{1,0:T(8,128)(2,1)S(1)} %multiply_convert_fusion.4), channel_id=1, source_target_pairs={{0,3},{1,2},{2,1},{3,0},{4,7},{5,6},{6,5},{7,4},{8,11},{9,10},{10,... | collective-permute-start | bytes 2359304 | tf_op jit(solution)/shard_map/ppermute | solution.py:103
  281.5 220.8 %reduce-scatter.6.cloned.1.call-start = ((), (), s32[]{:S(2)}) async-start(), calls=%async_computation.7 | async-start | bytes 15925248 | tf_op jit(solution)/shard_map/reduce_scatter | solution.py:494
  324.7 36.4 %collective-permute-start.25 = (bf16[256,1536]{1,0:T(8,128)(2,1)}, bf16[256,1536]{1,0:T(8,128)(2,1)}, u32[]{:S(2)}, u32[]{:S(2)}) collective-permute-start(bf16[256,1536]{1,0:T(8,128)(2,1)} %get-tuple-element.151), channel_id=1, source_target_pairs={{2,0},{3,1},{0,2},{1,3},{6,4},{7,5},{4,6},{5,7},{10,8},{11,9},{8,1... | collective-permute-start | bytes 2359304 | tf_op jit(solution)/shard_map/ppermute | solution.py:124
  324.7 36.4 %collective-permute-start.26 = (bf16[256,1536]{1,0:T(8,128)(2,1)}, bf16[256,1536]{1,0:T(8,128)(2,1)}, u32[]{:S(2)}, u32[]{:S(2)}) collective-permute-start(bf16[256,1536]{1,0:T(8,128)(2,1)} %get-tuple-element.150), channel_id=1, source_target_pairs={{1,0},{0,1},{3,2},{2,3},{5,4},{4,5},{7,6},{6,7},{9,8},{8,9},{11,10... | collective-permute-start | bytes 2359304 | tf_op jit(solution)/shard_map/ppermute | solution.py:124
  361.1 186.4 %reduce-scatter.8.cloned.1.call-start = ((), (), s32[]{:S(2)}) async-start(), calls=%async_computation.8 | async-start | bytes 3981312 | tf_op jit(solution)/shard_map/reduce_scatter | solution.py:286
  368.5 33.7 %collective-permute-start.29 = (bf16[256,1536]{1,0:T(8,128)(2,1)S(1)}, bf16[256,1536]{1,0:T(8,128)(2,1)S(1)}, u32[]{:S(2)}, u32[]{:S(2)}) collective-permute-start(bf16[256,1536]{1,0:T(8,128)(2,1)S(1)} %get-tuple-element.101), channel_id=1, source_target_pairs={{0,3},{1,2},{2,1},{3,0},{4,7},{5,6},{6,5},{7,4},{8,11},{9,10},{10,... | collective-permute-start | bytes 2359304 | tf_op jit(solution)/shard_map/ppermute | solution.py:103
  403.9 34.6 %collective-permute-start.30 = (bf16[256,1536]{1,0:T(8,128)(2,1)}, bf16[256,1536]{1,0:T(8,128)(2,1)}, u32[]{:S(2)}, u32[]{:S(2)}) collective-permute-start(bf16[256,1536]{1,0:T(8,128)(2,1)} %get-tuple-element.148), channel_id=1, source_target_pairs={{3,0},{2,1},{1,2},{0,3},{7,4},{6,5},{5,6},{4,7},{11,8},{10,9},{9,1... | collective-permute-start | bytes 2359304 | tf_op jit(solution)/shard_map/ppermute | solution.py:124
  404.9 36.5 %collective-permute-start.31 = (bf16[256,1536]{1,0:T(8,128)(2,1)}, bf16[256,1536]{1,0:T(8,128)(2,1)}, u32[]{:S(2)}, u32[]{:S(2)}) collective-permute-start(bf16[256,1536]{1,0:T(8,128)(2,1)} %get-tuple-element.147), channel_id=1, source_target_pairs={{2,0},{3,1},{0,2},{1,3},{6,4},{7,5},{4,6},{5,7},{10,8},{11,9},{8,1... | collective-permute-start | bytes 2359304 | tf_op jit(solution)/shard_map/ppermute | solution.py:124
  406.6 34.8 %collective-permute-start.32 = (bf16[256,1536]{1,0:T(8,128)(2,1)}, bf16[256,1536]{1,0:T(8,128)(2,1)}, u32[]{:S(2)}, u32[]{:S(2)}) collective-permute-start(bf16[256,1536]{1,0:T(8,128)(2,1)} %get-tuple-element.146), channel_id=1, source_target_pairs={{1,0},{0,1},{3,2},{2,3},{5,4},{4,5},{7,6},{6,7},{9,8},{8,9},{11,10... | collective-permute-start | bytes 2359304 | tf_op jit(solution)/shard_map/ppermute | solution.py:124
  449.7 36.5 %collective-permute-start.34 = (bf16[256,1536]{1,0:T(8,128)(2,1)}, bf16[256,1536]{1,0:T(8,128)(2,1)}, u32[]{:S(2)}, u32[]{:S(2)}) collective-permute-start(bf16[256,1536]{1,0:T(8,128)(2,1)} %get-tuple-element.143), channel_id=1, source_target_pairs={{2,0},{3,1},{0,2},{1,3},{6,4},{7,5},{4,6},{5,7},{10,8},{11,9},{8,1... | collective-permute-start | bytes 2359304 | tf_op jit(solution)/shard_map/ppermute | solution.py:124
  451.4 34.8 %collective-permute-start.35 = (bf16[256,1536]{1,0:T(8,128)(2,1)}, bf16[256,1536]{1,0:T(8,128)(2,1)}, u32[]{:S(2)}, u32[]{:S(2)}) collective-permute-start(bf16[256,1536]{1,0:T(8,128)(2,1)} %get-tuple-element.142), channel_id=1, source_target_pairs={{1,0},{0,1},{3,2},{2,3},{5,4},{4,5},{7,6},{6,7},{9,8},{8,9},{11,10... | collective-permute-start | bytes 2359304 | tf_op jit(solution)/shard_map/ppermute | solution.py:124
  (88 other events, 1109.6 us)
Sparse Core Ops, SparseCore 0:
  10.7 35.1 all-gather.8
  47.5 127.4 all-gather.4
  176.7 69.7 all-gather.6
  281.6 75.3 reduce-scatter.3
  361.3 141.0 reduce-scatter.5
  504.5 43.0 reduce-scatter.7

commit v5 on v4

--- a/solution.py
+++ b/solution.py
@@ -195,10 +195,6 @@
         ).astype(F32)
         return joint[:, self.cols].astype(F32), joint[:, self.cols + 1].astype(F32)
 
-    def hold(self, values):
-        self.joint, values = lax.optimization_barrier((self.joint, values))
-        return values
-
     def places(self):
         me = self.peers.me
         group = me // self.share
@@ -208,7 +204,7 @@
             (H * HD + KV * HD + group * HD, HD),
         )
 
-    def forward(self, blocks, segment_ids, gain, before):
+    def forward(self, blocks, segment_ids, gain):
         peers, n = self.peers, self.n
         span = blocks[0].shape[0]
         length = n * span
@@ -233,10 +229,10 @@
         attended, self.log_total = attend(
             self.query, self.key, self.values, self.visible, self.scale
         )
-        self.attended, before = lax.optimization_barrier((attended.astype(BF), before))
+        self.attended = attended.astype(BF)
         flat = self.attended.reshape(length, self.q_cols)
         mixed = add_up(peers.deliver(dot(flat, self.out_slice).astype(BF)))
-        return blocks[0].astype(F32) + mixed, before
+        return blocks[0].astype(F32) + mixed
 
     def backward(self, mid_grad, gain, gain_two_term, filled, joint_grad, finish):
         peers, n, rows, dp_n = self.peers, self.n, self.rows, self.dp_n
@@ -324,7 +320,7 @@
         self.bias = bias.astype(F32)
         return gain_one.astype(F32), gain_two.astype(F32)
 
-    def forward(self, blocks, segment_ids, gain, before):
+    def forward(self, blocks, segment_ids, gain):
         own = blocks[0]
         span = own.shape[0]
         width = KV * HD
@@ -364,10 +360,7 @@
         ]
         self.attended = jnp.concatenate([piece[0] for piece in pieces], axis=1).astype(BF)
         self.log_totals = [piece[1] for piece in pieces]
-        return self.resid + dot(self.attended.reshape(span, -1), self.out), before
-
-    def hold(self, values):
-        return values
+        return self.resid + dot(self.attended.reshape(span, -1), self.out)
 
     @staticmethod
     def part(group):
@@ -465,13 +458,14 @@
     gate_up = lax.all_gather(joint, "dp", axis=0, tiled=True)
     down = lax.all_gather(pad_to(down_weight, 0, padded), "dp", axis=0, tiled=True)
 
-    blocks, own_cotangent = lax.optimization_barrier((blocks, cotangent[0]))
-    grad_out = peers.spread(attention.hold(own_cotangent))
-    resid_mid, grad_out = attention.forward(blocks, segment_ids, gain_one, grad_out)
+    resid_mid = attention.forward(blocks, segment_ids, gain_one)
     inv_two = inv_rms_of(resid_mid)
     normed_own = (resid_mid * inv_two * gain_two).astype(BF)
-    normed = jnp.concatenate(peers.spread(normed_own))
-    grad_out = jnp.concatenate(grad_out)
+    blocks, gate_up, own_cotangent = lax.optimization_barrier(
+        (peers.spread(normed_own), gate_up, cotangent[0])
+    )
+    normed = jnp.concatenate(blocks)
+    grad_out = jnp.concatenate(peers.spread(own_cotangent))
     pre = dot(normed, gate_up)
     gate_pre = pre[:, :wide]
     up_pre = pre[:, wide:]

time: 588 us -> 576 us (0.980)
  waiting for transfers between devices: 250 us -> 238 us
    ppermute x12, waiting for transfers between devices: 76 us -> 53.2 us  [exchange(): received.append(lax.ppermute(block, self.axis, pairs))]
    ppermute x15, waiting for transfers between devices: 65.7 us -> 77.5 us  [spread(): blocks.append(lax.ppermute(own, self.axis, pairs))]
    unnamed x141 -> x160, local copies, waits for them, and re-layouts: 21.6 us -> 21.9 us
  transfers between devices with their start and end apart: 47 -> 47, of which waited for: 27 -> 26; matrix products, arithmetic and copies ran while one was open for 43% -> 43% of each run, Pallas kernels for 0% -> 0%
where the time goes in v5:
time: 576 us; the launch traced here: 569 us
  waiting for transfers between devices  238 us (41%)
  matrix products  140 us (24%)
  local copies, waits for them, and re-layouts  81 us (14%)
  other arithmetic  50.4 us (9%)
  starting transfers between devices  43.2 us (8%)
  between operations  16 us (3%)
    ppermute x12, waiting for transfers between devices, deliver(): received.append(lax.ppermute(share, self.axis, pairs))  78.2 us
    ppermute x15, waiting for transfers between devices, spread(): blocks.append(lax.ppermute(own, self.axis, pairs))  77.5 us
    ppermute x12, waiting for transfers between devices, exchange(): received.append(lax.ppermute(block, self.axis, pairs))  53.2 us
    dot_general x4, matrix products, dot_t(): lax.dot_general(a, b, (((1,), (1,)), ((), ())), preferred_element_type=F32)  44.8 us
    dot_general x4, matrix products, t_dot(): lax.dot_general(a, b, (((0,), (0,)), ((), ())), preferred_element_type=F32)  38.2 us
    dot_general x4, matrix products, dot(): return jnp.dot(a, b, preferred_element_type=F32)  36.1 us
    unnamed x160, local copies, waits for them, and re-layouts  21.9 us
    reduce_scatter x1, waiting for transfers between devices, on_device(): lax.psum_scatter(joint_term, 'dp', scatter_dimension=0, tiled=True)  14.8 us
  transfers between devices with their start and end apart: 47, of which 26 were waited for; matrix products, arithmetic and copies ran while one was open for 43% of the time, Pallas kernels for 0%

profile of v5, /device:TPU:25, one launch (start us, length us, event | category | flops | bytes accessed | tf_op | source)
XLA Modules:
  0.0 568.7 jit_solution(3580816049212186034)
XLA Ops:
  24.4 8.6 %collective-permute-done.18 = bf16[1,48,4608]{2,1,0:T(8,128)(2,1)S(1)} collective-permute-done((bf16[1,48,4608]{2,1,0:T(8,128)(2,1)S(1)}, bf16[1,48,4608]{2,1,0:T(8,128)(2,1)S(1)}, u32[]{:S(2)}, u32[]{:S(2)}) %collective-permute-start.18) | collective-permute-done | bytes 442400 | tf_op jit(solution)/shard_map/ppermute | solution.py:111
  33.9 9.5 %collective-permute-done.20 = bf16[1,48,4608]{2,1,0:T(8,128)(2,1)S(1)} collective-permute-done((bf16[1,48,4608]{2,1,0:T(8,128)(2,1)S(1)}, bf16[1,48,4608]{2,1,0:T(8,128)(2,1)S(1)}, u32[]{:S(2)}, u32[]{:S(2)}) %collective-permute-start.20) | collective-permute-done | bytes 442400 | tf_op jit(solution)/shard_map/ppermute | solution.py:111
  50.4 12.1 %collective-permute-done.6 = s32[1,256]{1,0:T(1,128)S(1)} collective-permute-done((s32[1,256]{1,0:T(1,128)S(1)}, s32[1,256]{1,0:T(1,128)S(1)}, u32[]{:S(2)}, u32[]{:S(2)}) %collective-permute-start.6) | collective-permute-done | bytes 1056 | tf_op jit(solution)/shard_map/ppermute | solution.py:103
  84.6 7.2 %collective-permute-done.3 = bf16[1,384,768]{1,2,0:T(8,128)(2,1)S(1)} collective-permute-done((bf16[1,384,768]{1,2,0:T(8,128)(2,1)S(1)}, bf16[1,384,768]{1,2,0:T(8,128)(2,1)S(1)}, u32[]{:S(2)}, u32[]{:S(2)}) %collective-permute-start.3) | collective-permute-done | bytes 589856 | tf_op jit(solution)/shard_map/ppermute | solution.py:111
  91.8 6.6 %collective-permute-done.4 = bf16[1,384,768]{1,2,0:T(8,128)(2,1)S(1)} collective-permute-done((bf16[1,384,768]{1,2,0:T(8,128)(2,1)S(1)}, bf16[1,384,768]{1,2,0:T(8,128)(2,1)S(1)}, u32[]{:S(2)}, u32[]{:S(2)}) %collective-permute-start.4) | collective-permute-done | bytes 589856 | tf_op jit(solution)/shard_map/ppermute | solution.py:111
  98.4 7.1 %collective-permute-done.5 = bf16[1,384,768]{1,2,0:T(8,128)(2,1)S(1)} collective-permute-done((bf16[1,384,768]{1,2,0:T(8,128)(2,1)S(1)}, bf16[1,384,768]{1,2,0:T(8,128)(2,1)S(1)}, u32[]{:S(2)}, u32[]{:S(2)}) %collective-permute-start.5) | collective-permute-done | bytes 589856 | tf_op jit(solution)/shard_map/ppermute | solution.py:111
  150.5 13.6 %collective-permute-done.12 = bf16[256,1536]{1,0:T(8,128)(2,1)S(1)} collective-permute-done((bf16[256,1536]{1,0:T(8,128)(2,1)S(1)}, bf16[256,1536]{1,0:T(8,128)(2,1)S(1)}, u32[]{:S(2)}, u32[]{:S(2)}) %collective-permute-start.12) | collective-permute-done | bytes 786464 | tf_op jit(solution)/shard_map/ppermute | solution.py:124
  164.1 21.0 %collective-permute-done.13 = bf16[256,1536]{1,0:T(8,128)(2,1)S(1)} collective-permute-done((bf16[256,1536]{1,0:T(8,128)(2,1)S(1)}, bf16[256,1536]{1,0:T(8,128)(2,1)S(1)}, u32[]{:S(2)}, u32[]{:S(2)}) %collective-permute-start.13) | collective-permute-done | bytes 786464 | tf_op jit(solution)/shard_map/ppermute | solution.py:124
  189.9 16.1 %collective-permute-done.15 = bf16[256,1536]{1,0:T(8,128)(2,1)S(1)} collective-permute-done((bf16[256,1536]{1,0:T(8,128)(2,1)S(1)}, bf16[256,1536]{1,0:T(8,128)(2,1)S(1)}, u32[]{:S(2)}, u32[]{:S(2)}) %collective-permute-start.15) | collective-permute-done | bytes 786464 | tf_op jit(solution)/shard_map/ppermute | solution.py:103
  205.9 16.8 %collective-permute-done.17 = bf16[256,1536]{1,0:T(8,128)(2,1)} collective-permute-done((bf16[256,1536]{1,0:T(8,128)(2,1)S(1)}, bf16[256,1536]{1,0:T(8,128)(2,1)}, u32[]{:S(2)}, u32[]{:S(2)}) %collective-permute-start.17) | collective-permute-done | bytes 786464 | tf_op jit(solution)/shard_map/ppermute | solution.py:103
  226.8 18.6 %fusion.52 = f32[1024,4608]{1,0:T(8,128)S(1)} fusion(bf16[1024,1536]{1,0:T(8,128)(2,1)S(1)} %constant_dynamic-update-slice_fusion.2, bf16[1536,4608]{1,0:T(8,128)(2,1)} %all-gather.5.cloned.1.call-done), kind=kOutput, calls=%fused_computation.182 | convolution fusion | flops 14495514624 | bytes 36175872 | tf_op jit(solution)/shard_map/dot_general | solution.py:48
  252.1 6.1 %collective-permute-done.23 = bf16[256,1536]{1,0:T(8,128)(2,1)S(1)} collective-permute-done((bf16[256,1536]{1,0:T(8,128)(2,1)S(1)}, bf16[256,1536]{1,0:T(8,128)(2,1)S(1)}, u32[]{:S(2)}, u32[]{:S(2)}) %collective-permute-start.23) | collective-permute-done | bytes 786464 | tf_op jit(solution)/shard_map/ppermute | solution.py:103
  260.0 9.6 %convolution_convert_fusion.1 = bf16[2304,1536]{1,0:T(8,128)(2,1)} fusion(bf16[1024,2304]{1,0:T(8,128)(2,1)S(1)} %multiply_convert_fusion.2, bf16[1024,1536]{1,0:T(8,128)(2,1)S(1)} %constant_dynamic-update-slice_fusion.6), kind=kOutput, calls=%fused_computation.8 | convolution fusion | flops 7251296256 | bytes 14942208 | tf_op jit(solution)/shard_map/dot_general | solution.py:56
  269.7 20.0 %multiply_convert_fusion.1 = (bf16[1024,2304]{1,0:T(8,128)(2,1)}, bf16[1024,2304]{1,0:T(8,128)(2,1)}) fusion(f32[1024,4608]{1,0:T(8,128)} %copy-done.2, bf16[1024,1536]{1,0:T(8,128)(2,1)} %copy-done.54, bf16[2304,1536]{1,0:T(8,128)(2,1)} %all-gather.7.cloned.1.call-done), kind=kOutput, calls=%fused_computation.12 | convolution fusion | flops 7278428160 | bytes 38535168 | tf_op jit(solution)/shard_map/dot_general | solution.py:52
  289.7 20.5 %fusion.7 = bf16[1024,1536]{1,0:T(8,128)(2,1)S(1)} fusion(bf16[1536,4608]{1,0:T(8,128)(2,1)} %all-gather.5.cloned.1.call-done, bf16[1024,2304]{1,0:T(8,128)(2,1)} %get-tuple-element.129, bf16[1024,2304]{1,0:T(8,128)(2,1)} %get-tuple-element.128), kind=kOutput, calls=%fused_computation.24 | convolution fusion | flops 14515961856 | bytes 26738688 | tf_op jit(solution)/shard_map/dot_general | solution.py:52
  314.3 21.5 %convolution_convert_fusion = bf16[1536,4608]{1,0:T(8,128)(2,1)} fusion(bf16[1024,1536]{1,0:T(8,128)(2,1)S(1)} %copy-done.56, bf16[1024,2304]{1,0:T(8,128)(2,1)} %get-tuple-element.129, bf16[1024,2304]{1,0:T(8,128)(2,1)} %get-tuple-element.128), kind=kOutput, calls=%fused_computation | convolution fusion | flops 14521466880 | bytes 26738688 | tf_op jit(solution)/shard_map/dot_general | solution.py:56
  335.8 12.5 %collective-permute-done.25 = bf16[256,1536]{1,0:T(8,128)(2,1)S(1)} collective-permute-done((bf16[256,1536]{1,0:T(8,128)(2,1)}, bf16[256,1536]{1,0:T(8,128)(2,1)S(1)}, u32[]{:S(2)}, u32[]{:S(2)}) %collective-permute-start.25) | collective-permute-done | bytes 786464 | tf_op jit(solution)/shard_map/ppermute | solution.py:124
  359.0 11.5 %convolution_convert_fusion.3 = bf16[1024,1536]{1,0:T(8,128)(2,1)S(1)} fusion(bf16[1024,2304]{1,0:T(8,128)(2,1)} %copy-done.25, bf16[2304,1536]{1,0:T(8,128)(2,1)} %all-gather.7.cloned.1.call-done), kind=kOutput, calls=%fused_computation.26 | convolution fusion | flops 7249330176 | bytes 14942208 | tf_op jit(solution)/shard_map/dot_general | solution.py:48
  375.7 16.3 %collective-permute-done.29 = bf16[256,1536]{1,0:T(8,128)(2,1)S(1)} collective-permute-done((bf16[256,1536]{1,0:T(8,128)(2,1)S(1)}, bf16[256,1536]{1,0:T(8,128)(2,1)S(1)}, u32[]{:S(2)}, u32[]{:S(2)}) %collective-permute-start.29) | collective-permute-done | bytes 786464 | tf_op jit(solution)/shard_map/ppermute | solution.py:103
  448.0 10.4 %collective-permute-done.33 = bf16[256,1536]{1,0:T(8,128)(2,1)} collective-permute-done((bf16[256,1536]{1,0:T(8,128)(2,1)}, bf16[256,1536]{1,0:T(8,128)(2,1)}, u32[]{:S(2)}, u32[]{:S(2)}) %collective-permute-start.33) | collective-permute-done | bytes 786464 | tf_op jit(solution)/shard_map/ppermute | solution.py:124
  458.4 17.6 %collective-permute-done.34 = bf16[256,1536]{1,0:T(8,128)(2,1)} collective-permute-done((bf16[256,1536]{1,0:T(8,128)(2,1)}, bf16[256,1536]{1,0:T(8,128)(2,1)}, u32[]{:S(2)}, u32[]{:S(2)}) %collective-permute-start.34) | collective-permute-done | bytes 786464 | tf_op jit(solution)/shard_map/ppermute | solution.py:124
  476.1 14.8 %reduce-scatter.6.cloned.1.call-done = bf16[192,4608]{1,0:T(8,128)(2,1)} async-done(((bf16[1536,4608]{1,0:T(8,128)(2,1)}), bf16[192,4608]{1,0:T(8,128)(2,1)}) %reduce-scatter.6.cloned.1.call-update) | async-done | bytes 1769488 | tf_op jit(solution)/shard_map/reduce_scatter | solution.py:488
  508.8 9.5 %collective-permute-done.38 = bf16[1,48,4608]{2,1,0:T(8,128)(2,1)S(1)} collective-permute-done((bf16[1,48,4608]{2,1,0:T(8,128)(2,1)S(1)}, bf16[1,48,4608]{2,1,0:T(8,128)(2,1)S(1)}, u32[]{:S(2)}, u32[]{:S(2)}) %collective-permute-start.38) | collective-permute-done | bytes 442400 | tf_op jit(solution)/shard_map/ppermute | solution.py:111
  547.9 10.3 %collective-permute-done.39 = bf16[48,1536]{1,0:T(8,128)(2,1)S(1)} collective-permute-done((bf16[48,1536]{1,0:T(8,128)(2,1)S(1)}, bf16[48,1536]{1,0:T(8,128)(2,1)S(1)}, u32[]{:S(2)}, u32[]{:S(2)}) %collective-permute-start.39) | collective-permute-done | bytes 147488 | tf_op jit(solution)/shard_map/ppermute | solution.py:290
  (396 shorter events, 235.0 us)
Async XLA Ops:
  7.2 59.0 %all-gather.9.cloned.1.call-start = ((), (), s32[]{:S(2)}) async-start(), calls=%async_computation.9 | async-start | bytes 3207168 | tf_op jit(solution)/shard_map/all_gather | solution.py:173
  10.5 212.2 %all-gather.5.cloned.1.call-start = ((), (), s32[]{:S(2)}) async-start(), calls=%async_computation.4 | async-start | bytes 15925248 | tf_op jit(solution)/shard_map/all_gather | solution.py:458
  44.8 224.9 %all-gather.7.cloned.1.call-start = ((), (), s32[]{:S(2)}) async-start(), calls=%async_computation.5 | async-start | bytes 7962624 | tf_op jit(solution)/shard_map/all_gather | solution.py:459
  44.8 29.1 %collective-permute-start = (bf16[256,1536]{1,0:T(8,128)(2,1)S(1)}, bf16[256,1536]{1,0:T(8,128)(2,1)}, u32[]{:S(2)}, u32[]{:S(2)}) collective-permute-start(bf16[256,1536]{1,0:T(8,128)(2,1)S(1)} %bitcast.165), channel_id=1, source_target_pairs={{0,1},{1,0},{2,3},{3,2},{4,5},{5,4},{6,7},{7,6},{8,9},{9,8},{10,11... | collective-permute-start | bytes 2359304 | tf_op jit(solution)/shard_map/ppermute | solution.py:103
  46.0 29.1 %collective-permute-start.1 = (bf16[256,1536]{1,0:T(8,128)(2,1)S(1)}, bf16[256,1536]{1,0:T(8,128)(2,1)}, u32[]{:S(2)}, u32[]{:S(2)}) collective-permute-start(bf16[256,1536]{1,0:T(8,128)(2,1)S(1)} %bitcast.166), channel_id=1, source_target_pairs={{0,2},{1,3},{2,0},{3,1},{4,6},{5,7},{6,4},{7,5},{8,10},{9,11},{10,... | collective-permute-start | bytes 2359304 | tf_op jit(solution)/shard_map/ppermute | solution.py:103
  50.0 299.2 %reduce-scatter.4.cloned.1.call-start = ((), (), s32[]{:S(2)}) async-start(), calls=%async_computation.6 | async-start | bytes 7962624 | tf_op jit(solution)/shard_map/reduce_scatter | solution.py:477
  72.7 25.7 %collective-permute-start.4 = (bf16[1,384,768]{1,2,0:T(8,128)(2,1)S(1)}, bf16[1,384,768]{1,2,0:T(8,128)(2,1)S(1)}, u32[]{:S(2)}, u32[]{:S(2)}) collective-permute-start(bf16[1,384,768]{1,2,0:T(8,128)(2,1)S(1)} %get-tuple-element.146), channel_id=1, source_target_pairs={{2,0},{3,1},{0,2},{1,3},{6,4},{7,5},{4,6},{5,7},{10,8},{11,9},{8,1... | collective-permute-start | bytes 1769480 | tf_op jit(solution)/shard_map/ppermute | solution.py:111
  73.9 31.5 %collective-permute-start.5 = (bf16[1,384,768]{1,2,0:T(8,128)(2,1)S(1)}, bf16[1,384,768]{1,2,0:T(8,128)(2,1)S(1)}, u32[]{:S(2)}, u32[]{:S(2)}) collective-permute-start(bf16[1,384,768]{1,2,0:T(8,128)(2,1)S(1)} %get-tuple-element.145), channel_id=1, source_target_pairs={{3,0},{2,1},{1,2},{0,3},{7,4},{6,5},{5,6},{4,7},{11,8},{10,9},{9,1... | collective-permute-start | bytes 1769480 | tf_op jit(solution)/shard_map/ppermute | solution.py:111
  149.0 36.1 %collective-permute-start.13 = (bf16[256,1536]{1,0:T(8,128)(2,1)S(1)}, bf16[256,1536]{1,0:T(8,128)(2,1)S(1)}, u32[]{:S(2)}, u32[]{:S(2)}) collective-permute-start(bf16[256,1536]{1,0:T(8,128)(2,1)S(1)} %get-tuple-element.144), channel_id=1, source_target_pairs={{2,0},{3,1},{0,2},{1,3},{6,4},{7,5},{4,6},{5,7},{10,8},{11,9},{8,1... | collective-permute-start | bytes 2359304 | tf_op jit(solution)/shard_map/ppermute | solution.py:124
  150.5 34.6 %collective-permute-start.14 = (bf16[256,1536]{1,0:T(8,128)(2,1)S(1)}, bf16[256,1536]{1,0:T(8,128)(2,1)S(1)}, u32[]{:S(2)}, u32[]{:S(2)}) collective-permute-start(bf16[256,1536]{1,0:T(8,128)(2,1)S(1)} %get-tuple-element.143), channel_id=1, source_target_pairs={{1,0},{0,1},{3,2},{2,3},{5,4},{4,5},{7,6},{6,7},{9,8},{8,9},{11,10... | collective-permute-start | bytes 2359304 | tf_op jit(solution)/shard_map/ppermute | solution.py:124
  188.7 34.1 %collective-permute-start.17 = (bf16[256,1536]{1,0:T(8,128)(2,1)S(1)}, bf16[256,1536]{1,0:T(8,128)(2,1)}, u32[]{:S(2)}, u32[]{:S(2)}) collective-permute-start(bf16[256,1536]{1,0:T(8,128)(2,1)S(1)} %multiply_convert_fusion.4), channel_id=1, source_target_pairs={{0,3},{1,2},{2,1},{3,0},{4,7},{5,6},{6,5},{7,4},{8,11},{9,10},{10,... | collective-permute-start | bytes 2359304 | tf_op jit(solution)/shard_map/ppermute | solution.py:103
  222.8 29.1 %collective-permute-start.21 = (bf16[256,1536]{1,0:T(8,128)(2,1)S(1)}, bf16[256,1536]{1,0:T(8,128)(2,1)S(1)}, u32[]{:S(2)}, u32[]{:S(2)}) collective-permute-start(bf16[256,1536]{1,0:T(8,128)(2,1)S(1)} %bitcast.190), channel_id=1, source_target_pairs={{0,1},{1,0},{2,3},{3,2},{4,5},{5,4},{6,7},{7,6},{8,9},{9,8},{10,11... | collective-permute-start | bytes 2359304 | tf_op jit(solution)/shard_map/ppermute | solution.py:103
  223.6 28.3 %collective-permute-start.22 = (bf16[256,1536]{1,0:T(8,128)(2,1)S(1)}, bf16[256,1536]{1,0:T(8,128)(2,1)S(1)}, u32[]{:S(2)}, u32[]{:S(2)}) collective-permute-start(bf16[256,1536]{1,0:T(8,128)(2,1)S(1)} %bitcast.191), channel_id=1, source_target_pairs={{0,2},{1,3},{2,0},{3,1},{4,6},{5,7},{6,4},{7,5},{8,10},{9,11},{10,... | collective-permute-start | bytes 2359304 | tf_op jit(solution)/shard_map/ppermute | solution.py:103
  224.1 34.1 %collective-permute-start.23 = (bf16[256,1536]{1,0:T(8,128)(2,1)S(1)}, bf16[256,1536]{1,0:T(8,128)(2,1)S(1)}, u32[]{:S(2)}, u32[]{:S(2)}) collective-permute-start(bf16[256,1536]{1,0:T(8,128)(2,1)S(1)} %bitcast.192), channel_id=1, source_target_pairs={{0,3},{1,2},{2,1},{3,0},{4,7},{5,6},{6,5},{7,4},{8,11},{9,10},{10,... | collective-permute-start | bytes 2359304 | tf_op jit(solution)/shard_map/ppermute | solution.py:103
  269.6 221.3 %reduce-scatter.6.cloned.1.call-start = ((), (), s32[]{:S(2)}) async-start(), calls=%async_computation.7 | async-start | bytes 15925248 | tf_op jit(solution)/shard_map/reduce_scatter | solution.py:488
  312.1 36.2 %collective-permute-start.25 = (bf16[256,1536]{1,0:T(8,128)(2,1)}, bf16[256,1536]{1,0:T(8,128)(2,1)S(1)}, u32[]{:S(2)}, u32[]{:S(2)}) collective-permute-start(bf16[256,1536]{1,0:T(8,128)(2,1)} %get-tuple-element.139), channel_id=1, source_target_pairs={{2,0},{3,1},{0,2},{1,3},{6,4},{7,5},{4,6},{5,7},{10,8},{11,9},{8,1... | collective-permute-start | bytes 2359304 | tf_op jit(solution)/shard_map/ppermute | solution.py:124
  312.6 35.6 %collective-permute-start.26 = (bf16[256,1536]{1,0:T(8,128)(2,1)}, bf16[256,1536]{1,0:T(8,128)(2,1)}, u32[]{:S(2)}, u32[]{:S(2)}) collective-permute-start(bf16[256,1536]{1,0:T(8,128)(2,1)} %get-tuple-element.138), channel_id=1, source_target_pairs={{1,0},{0,1},{3,2},{2,3},{5,4},{4,5},{7,6},{6,7},{9,8},{8,9},{11,10... | collective-permute-start | bytes 2359304 | tf_op jit(solution)/shard_map/ppermute | solution.py:124
  349.2 186.9 %reduce-scatter.8.cloned.1.call-start = ((), (), s32[]{:S(2)}) async-start(), calls=%async_computation.8 | async-start | bytes 3981312 | tf_op jit(solution)/shard_map/reduce_scatter | solution.py:282
  357.9 34.0 %collective-permute-start.29 = (bf16[256,1536]{1,0:T(8,128)(2,1)S(1)}, bf16[256,1536]{1,0:T(8,128)(2,1)S(1)}, u32[]{:S(2)}, u32[]{:S(2)}) collective-permute-start(bf16[256,1536]{1,0:T(8,128)(2,1)S(1)} %get-tuple-element.89), channel_id=1, source_target_pairs={{0,3},{1,2},{2,1},{3,0},{4,7},{5,6},{6,5},{7,4},{8,11},{9,10},{10,... | collective-permute-start | bytes 2359304 | tf_op jit(solution)/shard_map/ppermute | solution.py:103
  393.7 34.4 %collective-permute-start.30 = (bf16[256,1536]{1,0:T(8,128)(2,1)}, bf16[256,1536]{1,0:T(8,128)(2,1)}, u32[]{:S(2)}, u32[]{:S(2)}) collective-permute-start(bf16[256,1536]{1,0:T(8,128)(2,1)} %get-tuple-element.136), channel_id=1, source_target_pairs={{3,0},{2,1},{1,2},{0,3},{7,4},{6,5},{5,6},{4,7},{11,8},{10,9},{9,1... | collective-permute-start | bytes 2359304 | tf_op jit(solution)/shard_map/ppermute | solution.py:124
  395.2 36.1 %collective-permute-start.31 = (bf16[256,1536]{1,0:T(8,128)(2,1)}, bf16[256,1536]{1,0:T(8,128)(2,1)}, u32[]{:S(2)}, u32[]{:S(2)}) collective-permute-start(bf16[256,1536]{1,0:T(8,128)(2,1)} %get-tuple-element.135), channel_id=1, source_target_pairs={{2,0},{3,1},{0,2},{1,3},{6,4},{7,5},{4,6},{5,7},{10,8},{11,9},{8,1... | collective-permute-start | bytes 2359304 | tf_op jit(solution)/shard_map/ppermute | solution.py:124
  396.1 35.2 %collective-permute-start.32 = (bf16[256,1536]{1,0:T(8,128)(2,1)}, bf16[256,1536]{1,0:T(8,128)(2,1)}, u32[]{:S(2)}, u32[]{:S(2)}) collective-permute-start(bf16[256,1536]{1,0:T(8,128)(2,1)} %get-tuple-element.134), channel_id=1, source_target_pairs={{1,0},{0,1},{3,2},{2,3},{5,4},{4,5},{7,6},{6,7},{9,8},{8,9},{11,10... | collective-permute-start | bytes 2359304 | tf_op jit(solution)/shard_map/ppermute | solution.py:124
  439.9 36.1 %collective-permute-start.34 = (bf16[256,1536]{1,0:T(8,128)(2,1)}, bf16[256,1536]{1,0:T(8,128)(2,1)}, u32[]{:S(2)}, u32[]{:S(2)}) collective-permute-start(bf16[256,1536]{1,0:T(8,128)(2,1)} %get-tuple-element.131), channel_id=1, source_target_pairs={{2,0},{3,1},{0,2},{1,3},{6,4},{7,5},{4,6},{5,7},{10,8},{11,9},{8,1... | collective-permute-start | bytes 2359304 | tf_op jit(solution)/shard_map/ppermute | solution.py:124
  440.5 35.5 %collective-permute-start.35 = (bf16[256,1536]{1,0:T(8,128)(2,1)}, bf16[256,1536]{1,0:T(8,128)(2,1)}, u32[]{:S(2)}, u32[]{:S(2)}) collective-permute-start(bf16[256,1536]{1,0:T(8,128)(2,1)} %get-tuple-element.130), channel_id=1, source_target_pairs={{1,0},{0,1},{3,2},{2,3},{5,4},{4,5},{7,6},{6,7},{9,8},{8,9},{11,10... | collective-permute-start | bytes 2359304 | tf_op jit(solution)/shard_map/ppermute | solution.py:124
  (96 other events, 1173.9 us)
Sparse Core Ops, SparseCore 0:
  10.7 35.1 all-gather.8
  47.5 127.4 all-gather.4
  176.7 69.7 all-gather.6
  269.7 76.4 reduce-scatter.3
  349.4 141.4 reduce-scatter.5
  493.1 43.0 reduce-scatter.7
